TPU v7x, 32 devices: a whole 2x2x4 slice. The times are simulated.
32 devices in a mesh: ctx: 16 (over z, x, core), head: 2 (over y).
Axes of the slice: x: 2, y: 2, z: 4, core: 2. Of those that a mesh axis runs over, the one named last changes fastest.
Arguments:
- query_proj: bfloat16 [2048, 4096], P('ctx', 'head'), may hold values from -4 to 4
- key_proj: bfloat16 [2048, 4096], P('ctx', 'head'), may hold values from -6 to 6
- value_proj: bfloat16 [2048, 4096], P('ctx', 'head'), may hold values from -6 to 6
- grad_out: bfloat16 [2048, 4096], P('ctx', 'head'), may hold values from -4 to 4
- out_proj: bfloat16 [4096, 4096], P('head'), may hold values from -0.09375 to 0.09375
- filters: bfloat16 [256, 2048], P('head'), may hold values from -1 to 1, as said below
- skip_gain: float32 [4096], P('head'), may hold values from 0.5 to 1.5
- doc_lengths: int32 [4], replicated, may hold values from 1 to 9, 16 in all
- group_of: int32 [4096], P('head'), may hold values from 0 to 255, as said below
Outputs:
- grad_query: bfloat16 [2048, 4096], P('ctx', 'head')
- grad_key: bfloat16 [2048, 4096], P('ctx', 'head')
- grad_filters: float32 [256, 2048], P('head', 'ctx')
Inputs may be any that keep to these rules, and one draw needn't show every extreme that they name: `filters`: filter entries never above 1 in magnitude. `group_of`: each filter group is named by exactly 16 channels, and the channels of the k-th block of 2048 channels name only groups k * 128 to (k + 1) * 128 - 1.
All inputs are finite; a program needn't handle non-finite values.
Results may differ from a plain program's by a relative error of at most 0.005.
Values may be sent and summed in bfloat16 or wider, within the bound.
No kernel may reach another device: no remote copies, remote signals or barrier semaphores. Data moves between devices by JAX's collectives and lax.ppermute only.
A program may use at most 128 MiB of HBM per device.

v0:
```python
import jax
import jax.numpy as jnp
from jax import lax
from jax.sharding import PartitionSpec as P


def skew_rows(vector, block_rows):
    lead = vector.shape[:-1]
    extended = jnp.concatenate([vector, jnp.zeros(lead + (1,), vector.dtype)], -1)
    tiled = jnp.broadcast_to(extended[..., None, :], lead + (block_rows, 2 * block_rows + 1))
    tiled = tiled.reshape(lead + (block_rows * (2 * block_rows + 1),))
    shaped = tiled[..., : 2 * block_rows * block_rows].reshape(lead + (block_rows, 2 * block_rows))
    return shaped[..., block_rows:]


def diagonal_sums(matrix, block_rows):
    lead = matrix.shape[:-2]
    padded = jnp.concatenate([jnp.zeros(lead + (block_rows, block_rows), matrix.dtype), matrix], -1)
    flat = padded.reshape(lead + (2 * block_rows * block_rows,))
    flat = jnp.concatenate([flat, jnp.zeros(lead + (block_rows,), matrix.dtype)], -1)
    rows_view = flat.reshape(lead + (block_rows, 2 * block_rows + 1))
    return jnp.sum(rows_view[..., : 2 * block_rows], axis=-2)


def span_documents(doc_lengths, count):
    bounds = jnp.cumsum(doc_lengths)
    positions = jnp.arange(count, dtype=jnp.int32)
    return jnp.sum((bounds[None, :] <= positions[:, None]).astype(jnp.int32), axis=1)


def per_device(
    query_proj, key_proj, value_proj, grad_out, out_proj, filters, skip_gain, doc_lengths, group_of
):
    block_rows = query_proj.shape[0]
    channels = query_proj.shape[1]
    groups_here = filters.shape[0]
    per_group = channels // groups_here
    spans = lax.axis_size("ctx")
    position = lax.axis_index("ctx")
    feature_grad = jnp.einsum(
        "tm,cm->tc",
        lax.all_gather(grad_out, "head", axis=1, tiled=True),
        out_proj,
        preferred_element_type=jnp.float32,
    )
    conv_grad = (feature_grad * value_proj.astype(jnp.float32)).astype(jnp.bfloat16)
    local_group = group_of - lax.axis_index("head") * groups_here
    ranking = jnp.argsort(local_group)
    inverse = jnp.argsort(ranking)
    grad_sorted = jnp.take(conv_grad, ranking, axis=1)
    query_sorted = jnp.take(query_proj, ranking, axis=1)
    key_sorted = jnp.take(key_proj, ranking, axis=1)
    skip_sorted = jnp.take(skip_gain, ranking)
    span_doc = span_documents(doc_lengths, spans)
    zero_rim = jnp.zeros((groups_here, block_rows), filters.dtype)
    filt_padded = jnp.concatenate([zero_rim, filters, zero_rim], 1)
    moved_grad, moved_query, moved_key = (
        lax.all_to_all(grad_sorted, "ctx", split_axis=1, concat_axis=0, tiled=True),
        lax.all_to_all(query_sorted, "ctx", split_axis=1, concat_axis=0, tiled=True),
        lax.all_to_all(key_sorted, "ctx", split_axis=1, concat_axis=0, tiled=True),
    )
    sub_channels = channels // spans
    sub_groups = sub_channels // per_group
    gated = (moved_query.astype(jnp.float32) * moved_key.astype(jnp.float32)).astype(jnp.bfloat16)
    grad_blocks = moved_grad.reshape(spans, block_rows, sub_groups, per_group)
    gated_blocks = gated.reshape(spans, block_rows, sub_groups, per_group)
    filt_sub = lax.dynamic_slice_in_dim(filt_padded, position * sub_groups, sub_groups, 0)
    leading = filt_sub[:, : spans * block_rows].reshape(sub_groups, spans, block_rows)
    trailing = filt_sub[:, block_rows : block_rows + spans * block_rows].reshape(
        sub_groups, spans, block_rows
    )
    toeplitz = skew_rows(jnp.concatenate([leading, trailing], -1), block_rows)
    offsets = jnp.arange(spans, dtype=jnp.int32)
    target = offsets[:, None] + offsets[None, :]
    clipped = jnp.clip(target, 0, spans - 1)
    same_doc = (target < spans) & (span_doc[clipped] == span_doc[None, :])
    shifted = (
        jnp.take(grad_blocks, clipped, axis=0)
        * same_doc.astype(jnp.bfloat16)[:, :, None, None, None]
    )
    gated_grad = jnp.einsum(
        "gkst,kitgc->isgc", toeplitz, shifted, preferred_element_type=jnp.float32
    )
    corr = jnp.einsum("isgc,kitgc->kgst", gated_blocks, shifted, preferred_element_type=jnp.float32)
    sums = diagonal_sums(corr, block_rows)
    front = jnp.pad(sums[:, :, :block_rows], ((0, 1), (0, 0), (0, 0)))
    behind_part = jnp.pad(sums[:, :, block_rows:], ((1, 0), (0, 0), (0, 0)))
    lag_full = jnp.transpose(front + behind_part, (1, 0, 2)).reshape(
        sub_groups, (spans + 1) * block_rows
    )
    lag_full = lag_full[:, block_rows : block_rows + spans * block_rows]
    skip_sub = lax.dynamic_slice_in_dim(skip_sorted, position * sub_channels, sub_channels, 0)
    gated_grad = gated_grad.reshape(spans * block_rows, sub_channels) + skip_sub[
        None, :
    ] * moved_grad.astype(jnp.float32)
    query_part = (gated_grad * moved_key.astype(jnp.float32)).astype(jnp.bfloat16)
    key_part = (gated_grad * moved_query.astype(jnp.float32)).astype(jnp.bfloat16)
    query_out, key_out = (
        lax.all_to_all(query_part, "ctx", split_axis=0, concat_axis=1, tiled=True),
        lax.all_to_all(key_part, "ctx", split_axis=0, concat_axis=1, tiled=True),
    )
    grad_filters = lax.all_to_all(lag_full, "ctx", split_axis=1, concat_axis=0, tiled=True)
    grad_query = jnp.take(query_out, inverse, axis=1)
    grad_key = jnp.take(key_out, inverse, axis=1)
    return (grad_query, grad_key, grad_filters)


def solution(mesh):
    in_specs = (
        P("ctx", "head"),
        P("ctx", "head"),
        P("ctx", "head"),
        P("ctx", "head"),
        P("head", None),
        P("head", None),
        P("head"),
        P(),
        P("head"),
    )
    out_specs = (P("ctx", "head"), P("ctx", "head"), P("head", "ctx"))
    return jax.shard_map(
        per_device, mesh=mesh, in_specs=in_specs, out_specs=out_specs, check_vma=False
    )
```

profile of v0, /device:TPU:0, one launch (start us, length us, event | category | flops | bytes accessed | tf_op | source)
XLA Modules:
  0.0 316.5 jit_solution(4945798456984137475)
XLA Ops:
  16.3 6.2 %gather_fusion.6 = bf16[2048,128]{1,0:T(8,128)(2,1)S(1)} fusion(bf16[128,2048]{0,1:T(8,128)(2,1)S(1)} %copy.35, s32[2048]{0:T(1024)S(1)} %fusion.22), kind=kCustom, calls=%fused_computation.3.clone | custom fusion | bytes 1056768 | tf_op jit(solution)/shard_map/jit(_take)/gather | solution.py:51
  22.5 6.2 %gather_fusion.4 = bf16[2048,128]{1,0:T(8,128)(2,1)S(1)} fusion(bf16[128,2048]{0,1:T(8,128)(2,1)S(1)} %copy.34, s32[2048]{0:T(1024)S(1)} %fusion.22), kind=kCustom, calls=%fused_computation.1.clone | custom fusion | bytes 1056768 | tf_op jit(solution)/shard_map/jit(_take)/gather | solution.py:52
  33.6 11.8 %fusion.7 = bf16[128,2048]{1,0:T(8,128)(2,1)S(1)} fusion(bf16[128,4096]{1,0:T(8,128)(2,1)} %all-gather.2.cloned.1.call-done, bf16[2048,4096]{1,0:T(8,128)(2,1)} %param.15, bf16[128,2048]{1,0:T(8,128)(2,1)S(1)} %copy-done.2), kind=kOutput, calls=%fused_computation.17 | convolution fusion | flops 2148270080 | bytes 18874368 | tf_op jit(solution)/shard_map/tm,cm->tc/dot_general | solution.py:40
  45.7 6.2 %gather_fusion.3 = bf16[2048,128]{1,0:T(8,128)(2,1)S(1)} fusion(bf16[128,2048]{0,1:T(8,128)(2,1)S(1)} %copy.31, s32[2048]{0:T(1024)S(1)} %fusion.22), kind=kCustom, calls=%fused_computation.clone | custom fusion | bytes 1056768 | tf_op jit(solution)/shard_map/jit(_take)/gather | solution.py:50
  61.2 11.9 %all-to-all-done = bf16[128,16,128]{0,2,1:T(8,128)(2,1)S(1)} async-done(((bf16[128,16,128]{0,2,1:T(8,128)(2,1)}), bf16[128,16,128]{0,2,1:T(8,128)(2,1)S(1)}, u32[]{:S(2)}, u32[]{:S(2)}) %all-to-all-start) | async-done | bytes 524320 | tf_op jit(solution)/shard_map/all_to_all | solution.py:58
  83.0 20.2 %reshape.182 = bf16[8,16,32896]{2,1,0:T(8,128)(2,1)} reshape(bf16[8,16,128,257]{3,2,1,0:T(8,128)(2,1)} %broadcast_in_dim.53) | data formatting | bytes 16842752 | tf_op jit(solution)/shard_map/reshape | solution.py:11
  103.2 7.3 %slice.50 = bf16[8,16,32768]{2,1,0:T(8,128)(2,1)} slice(bf16[8,16,32896]{2,1,0:T(8,128)(2,1)} %reshape.182), slice={[0:8], [0:16], [0:32768]} | slice | bytes 16777216 | tf_op jit(solution)/shard_map/slice | solution.py:12
  110.5 9.1 %copy.51 = bf16[16,8,128,256]{3,2,1,0:T(8,128)(2,1)} copy(bf16[16,8,128,256]{3,1,2,0:T(8,128)(2,1)} %bitcast.90) | data formatting | bytes 16777216
  119.6 11.8 %gather_fusion.2 = f32[2048]{0:T(1024)S(1)} fusion(f32[2048]{0:T(1024)S(1)} %copy-done, s32[2048]{0:T(1024)S(1)} %fusion.22), kind=kCustom, calls=%fused_computation.7 | custom fusion | bytes 24576 | tf_op jit(solution)/shard_map/jit(_take)/gather | solution.py:53
  131.5 8.5 %gather_fusion = bf16[256,128,8,16]{1,3,2,0:T(8,128)(2,1)} fusion(bf16[16,128,8,16]{1,3,2,0:T(8,128)(2,1)S(1)} %bitcast.85, s32[1024]{0:T(1024)S(1)} %pad_clamp_fusion), kind=kCustom, calls=%fused_computation.5 | custom fusion | bytes 16778240 | tf_op jit(solution)/shard_map/jit(_take)/gather | solution.py:78
  140.0 6.0 %all-to-all-start.1 = ((bf16[128,16,128]{0,2,1:T(8,128)(2,1)}), bf16[128,16,128]{0,2,1:T(8,128)(2,1)S(1)}, u32[]{:S(2)}, u32[]{:S(2)}) async-start(bf16[128,16,128]{0,2,1:T(8,128)(2,1)} %bitcast.15), calls=%async_computation.1 | async-start | bytes 1048576 | tf_op jit(solution)/shard_map/all_to_all | solution.py:60
  146.0 6.0 %fusion = f32[8,16,16,128,1]{3,2,1,0,4:T(8,128)S(1)} fusion(bf16[16,16,128,8,16]{2,4,3,1,0:T(8,128)(2,1)} %bitcast.86, pred[16,16]{1,0:T(8,128)(4,1)S(1)} %get-tuple-element.28, bf16[16,16]{1,0:T(8,128)(2,1)S(1)} %get-tuple-element.29, bf16[8,16,128,256]{3,2,1,0:T(8,128)(2,1)} %bitcast.91), kind=kOutput, calls=%fused_computation.9 | convolution fusion | flops 1082130432 | bytes 13632256 | tf_op jit(solution)/shard_map/gkst,kitgc->isgc/dot_general | solution.py:81
  152.2 8.1 %all-to-all-done.1 = bf16[128,16,128]{0,2,1:T(8,128)(2,1)S(1)} async-done(((bf16[128,16,128]{0,2,1:T(8,128)(2,1)}), bf16[128,16,128]{0,2,1:T(8,128)(2,1)S(1)}, u32[]{:S(2)}, u32[]{:S(2)}) %all-to-all-start.1) | async-done | bytes 524320 | tf_op jit(solution)/shard_map/all_to_all | solution.py:60
  160.4 8.3 %fusion.4 = f32[16,8,128,128]{2,3,0,1:T(8,128)} fusion(bf16[16,128,8,16,1]{1,3,2,0,4:T(8,128)(2,1)S(1)} %bitcast.93, bf16[16,16,128,8,16]{2,4,3,1,0:T(8,128)(2,1)} %bitcast.87, pred[16,16]{1,0:T(8,128)(4,1)S(1)} %get-tuple-element.28, bf16[16,16]{1,0:T(8,128)(2,1)S(1)} %get-tuple-element.29), kind=kOutput, calls=%fused_computation.15 | convolution fusion | flops 1082130432 | bytes 17302272 | tf_op jit(solution)/shard_map/isgc,kitgc->kgst/dot_general | solution.py:84
  168.8 9.3 %copy.50 = f32[16,8,128,128]{3,2,1,0:T(8,128)} copy(f32[16,8,128,128]{2,3,0,1:T(8,128)} %fusion.4) | data formatting | bytes 16777216
  178.0 11.0 %concatenate.14.clone = f32[16,8,128,256]{3,2,1,0:T(8,128)} pad(f32[16,8,128,128]{3,2,1,0:T(8,128)} %copy.50, f32[]{:T(128)} %constant.68.clone.1), padding=0_0x0_0x0_0x128_0 | pad | bytes 25165828 | tf_op jit(solution)/shard_map/concatenate | solution.py:18
  189.1 18.2 %reshape.185 = f32[16,8,32768]{2,1,0:T(8,128)} reshape(f32[16,8,128,256]{3,2,1,0:T(8,128)} %concatenate.14.clone) | data formatting | bytes 33554432 | tf_op jit(solution)/shard_map/reshape | solution.py:19
  207.3 11.3 %concatenate.15 = f32[16,8,32896]{2,1,0:T(8,128)} pad(f32[16,8,32768]{2,1,0:T(8,128)} %reshape.185, f32[]{:T(128)} %constant.68.clone.1), padding=0_0x0_0x0_128 | pad | bytes 33619972 | tf_op jit(solution)/shard_map/concatenate | solution.py:20
  218.6 26.6 %reshape.186 = f32[16,8,128,257]{3,2,1,0:T(8,128)} reshape(f32[16,8,32896]{2,1,0:T(8,128)} %concatenate.15) | data formatting | bytes 33685504 | tf_op jit(solution)/shard_map/reshape | solution.py:21
  245.2 8.1 %slice_reduce_fusion = f32[16,8,256]{2,1,0:T(8,128)S(1)} fusion(f32[16,8,128,257]{3,2,1,0:T(8,128)} %reshape.186), kind=kLoop, calls=%fused_computation.8 | loop fusion | flops 4161536 | bytes 16908288 | tf_op jit(solution)/shard_map/reduce_sum | solution.py:22
  259.4 5.7 %all-to-all-done.5 = f32[8,16,128]{2,0,1:T(8,128)S(1)} async-done(((f32[8,16,128]{2,0,1:T(8,128)}), f32[8,16,128]{2,0,1:T(8,128)S(1)}, u32[]{:S(2)}, u32[]{:S(2)}) %all-to-all-start.5) | async-done | bytes 65568 | tf_op jit(solution)/shard_map/all_to_all | solution.py:102
  265.1 16.9 %all_to_all.93 = bf16[16,128,128]{1,2,0:T(8,128)(2,1)S(1)} all-to-all(bf16[16,128,128]{1,2,0:T(8,128)(2,1)S(1)} %get-tuple-element.17), channel_id=1, replica_groups=mesh['ctx'=16,'head'=2] {'ctx'}, dimensions={0} | all-to-all | bytes 1048576 | tf_op jit(solution)/shard_map/all_to_all | solution.py:100
  291.1 6.2 %gather_fusion.7 = bf16[2048,128]{1,0:T(8,128)(2,1)S(1)} fusion(bf16[128,2048]{0,1:T(8,128)(2,1)S(1)} %bitcast.89, s32[2048]{0:T(1024)S(1)} %fusion.23), kind=kCustom, calls=%fused_computation.4.clone | custom fusion | bytes 1056768 | tf_op jit(solution)/shard_map/jit(_take)/gather | solution.py:104
  300.3 6.2 %gather_fusion.5 = bf16[2048,128]{1,0:T(8,128)(2,1)S(1)} fusion(bf16[128,2048]{0,1:T(8,128)(2,1)S(1)} %bitcast.88, s32[2048]{0:T(1024)S(1)} %fusion.23), kind=kCustom, calls=%fused_computation.2.clone | custom fusion | bytes 1056768 | tf_op jit(solution)/shard_map/jit(_take)/gather | solution.py:103
  (62 shorter events, 55.0 us)
Async XLA Ops:
  7.2 112.5 %copy-start = (f32[2048]{0:T(1024)S(1)}, f32[2048]{0:T(1024)}, u32[]{:S(2)}) copy-start(f32[2048]{0:T(1024)} %param.17) | copy-start | bytes 24580
  7.2 26.4 %copy-start.2 = (bf16[128,2048]{1,0:T(8,128)(2,1)S(1)}, bf16[128,2048]{1,0:T(8,128)(2,1)}, u32[]{:S(2)}) copy-start(bf16[128,2048]{1,0:T(8,128)(2,1)} %param.13) | copy-start | bytes 1572868
  7.2 26.4 %all-gather.2.cloned.1.call-start = ((), (), s32[]{:S(2)}) async-start(), calls=%async_computation.6 | async-start | bytes 1572864 | tf_op jit(solution)/shard_map/all_gather | solution.py:42
  16.3 29.1 %copy-start.4 = (s32[2048]{0:T(1024)}, s32[2048]{0:T(1024)S(1)}, u32[]{:S(2)}) copy-start(s32[2048]{0:T(1024)S(1)} %get-tuple-element.6) | copy-start | bytes 24580
  45.4 13.6 %copy-start.6 = (s32[4]{0:T(128)S(1)}, s32[4]{0:T(128)}, u32[]{:S(2)}) copy-start(s32[4]{0:T(128)} %param.18) | copy-start | bytes 52
  45.7 31.7 %copy-start.3 = (bf16[128,2048]{1,0:T(8,128)(2,1)S(1)}, bf16[128,2048]{1,0:T(8,128)(2,1)}, u32[]{:S(2)}) copy-start(bf16[128,2048]{1,0:T(8,128)(2,1)} %param.16) | copy-start | bytes 1572868
  53.2 19.9 %all-to-all-start = ((bf16[128,16,128]{0,2,1:T(8,128)(2,1)}), bf16[128,16,128]{0,2,1:T(8,128)(2,1)S(1)}, u32[]{:S(2)}, u32[]{:S(2)}) async-start(bf16[128,16,128]{0,2,1:T(8,128)(2,1)} %bitcast.1), calls=%async_computation | async-start | bytes 1048576 | tf_op jit(solution)/shard_map/all_to_all | solution.py:58
  73.1 66.9 %all-to-all-start.3 = ((bf16[128,16,128]{0,2,1:T(8,128)(2,1)}), bf16[128,16,128]{0,2,1:T(8,128)(2,1)S(1)}, u32[]{:S(2)}, u32[]{:S(2)}) async-start(bf16[128,16,128]{0,2,1:T(8,128)(2,1)} %bitcast.21), calls=%async_computation.3 | async-start | bytes 1048576 | tf_op jit(solution)/shard_map/all_to_all | solution.py:59
  140.0 20.3 %all-to-all-start.1 = ((bf16[128,16,128]{0,2,1:T(8,128)(2,1)}), bf16[128,16,128]{0,2,1:T(8,128)(2,1)S(1)}, u32[]{:S(2)}, u32[]{:S(2)}) async-start(bf16[128,16,128]{0,2,1:T(8,128)(2,1)} %bitcast.15), calls=%async_computation.1 | async-start | bytes 1048576 | tf_op jit(solution)/shard_map/all_to_all | solution.py:60
  245.2 40.9 %copy-start.5 = (s32[2048]{0:T(1024)S(1)}, s32[2048]{0:T(1024)}, u32[]{:S(2)}) copy-start(s32[2048]{0:T(1024)} %copy-done.4) | copy-start | bytes 24580
  254.0 11.1 %all-to-all-start.5 = ((f32[8,16,128]{2,0,1:T(8,128)}), f32[8,16,128]{2,0,1:T(8,128)S(1)}, u32[]{:S(2)}, u32[]{:S(2)}) async-start(f32[8,16,128]{2,0,1:T(8,128)} %slice_bitcast_fusion), calls=%async_computation.5 | async-start | bytes 131072 | tf_op jit(solution)/shard_map/all_to_all | solution.py:102
  258.2 51.5 %copy-start.1 = (f32[2048]{0:T(1024)S(1)}, f32[2048]{0:T(1024)}, u32[]{:S(2)}) copy-start(f32[2048]{0:T(1024)} %param.17) | copy-start | bytes 24580
  281.9 18.4 %all-to-all-start.2 = ((bf16[16,128,128]{1,2,0:T(8,128)(2,1)}), bf16[16,128,128]{1,2,0:T(8,128)(2,1)S(1)}, u32[]{:S(2)}, u32[]{:S(2)}) async-start(bf16[16,128,128]{1,2,0:T(8,128)(2,1)} %get-tuple-element.18), calls=%async_computation.2 | async-start | bytes 1048576 | tf_op jit(solution)/shard_map/all_to_all | solution.py:99
Sparse Core Ops, SparseCore 0:
  9.5 23.9 all-gather.1
where the time goes:
time: 319 us; the launch traced here: 316 us
  local copies, waits for them, and re-layouts  178 us (56%)
  waiting for transfers between devices  34.3 us (11%)
  matrix products  26.1 us (8%)
  starting transfers between devices  24.1 us (8%)
  other arithmetic  22.5 us (7%)
  blocking collectives  16.9 us (5%)
  between operations  14.4 us (5%)
    reshape x1, local copies, waits for them, and re-layouts, diagonal_sums(): rows_view = flat.reshape(lead + (block_rows, 2 * block_rows + 1))  26.6 us
    unnamed x21, local copies, waits for them, and re-layouts  23.7 us
    reshape x1, local copies, waits for them, and re-layouts, skew_rows(): tiled = tiled.reshape(lead + (block_rows * (2 * block_rows + 1),))  20.2 us
    reshape x1, local copies, waits for them, and re-layouts, diagonal_sums(): flat = padded.reshape(lead + (2 * block_rows * block_rows,))  18.2 us
    all_to_all x1, blocking collectives, per_device(): lax.all_to_all(key_part, 'ctx', split_axis=0, concat_axis=1, tiled=True)  16.9 us
    all_to_all x1, waiting for transfers between devices, per_device(): lax.all_to_all(grad_sorted, 'ctx', split_axis=1, concat_axis=0, tiled=True)  11.9 us
    dot_general x1, matrix products, per_device(): jnp.einsum('tm,cm->tc', lax.all_gather(grad_out, 'head', axis=1, tiled=Tr...  11.8 us
    gather x1, local copies, waits for them, and re-layouts, per_device(): skip_sorted = jnp.take(skip_gain, ranking)  11.8 us
  transfers between devices with their start and end apart: 6, of which 5 were waited for; matrix products, arithmetic and copies ran while one was open for 33% of the time, Pallas kernels for 0%

commit v1 on v0

v1 whole, which is shorter than its diff:
```python
import functools

import jax
import jax.numpy as jnp
from jax import lax
from jax.experimental import pallas as pl
from jax.experimental.pallas import tpu as pltpu
from jax.sharding import PartitionSpec as P

F32 = jnp.float32
BF16 = jnp.bfloat16
I32 = jnp.int32
NT = (((1,), (1,)), ((), ()))
NN = (((1,), (0,)), ((), ()))
EXTRA = 16


def dot(a, b, dims):
    return lax.dot_general(a, b, dims, preferred_element_type=F32)


def one_hot(rank_row, first, rows):
    shape = (rows, rank_row.shape[1])
    return jnp.where(lax.broadcasted_iota(I32, shape, 0) + first == rank_row, 1.0, 0.0).astype(BF16)


def params(**kw):
    return pltpu.CompilerParams(vmem_limit_bytes=56 * 1024 * 1024, **kw)


def gate_kernel(head_ref, group_ref, query_ref, key_ref, out_ref, rank_ref, *, groups, per_group, chunk):
    channels = group_ref.shape[1]
    local = group_ref[...] - head_ref[0] * groups
    width = 128
    upper = (
        lax.broadcasted_iota(I32, (width, width), 0) < lax.broadcasted_iota(I32, (width, width), 1)
    )
    upper = jnp.where(upper, 1.0, 0.0).astype(BF16)
    base = jnp.zeros((groups, 1), F32)
    for b in range(channels // width):
        here = local[:, b * width : (b + 1) * width]
        member = jnp.where(lax.broadcasted_iota(I32, (groups, width), 0) == here, 1.0, 0.0)
        before = dot(member.astype(BF16), upper, NN) + base
        place = jnp.sum(member * before, axis=0, keepdims=True)
        rank_ref[:, b * width : (b + 1) * width] = here * per_group + place.astype(I32)
        base = base + jnp.sum(member, axis=1, keepdims=True)
    rank = rank_ref[...]
    gated = (query_ref[...].astype(F32) * key_ref[...].astype(F32)).astype(BF16)
    gated_t = gated.T
    permute_rows(rank, gated_t, out_ref, chunk)


def permute_rows(rank, by_channel, out_ref, chunk):
    channels = by_channel.shape[0]
    rows = out_ref.shape[1]
    for p in range(0, channels, chunk):
        moved = dot(one_hot(rank, p, chunk), by_channel, NN).astype(BF16)
        out_ref[p // rows : (p + chunk) // rows] = moved.reshape(chunk // rows, rows, -1)


def partial_kernel(half_ref, grad_ref, weight_ref, out_ref):
    out_ref[...] = dot(weight_ref[...], grad_ref[...], NT)


def add_kernel(half_ref, grad_ref, weight_ref, acc_ref, out_ref):
    out_ref[...] = acc_ref[...] + dot(weight_ref[...], grad_ref[...], NT)


def last_kernel(
    half_ref, rank_ref, grad_ref, weight_ref, acc_ref, value_ref, out_ref, conv_ref, *, chunk
):
    step = pl.program_id(0)
    block = weight_ref.shape[0]
    total = acc_ref[...] + dot(weight_ref[...], grad_ref[...], NT)
    conv = (total * value_ref[...].astype(F32).T).astype(BF16)
    conv_ref[pl.ds(pl.multiple_of(step * block, block), block), :] = conv

    @pl.when(step == pl.num_programs(0) - 1)
    def _():
        permute_rows(rank_ref[...], conv_ref[...], out_ref, chunk)


def prepare_kernel(docs_ref, filt_ref, toep_ref, mask_ref, *, per_group, spans):
    groups, width = filt_ref.shape
    tokens = toep_ref.shape[1]
    for g in range(groups):
        row = jnp.concatenate([filt_ref[g : g + 1, :], jnp.zeros((1, tokens), F32)], axis=1)
        wide = jnp.broadcast_to(row, (tokens, width + tokens))
        skewed = pltpu.roll(wide, 0, 1, stride=1, stride_axis=0)
        toep_ref[g] = skewed[:, :width].astype(BF16)
    rows = mask_ref.shape[0]
    block = lax.broadcasted_iota(I32, (rows, tokens), 0) // per_group

    def doc_of(index):
        bound = 0
        doc = jnp.zeros(index.shape, I32)
        for d in range(docs_ref.shape[0]):
            bound = bound + docs_ref[d]
            doc = doc + jnp.where(index >= bound, 1, 0)
        return doc

    mine = doc_of(block)
    for k in range(width // tokens):
        same = (doc_of(block + k) == mine) & (block + k < spans)
        mask_ref[:, k * tokens : (k + 1) * tokens] = jnp.where(same, 1.0, 0.0).astype(BF16)


def conv_kernel(grad_ref, gate_ref, toep_ref, mask_ref, out_ref, moved_ref, sums_ref, *, per_group):
    step = pl.program_id(0)
    spans, rows, tokens = grad_ref.shape
    here = rows // per_group
    lags = mask_ref.shape[1]
    reach = lags // tokens
    channels = out_ref.shape[1] - EXTRA

    @pl.when(step == 0)
    def _():
        moved_ref[...] = jnp.zeros(moved_ref.shape, BF16)
        sums_ref[...] = jnp.zeros(sums_ref.shape, F32)

    flip = lax.broadcasted_iota(I32, (tokens, tokens), 0) + lax.broadcasted_iota(I32, (tokens, tokens), 1)
    flip = jnp.where(flip == tokens - 1, 1.0, 0.0).astype(BF16)
    for g in range(here):
        grad = grad_ref[:, g * per_group : (g + 1) * per_group, :].reshape(spans * per_group, tokens)
        for k in range(reach):
            keep = (spans - k) * per_group
            cols = slice(k * tokens, (k + 1) * tokens)
            moved_ref[g, :keep, cols] = grad[k * per_group :, :] * mask_ref[:keep, cols]
        moved = moved_ref[g]
        back = dot(moved, toep_ref[g], NT)
        start = pl.multiple_of((step * here + g) * per_group, per_group)
        out_ref[:, pl.ds(start, per_group), :] = back.astype(BF16).reshape(spans, per_group, tokens)
        gate = gate_ref[:, g * per_group : (g + 1) * per_group, :].reshape(spans * per_group, tokens)
        gate_t = dot(flip, gate, NT).astype(BF16)
        corr = dot(gate_t, moved, NN)
        wide = jnp.concatenate([corr, jnp.zeros((tokens, tokens), F32)], axis=1)
        skewed = pltpu.roll(wide, lags + 1, 1, stride=1, stride_axis=0)
        sums_ref[pl.ds(step * here + g, 1), :] = jnp.sum(skewed[:, :lags], axis=0, keepdims=True)

    @pl.when(step == pl.num_programs(0) - 1)
    def _():
        for k in range(spans):
            if k < reach:
                exact = sums_ref[:, k * tokens : (k + 1) * tokens]
                high = exact.astype(BF16).astype(F32)
                both = jnp.concatenate([high, exact - high], axis=0).astype(BF16)
            else:
                both = jnp.zeros((EXTRA, tokens), BF16)
            out_ref[k, channels:, :] = both


def skip_kernel(conv_ref, skip_ref, out_ref):
    out_ref[...] = conv_ref[...].astype(F32).T * skip_ref[...]


def gates_kernel(
    back_ref, rank_ref, skip_ref, query_ref, key_ref, grad_query_ref, grad_key_ref, filt_ref, sorted_ref, *, sub_groups
):
    spans, rows, tokens = back_ref.shape
    sub = rows - EXTRA

    @pl.when(pl.program_id(0) == 0)
    def _():
        flat = back_ref[:, :sub, :].reshape(spans * sub, tokens)
        sorted_ref[...] = flat.T
        for d in range(spans):
            tail = back_ref[d, sub:, :].astype(F32)
            both = tail[: EXTRA // 2] + tail[EXTRA // 2 :]
            filt_ref[d * sub_groups : (d + 1) * sub_groups, :] = both[:sub_groups]

    channels = sorted_ref.shape[1]
    conv = dot(sorted_ref[...], one_hot(rank_ref[...], 0, channels), NN)
    gated_grad = conv + skip_ref[...]
    grad_query_ref[...] = (gated_grad * key_ref[...].astype(F32)).astype(BF16)
    grad_key_ref[...] = (gated_grad * query_ref[...].astype(F32)).astype(BF16)


def whole(shape):
    return pl.BlockSpec(shape, lambda *_: (0,) * len(shape))


def scalars():
    return pl.BlockSpec(memory_space=pltpu.SMEM)


def per_device(
    query_proj, key_proj, value_proj, grad_out, out_proj, filters, skip_gain, doc_lengths, group_of
):
    tokens, channels = query_proj.shape
    groups = filters.shape[0]
    per_group = channels // groups
    spans = lax.axis_size("ctx")
    heads = lax.axis_size("head")
    position = lax.axis_index("ctx")
    head = lax.axis_index("head")
    sub = channels // spans
    sub_groups = sub // per_group
    reach = spans // 2 + 1
    lags = reach * tokens
    chunk = min(256, channels)

    arrived = [
        lax.ppermute(grad_out, "head", [(i, (i + r) % heads) for i in range(heads)])
        for r in range(1, heads)
    ]

    gate_sorted, rank = pl.pallas_call(
        functools.partial(gate_kernel, groups=groups, per_group=per_group, chunk=chunk),
        out_shape=(
            jax.ShapeDtypeStruct((spans, sub, tokens), BF16),
            jax.ShapeDtypeStruct((1, channels), I32),
        ),
        in_specs=[scalars(), whole((1, channels)), whole((tokens, channels)), whole((tokens, channels))],
        out_specs=(whole((spans, sub, tokens)), whole((1, channels))),
        compiler_params=params(),
        name="gate",
    )(head.reshape(1), group_of.reshape(1, channels), query_proj, key_proj)
    gate_moved = lax.all_to_all(gate_sorted, "ctx", 0, 0)

    block = min(256, channels)
    feats = grad_out.shape[1]
    steps = channels // block
    acc = None
    for r, grad in enumerate([grad_out] + arrived):
        source = ((head + heads - r) % heads).reshape(1)
        grad_spec = pl.BlockSpec((tokens, feats), lambda j, s: (0, 0))
        weight_spec = pl.BlockSpec((block, feats), lambda j, s: (j, s[0]))
        acc_spec = pl.BlockSpec((block, tokens), lambda j, s: (j, 0))
        if r < heads - 1:
            first = acc is None
            acc = pl.pallas_call(
                partial_kernel if first else add_kernel,
                out_shape=jax.ShapeDtypeStruct((channels, tokens), F32),
                grid_spec=pltpu.PrefetchScalarGridSpec(
                    num_scalar_prefetch=1,
                    grid=(steps,),
                    in_specs=[grad_spec, weight_spec] + ([] if first else [acc_spec]),
                    out_specs=acc_spec,
                ),
                compiler_params=params(),
                name="own" if first else "more",
            )(source, grad, out_proj, *([] if first else [acc]))
        else:
            conv_sorted, conv_grad = pl.pallas_call(
                functools.partial(last_kernel, chunk=chunk),
                out_shape=(
                    jax.ShapeDtypeStruct((spans, sub, tokens), BF16),
                    jax.ShapeDtypeStruct((channels, tokens), BF16),
                ),
                grid_spec=pltpu.PrefetchScalarGridSpec(
                    num_scalar_prefetch=1,
                    grid=(steps,),
                    in_specs=[
                        pl.BlockSpec((1, channels), lambda j, s: (0, 0)),
                        grad_spec,
                        weight_spec,
                        acc_spec,
                        pl.BlockSpec((tokens, block), lambda j, s: (0, j)),
                    ],
                    out_specs=(
                        pl.BlockSpec((spans, sub, tokens), lambda j, s: (0, 0, 0)),
                        pl.BlockSpec((channels, tokens), lambda j, s: (0, 0)),
                    ),
                ),
                compiler_params=params(),
                name="last",
            )(source, rank, grad, out_proj, acc, value_proj)
    conv_moved = lax.all_to_all(conv_sorted, "ctx", 0, 0)

    filt_sub = lax.dynamic_slice(filters, (position * sub_groups, 0), (sub_groups, lags)).astype(F32)
    toep, mask = pl.pallas_call(
        functools.partial(prepare_kernel, per_group=per_group, spans=spans),
        out_shape=(
            jax.ShapeDtypeStruct((sub_groups, tokens, lags), BF16),
            jax.ShapeDtypeStruct((spans * per_group, lags), BF16),
        ),
        in_specs=[scalars(), whole((sub_groups, lags))],
        out_specs=(whole((sub_groups, tokens, lags)), whole((spans * per_group, lags))),
        compiler_params=params(),
        name="prepare",
    )(doc_lengths, filt_sub)
    skip_part = pl.pallas_call(
        skip_kernel,
        out_shape=jax.ShapeDtypeStruct((tokens, channels), F32),
        in_specs=[whole((channels, tokens)), whole((1, channels))],
        out_specs=whole((tokens, channels)),
        compiler_params=params(),
        name="skip",
    )(conv_grad, skip_gain.reshape(1, channels))

    here = 2 if sub_groups % 2 == 0 else 1
    back = pl.pallas_call(
        functools.partial(conv_kernel, per_group=per_group),
        out_shape=jax.ShapeDtypeStruct((spans, sub + EXTRA, tokens), BF16),
        grid=(sub_groups // here,),
        in_specs=[
            pl.BlockSpec((spans, here * per_group, tokens), lambda g: (0, g, 0)),
            pl.BlockSpec((spans, here * per_group, tokens), lambda g: (0, g, 0)),
            pl.BlockSpec((here, tokens, lags), lambda g: (g, 0, 0)),
            whole((spans * per_group, lags)),
        ],
        out_specs=whole((spans, sub + EXTRA, tokens)),
        scratch_shapes=[
            pltpu.VMEM((here, spans * per_group, lags), BF16),
            pltpu.VMEM((EXTRA // 2, lags), F32),
        ],
        compiler_params=params(),
        name="conv",
    )(conv_moved, gate_moved, toep, mask)
    back_moved = lax.all_to_all(back, "ctx", 0, 0)

    cols = pl.BlockSpec((tokens, block), lambda j: (0, j))
    grad_query, grad_key, grad_filters = pl.pallas_call(
        functools.partial(gates_kernel, sub_groups=sub_groups),
        out_shape=(
            jax.ShapeDtypeStruct((tokens, channels), BF16),
            jax.ShapeDtypeStruct((tokens, channels), BF16),
            jax.ShapeDtypeStruct((groups, tokens), F32),
        ),
        grid=(steps,),
        in_specs=[
            whole((spans, sub + EXTRA, tokens)),
            pl.BlockSpec((1, block), lambda j: (0, j)),
            cols,
            cols,
            cols,
        ],
        out_specs=(cols, cols, whole((groups, tokens))),
        scratch_shapes=[pltpu.VMEM((tokens, channels), BF16)],
        compiler_params=params(),
        name="gates",
    )(back_moved, rank, skip_part, query_proj, key_proj)
    return (grad_query, grad_key, grad_filters)


def solution(mesh):
    in_specs = (
        P("ctx", "head"),
        P("ctx", "head"),
        P("ctx", "head"),
        P("ctx", "head"),
        P("head", None),
        P("head", None),
        P("head"),
        P(),
        P("head"),
    )
    out_specs = (P("ctx", "head"), P("ctx", "head"), P("head", "ctx"))
    return jax.shard_map(
        per_device, mesh=mesh, in_specs=in_specs, out_specs=out_specs, check_vma=False
    )
```

time: 319 us -> 94.7 us (0.30)
  local copies, waits for them, and re-layouts: 178 us -> 2.43 us
  Pallas kernels: 0 us -> 42.8 us
  matrix products: 26.1 us -> 0 us
  other arithmetic: 22.5 us -> 1.35 us
  blocking collectives: 16.9 us -> 0 us
  between operations: 14.4 us -> 0.68 us
  waiting for transfers between devices: 34.3 us -> 27.4 us
  starting transfers between devices: 24.1 us -> 18.9 us
    reshape x4 -> x0, local copies, waits for them, and re-layouts: 65 us -> none  [the longest x1 26.6 us: diagonal_sums(): rows_view = flat.reshape(lead + (block_rows, 2 * block_rows + 1))]
    gather x9 -> x0, local copies, waits for them, and re-layouts: 53.1 us -> none  [the longest x1 11.8 us: per_device(): skip_sorted = jnp.take(skip_gain, ranking)]
    pallas_call x0 -> x7, Pallas kernels: none -> 42.8 us  [the longest x1 11.2 us: per_device(): pl.pallas_call(functools.partial(last_kernel, chunk=chunk), out_shape=(ja...]
    dot_general x3 -> x0, matrix products: 26.1 us -> none  [the longest x1 11.8 us: per_device(): jnp.einsum('tm,cm->tc', lax.all_gather(grad_out, 'head', axis=1, tiled=Tr...]
    concatenate x4 -> x0, local copies, waits for them, and re-layouts: 22.3 us -> none  [the longest x1 11.3 us: diagonal_sums(): jnp.concatenate([flat, jnp.zeros(lead + (block_rows,), matrix.dtype)], -1)]
    unnamed x21 -> x8, local copies, waits for them, and re-layouts: 23.7 us -> 2.43 us
    all_to_all x1 -> x0, blocking collectives: 16.9 us -> none  [per_device(): lax.all_to_all(key_part, 'ctx', split_axis=0, concat_axis=1, tiled=True)]
    sort x2 -> x0, other arithmetic: 10.1 us -> none  [the longest x1 5.04 us: per_device(): ranking = jnp.argsort(local_group)]
  transfers between devices with their start and end apart: 6 -> 4, of which waited for: 5 -> 3; matrix products, arithmetic and copies ran while one was open for 33% -> 1% of each run, Pallas kernels for 0% -> 27%
where the time goes in v1:
time: 94.7 us; the launch traced here: 93.6 us
  Pallas kernels  42.8 us (45%)
  waiting for transfers between devices  27.4 us (29%)
  starting transfers between devices  18.9 us (20%)
  local copies, waits for them, and re-layouts  2.43 us (3%)
  other arithmetic  1.35 us (1%)
    all_to_all x1, waiting for transfers between devices, per_device(): back_moved = lax.all_to_all(back, 'ctx', 0, 0)  13.1 us
    pallas_call x1, Pallas kernels, per_device(): pl.pallas_call(functools.partial(last_kernel, chunk=chunk), out_shape=(ja...  11.2 us
    all_to_all x1, waiting for transfers between devices, per_device(): conv_moved = lax.all_to_all(conv_sorted, 'ctx', 0, 0)  9.85 us
    pallas_call x1, Pallas kernels, per_device(): pl.pallas_call(partial_kernel if first else add_kernel, out_shape=jax.Sha...  8.42 us
    all_to_all x1, starting transfers between devices, per_device(): gate_moved = lax.all_to_all(gate_sorted, 'ctx', 0, 0)  7.39 us
    pallas_call x1, Pallas kernels, per_device(): pl.pallas_call(functools.partial(gates_kernel, sub_groups=sub_groups), ou...  7.1 us
    pallas_call x1, Pallas kernels, per_device(): pl.pallas_call(functools.partial(conv_kernel, per_group=per_group), out_s...  6.14 us
    all_to_all x1, starting transfers between devices, per_device(): conv_moved = lax.all_to_all(conv_sorted, 'ctx', 0, 0)  5.73 us
  transfers between devices with their start and end apart: 4, of which 3 were waited for; matrix products, arithmetic and copies ran while one was open for 1% of the time, Pallas kernels for 27%

profile of v1, /device:TPU:0, one launch (start us, length us, event | category | flops | bytes accessed | tf_op | source)
XLA Modules:
  0.0 93.6 jit_solution(10089886133791440088)
XLA Ops:
  0.6 4.7 %gate.1 = (bf16[16,128,128]{2,1,0:T(8,128)(2,1)}, s32[1,2048]{1,0:T(1,128)}) custom-call(s32[1]{0:T(128)} %bitcast.1.head_ref, s32[1,2048]{1,0:T(1,128)} %bitcast.5, bf16[128,2048]{1,0:T(8,128)(2,1)} %query_ref.3, bf16[128,2048]{1,0:T(8,128)(2,1)} %key_ref.3), custom_call_target="tpu_custom_call" | custom-call | tf_op jit(solution)/shard_map/gate/pallas_call | solution.py:207
  5.3 7.4 %all-to-all-start.1 = ((bf16[16,128,128]{2,1,0:T(8,128)(2,1)}), bf16[16,128,128]{2,1,0:T(8,128)(2,1)S(1)}, u32[]{:S(2)}, u32[]{:S(2)}) async-start(bf16[16,128,128]{2,1,0:T(8,128)(2,1)} %get-tuple-element.11), calls=%async_computation.1 | async-start | bytes 1048576 | tf_op jit(solution)/shard_map/all_to_all | solution.py:218
  12.7 1.6 %collective-permute-start = (bf16[128,2048]{1,0:T(8,128)(2,1)}, bf16[128,2048]{1,0:T(8,128)(2,1)S(1)}, u32[]{:S(2)}, u32[]{:S(2)}) collective-permute-start(bf16[128,2048]{1,0:T(8,128)(2,1)} %grad_ref.1), channel_id=1, source_target_pairs={{0,1},{1,0},{2,3},{3,2},{4,5},{5,4},{6,7},{7,6},{8,9},{9,8},{10,11... | collective-permute-start | bytes 1572872 | tf_op jit(solution)/shard_map/ppermute | solution.py:203
  14.3 8.4 %own.1.acc_ref = f32[2048,128]{1,0:T(8,128)} custom-call(s32[1]{0:T(128)} %bitcast.3.half_ref, bf16[128,2048]{1,0:T(8,128)(2,1)} %grad_ref.1, bf16[2048,4096]{1,0:T(8,128)(2,1)} %weight_ref.3), custom_call_target="tpu_custom_call" | custom-call | tf_op jit(solution)/shard_map/own/pallas_call | solution.py:231
  22.7 4.4 %collective-permute-done.grad_ref = bf16[128,2048]{1,0:T(8,128)(2,1)S(1)} collective-permute-done((bf16[128,2048]{1,0:T(8,128)(2,1)}, bf16[128,2048]{1,0:T(8,128)(2,1)S(1)}, u32[]{:S(2)}, u32[]{:S(2)}) %collective-permute-start) | collective-permute-done | bytes 524320 | tf_op jit(solution)/shard_map/ppermute | solution.py:203
  27.1 0.0 copy-start.3
  27.1 0.8 copy-done.3
  27.9 11.2 %last.1 = (bf16[16,128,128]{2,1,0:T(8,128)(2,1)}, bf16[2048,128]{1,0:T(8,128)(2,1)}) custom-call(s32[1]{0:T(128)} %bitcast.half_ref, s32[1,2048]{1,0:T(1,128)} %get-tuple-element.9.rank_ref, bf16[128,2048]{1,0:T(8,128)(2,1)} %copy-done.3, bf16[2048,4096]{1,0:T(8,128)(2,1)} %weight_ref.3, f32[2048,128]{1,0:T(8,128)} %own.1.acc_ref, bf16[128,2048]{1,0:T(8,128)(2,1)} %value_ref.1), custom_call_target="tpu_custom_call" | custom-call | tf_op jit(solution)/shard_map/last/pallas_call | solution.py:244
  39.1 0.0 all-to-all-done.1.gate_ref
  39.1 0.0 copy-start.1
  39.1 5.7 %all-to-all-start = ((bf16[16,128,128]{2,1,0:T(8,128)(2,1)}), bf16[16,128,128]{2,1,0:T(8,128)(2,1)S(1)}, u32[]{:S(2)}, u32[]{:S(2)}) async-start(bf16[16,128,128]{2,1,0:T(8,128)(2,1)} %get-tuple-element.10), calls=%async_computation | async-start | bytes 1048576 | tf_op jit(solution)/shard_map/all_to_all | solution.py:268
  44.9 1.3 %dynamic-slice_convert_fusion.filt_ref = f32[8,1152]{1,0:T(8,128)} fusion(bf16[128,2048]{1,0:T(8,128)(2,1)} %param.14, s32[]{:T(128)S(6)} %select_n.16), kind=kLoop, calls=%fused_computation | loop fusion | flops 9216 | bytes 55300 | tf_op jit(solution)/shard_map/convert_element_type | solution.py:270
  46.2 3.1 %prepare.1 = (bf16[8,128,1152]{2,1,0:T(8,128)(2,1)}, bf16[256,1152]{1,0:T(8,128)(2,1)}) custom-call(s32[4]{0:T(128)} %docs_ref.1, f32[8,1152]{1,0:T(8,128)} %dynamic-slice_convert_fusion.filt_ref), custom_call_target="tpu_custom_call" | custom-call | tf_op jit(solution)/shard_map/prepare/pallas_call | solution.py:271
  49.3 9.9 %all-to-all-done.grad_ref = bf16[16,128,128]{2,1,0:T(8,128)(2,1)S(1)} async-done(((bf16[16,128,128]{2,1,0:T(8,128)(2,1)}), bf16[16,128,128]{2,1,0:T(8,128)(2,1)S(1)}, u32[]{:S(2)}, u32[]{:S(2)}) %all-to-all-start) | async-done | bytes 524320 | tf_op jit(solution)/shard_map/all_to_all | solution.py:268
  59.1 0.0 copy-start.2
  59.1 0.0 copy-done.1
  59.1 0.8 copy-done.2
  59.9 6.1 %conv.1 = bf16[16,144,128]{2,1,0:T(8,128)(2,1)} custom-call(bf16[16,128,128]{2,1,0:T(8,128)(2,1)} %copy-done.2, bf16[16,128,128]{2,1,0:T(8,128)(2,1)} %copy-done.1, bf16[8,128,1152]{2,1,0:T(8,128)(2,1)} %get-tuple-element.12.toep_ref, bf16[256,1152]{1,0:T(8,128)(2,1)} %get-tuple-element.13.mask_ref), custom_call_target="tpu_custom_call" | custom-call | tf_op jit(solution)/shard_map/conv/pallas_call | solution.py:292
  66.1 4.2 %all-to-all-start.2 = ((bf16[16,144,128]{2,1,0:T(8,128)(2,1)}), bf16[16,144,128]{2,1,0:T(8,128)(2,1)S(1)}, u32[]{:S(2)}, u32[]{:S(2)}) async-start(bf16[16,144,128]{2,1,0:T(8,128)(2,1)} %conv.1), calls=%async_computation.2 | async-start | bytes 1179648 | tf_op jit(solution)/shard_map/all_to_all | solution.py:310
  70.2 2.2 %skip.1.skip_ref = f32[128,2048]{1,0:T(8,128)} custom-call(bf16[2048,128]{1,0:T(8,128)(2,1)} %get-tuple-element.14.conv_ref, f32[1,2048]{1,0:T(1,128)} %bitcast.6), custom_call_target="tpu_custom_call" | custom-call | tf_op jit(solution)/shard_map/skip/pallas_call | solution.py:282
  72.5 13.1 %all-to-all-done.2.back_ref = bf16[16,144,128]{2,1,0:T(8,128)(2,1)S(1)} async-done(((bf16[16,144,128]{2,1,0:T(8,128)(2,1)}), bf16[16,144,128]{2,1,0:T(8,128)(2,1)S(1)}, u32[]{:S(2)}, u32[]{:S(2)}) %all-to-all-start.2) | async-done | bytes 589856 | tf_op jit(solution)/shard_map/all_to_all | solution.py:310
  85.6 0.0 copy-start
  85.6 0.8 copy-done
  86.5 7.1 %gates.1 = (bf16[128,2048]{1,0:T(8,128)(2,1)}, bf16[128,2048]{1,0:T(8,128)(2,1)}, f32[128,128]{1,0:T(8,128)}) custom-call(bf16[16,144,128]{2,1,0:T(8,128)(2,1)} %copy-done, s32[1,2048]{1,0:T(1,128)} %get-tuple-element.9.rank_ref, f32[128,2048]{1,0:T(8,128)} %skip.1.skip_ref, bf16[128,2048]{1,0:T(8,128)(2,1)} %query_ref.3, bf16[128,2048]{1,0:T(8,128)(2,1)} %key_ref.3), custom_call_target="tpu_custom_call" | custom-call | tf_op jit(solution)/shard_map/gates/pallas_call | solution.py:313
Async XLA Ops:
  5.3 33.8 %all-to-all-start.1 = ((bf16[16,128,128]{2,1,0:T(8,128)(2,1)}), bf16[16,128,128]{2,1,0:T(8,128)(2,1)S(1)}, u32[]{:S(2)}, u32[]{:S(2)}) async-start(bf16[16,128,128]{2,1,0:T(8,128)(2,1)} %get-tuple-element.11), calls=%async_computation.1 | async-start | bytes 1048576 | tf_op jit(solution)/shard_map/all_to_all | solution.py:218
  12.7 14.4 %collective-permute-start = (bf16[128,2048]{1,0:T(8,128)(2,1)}, bf16[128,2048]{1,0:T(8,128)(2,1)S(1)}, u32[]{:S(2)}, u32[]{:S(2)}) collective-permute-start(bf16[128,2048]{1,0:T(8,128)(2,1)} %grad_ref.1), channel_id=1, source_target_pairs={{0,1},{1,0},{2,3},{3,2},{4,5},{5,4},{6,7},{7,6},{8,9},{9,8},{10,11... | collective-permute-start | bytes 1572872 | tf_op jit(solution)/shard_map/ppermute | solution.py:203
  27.1 0.8 copy-start.3
  39.1 20.0 %copy-start.1 = (bf16[16,128,128]{2,1,0:T(8,128)(2,1)}, bf16[16,128,128]{2,1,0:T(8,128)(2,1)S(1)}, u32[]{:S(2)}) copy-start(bf16[16,128,128]{2,1,0:T(8,128)(2,1)S(1)} %all-to-all-done.1.gate_ref) | copy-start | bytes 1572868
  39.1 20.0 %all-to-all-start = ((bf16[16,128,128]{2,1,0:T(8,128)(2,1)}), bf16[16,128,128]{2,1,0:T(8,128)(2,1)S(1)}, u32[]{:S(2)}, u32[]{:S(2)}) async-start(bf16[16,128,128]{2,1,0:T(8,128)(2,1)} %get-tuple-element.10), calls=%async_computation | async-start | bytes 1048576 | tf_op jit(solution)/shard_map/all_to_all | solution.py:268
  59.1 0.8 copy-start.2
  66.1 19.5 %all-to-all-start.2 = ((bf16[16,144,128]{2,1,0:T(8,128)(2,1)}), bf16[16,144,128]{2,1,0:T(8,128)(2,1)S(1)}, u32[]{:S(2)}, u32[]{:S(2)}) async-start(bf16[16,144,128]{2,1,0:T(8,128)(2,1)} %conv.1), calls=%async_computation.2 | async-start | bytes 1179648 | tf_op jit(solution)/shard_map/all_to_all | solution.py:310
  85.6 0.8 copy-start

commit v2 on v0

v2 whole, which is shorter than its diff:
```python
import functools

import jax
import jax.numpy as jnp
from jax import lax
from jax.experimental import pallas as pl
from jax.experimental.pallas import tpu as pltpu
from jax.sharding import PartitionSpec as P

F32 = jnp.float32
BF16 = jnp.bfloat16
I32 = jnp.int32
NT = (((1,), (1,)), ((), ()))
NN = (((1,), (0,)), ((), ()))
LANES = 128
EXTRA = 16
VMEM = pl.BlockSpec(memory_space=pltpu.VMEM)
SMEM = pl.BlockSpec(memory_space=pltpu.SMEM)
ANY = pl.BlockSpec(memory_space=pl.ANY)


def dot(a, b, dims):
    return lax.dot_general(a, b, dims, preferred_element_type=F32)


def on_chip(x):
    return pltpu.with_memory_space_constraint(x, pltpu.VMEM)


def call(kernel, out_shape, in_specs, scratch=(), out_specs=None):
    return pl.pallas_call(
        kernel,
        out_shape=out_shape,
        in_specs=in_specs,
        out_specs=jax.tree.map(lambda _: VMEM, out_shape) if out_specs is None else out_specs,
        scratch_shapes=scratch,
        compiler_params=pltpu.CompilerParams(vmem_limit_bytes=56 * 1024 * 1024),
    )


def rank_column(rank_row, column_ref):
    wide = jnp.broadcast_to(rank_row.astype(F32), (LANES, rank_row.shape[1]))
    column_ref[...] = wide.T.astype(I32)


def permute(by_token, column_ref, out_ref):
    channels = column_ref.shape[0]
    rows = out_ref.shape[1]
    width = min(2 * LANES, channels)
    lane = lax.broadcasted_iota(I32, (channels, LANES), 1)
    for p in range(0, channels, width):
        picks = [
            jnp.where(column_ref[...] == lane + (p + q), 1.0, 0.0).astype(BF16)
            for q in range(0, width, LANES)
        ]
        moved = dot(by_token, jnp.concatenate(picks, axis=1), NN).T.astype(BF16)
        out_ref[p // rows : (p + width) // rows] = moved.reshape(width // rows, rows, -1)


def gate_kernel(
    head_ref, group_ref, query_hbm, key_hbm, out_ref, rank_ref, query_ref, key_ref, column_ref, sem, *, groups, per_group
):
    loads = [
        pltpu.make_async_copy(query_hbm, query_ref, sem.at[0]),
        pltpu.make_async_copy(key_hbm, key_ref, sem.at[1]),
    ]
    for load in loads:
        load.start()
    channels = group_ref.shape[1]
    local = group_ref[...] - head_ref[0] * groups
    upper = lax.broadcasted_iota(I32, (LANES, LANES), 0) < lax.broadcasted_iota(I32, (LANES, LANES), 1)
    upper = jnp.where(upper, 1.0, 0.0).astype(BF16)
    base = jnp.zeros((groups, 1), F32)
    for b in range(channels // LANES):
        here = local[:, b * LANES : (b + 1) * LANES]
        member = jnp.where(lax.broadcasted_iota(I32, (groups, LANES), 0) == here, 1.0, 0.0)
        before = dot(member.astype(BF16), upper, NN) + base
        place = jnp.sum(member * before, axis=0, keepdims=True)
        rank_ref[:, b * LANES : (b + 1) * LANES] = here * per_group + place.astype(I32)
        base = base + jnp.sum(member, axis=1, keepdims=True)
    rank_column(rank_ref[...], column_ref)
    for load in loads:
        load.wait()
    gated = (query_ref[...].astype(F32) * key_ref[...].astype(F32)).astype(BF16)
    permute(gated, column_ref, out_ref)


def stream_weights(half, weight_hbm, weight_ref, sem):
    _, feats = weight_ref.shape
    count = sem.shape[0]
    width = feats // count
    copies = [
        pltpu.make_async_copy(
            weight_hbm.at[:, pl.ds(pl.multiple_of(half * feats + j * width, width), width)],
            weight_ref.at[:, pl.ds(j * width, width)],
            sem.at[j],
        )
        for j in range(count)
    ]
    for copy in copies:
        copy.start()
    return copies, width


def product(copies, width, grad_ref, weight_ref, out_ref, fresh):
    for j, copy in enumerate(copies):
        copy.wait()
        cols = slice(j * width, (j + 1) * width)
        part = dot(grad_ref[:, cols], weight_ref[:, cols], NT)
        out_ref[...] = part if fresh and j == 0 else out_ref[...] + part


def partial_kernel(half_ref, grad_hbm, weight_hbm, *refs):
    *acc, out_ref, grad_ref, weight_ref, sem, grad_sem = refs
    load = pltpu.make_async_copy(grad_hbm, grad_ref, grad_sem)
    load.start()
    copies, width = stream_weights(half_ref[0], weight_hbm, weight_ref, sem)
    if acc:
        out_ref[...] = acc[0][...]
    load.wait()
    product(copies, width, grad_ref, weight_ref, out_ref, not acc)


def last_kernel(
    half_ref, rank_ref, grad_ref, acc_ref, weight_hbm, value_hbm, out_ref, conv_ref, total_ref, weight_ref, value_ref, column_ref, sem, value_sem
):
    load = pltpu.make_async_copy(value_hbm, value_ref, value_sem)
    copies, width = stream_weights(half_ref[0], weight_hbm, weight_ref, sem)
    load.start()
    rank_column(rank_ref[...], column_ref)
    total_ref[...] = acc_ref[...]
    product(copies, width, grad_ref, weight_ref, total_ref, False)
    load.wait()
    conv_ref[...] = (total_ref[...] * value_ref[...].astype(F32)).astype(BF16)
    permute(conv_ref[...], column_ref, out_ref)


def prepare_kernel(docs_ref, filt_ref, gate_ref, skip_ref, gate_t_ref, rows_ref, doc_ref, skip_out_ref, *, per_group):
    spans, _, tokens = gate_ref.shape
    groups, lags = filt_ref.shape
    flip = lax.broadcasted_iota(I32, (tokens, tokens), 0) + lax.broadcasted_iota(I32, (tokens, tokens), 1)
    flip = jnp.where(flip == tokens - 1, 1.0, 0.0).astype(BF16)
    for g in range(groups):
        gate = gate_ref[:, g * per_group : (g + 1) * per_group, :].reshape(spans * per_group, tokens)
        gate_t_ref[g] = dot(flip, gate, NT).astype(BF16)
    rows_ref[:, :lags] = filt_ref[...]
    rows_ref[:, lags:] = jnp.zeros((groups, tokens), F32)
    index = lax.broadcasted_iota(I32, doc_ref.shape, 0) // per_group
    bound = 0
    doc = jnp.zeros(doc_ref.shape, F32)
    for d in range(docs_ref.shape[0]):
        bound = bound + docs_ref[d]
        doc = doc + jnp.where(index >= bound, 1.0, 0.0)
    doc_ref[...] = doc
    skip_out_ref[...] = skip_ref[...]


def conv_kernel(grad_ref, gate_t_ref, rows_ref, doc_ref, out_ref, moved_ref, sums_ref, *, per_group):
    spans, sub, tokens = grad_ref.shape
    groups, padded = rows_ref.shape
    lags = padded - tokens
    reach = lags // tokens
    for k in range(reach):
        cut = k * per_group
        keep = (spans - k) * per_group
        same = jnp.where(doc_ref[cut:, :] == doc_ref[:keep, :], 1.0, 0.0).astype(BF16)
        cols = slice(k * tokens, (k + 1) * tokens)
        for g in range(groups):
            grad = grad_ref[k:, g * per_group : (g + 1) * per_group, :].reshape(keep, tokens)
            moved_ref[g, :keep, cols] = grad * same
            if k:
                moved_ref[g, keep:, cols] = jnp.zeros((cut, tokens), BF16)
    sums_ref[...] = jnp.zeros(sums_ref.shape, F32)
    for g in range(groups):
        moved = moved_ref[g]
        wide = jnp.broadcast_to(rows_ref[g : g + 1, :], (tokens, padded))
        toeplitz = pltpu.roll(wide, 0, 1, stride=1, stride_axis=0)[:, :lags].astype(BF16)
        back = dot(moved, toeplitz, NT)
        out_ref[:, g * per_group : (g + 1) * per_group, :] = back.astype(BF16).reshape(spans, per_group, tokens)
        corr = dot(gate_t_ref[g], moved, NN)
        wide = jnp.concatenate([corr, jnp.zeros((tokens, tokens), F32)], axis=1)
        skewed = pltpu.roll(wide, lags + 1, 1, stride=1, stride_axis=0)
        sums_ref[g : g + 1, :] = jnp.sum(skewed[:, :lags], axis=0, keepdims=True)
    for k in range(spans):
        if k < reach:
            exact = sums_ref[:, k * tokens : (k + 1) * tokens]
            high = exact.astype(BF16).astype(F32)
            both = jnp.concatenate([high, exact - high], axis=0).astype(BF16)
        else:
            both = jnp.zeros((EXTRA, tokens), BF16)
        out_ref[k, sub:, :] = both


def gates_kernel(
    back_ref, rank_ref, conv_ref, skip_ref, query_hbm, key_hbm, grad_query_hbm, grad_key_hbm, filt_hbm,
    query_ref, key_ref, grad_query_ref, grad_key_ref, filt_ref, sorted_ref, load_sem, store_sem, filt_sem, *, sub_groups
):
    spans, rows, tokens = back_ref.shape
    sub = rows - EXTRA
    channels = rank_ref.shape[1]
    loads = [
        pltpu.make_async_copy(query_hbm, query_ref, load_sem.at[0]),
        pltpu.make_async_copy(key_hbm, key_ref, load_sem.at[1]),
    ]
    for load in loads:
        load.start()
    for d in range(spans):
        tail = back_ref[d, sub:, :].astype(F32)
        both = tail[: EXTRA // 2] + tail[EXTRA // 2 :]
        filt_ref[d * sub_groups : (d + 1) * sub_groups, :] = both[:sub_groups]
    stores = [pltpu.make_async_copy(filt_ref, filt_hbm, filt_sem)]
    stores[0].start()
    sorted_ref[...] = back_ref[:, :sub, :].reshape(spans * sub, tokens).T
    for load in loads:
        load.wait()
    width = channels // store_sem.shape[1]
    for j in range(store_sem.shape[1]):
        cols = slice(j * width, (j + 1) * width)
        place = lax.broadcasted_iota(I32, (channels, width), 0)
        picks = jnp.where(place == rank_ref[:, cols], 1.0, 0.0).astype(BF16)
        gated_grad = dot(sorted_ref[...], picks, NN) + conv_ref[:, cols].astype(F32) * skip_ref[:, cols]
        grad_query_ref[:, cols] = (gated_grad * key_ref[:, cols].astype(F32)).astype(BF16)
        grad_key_ref[:, cols] = (gated_grad * query_ref[:, cols].astype(F32)).astype(BF16)
        for which, (source, target) in enumerate(((grad_query_ref, grad_query_hbm), (grad_key_ref, grad_key_hbm))):
            part = pl.ds(j * width, width)
            stores.append(pltpu.make_async_copy(source.at[:, part], target.at[:, part], store_sem.at[which, j]))
            stores[-1].start()
    for store in stores:
        store.wait()


def per_device(
    query_proj, key_proj, value_proj, grad_out, out_proj, filters, skip_gain, doc_lengths, group_of
):
    tokens, channels = query_proj.shape
    groups = filters.shape[0]
    per_group = channels // groups
    spans = lax.axis_size("ctx")
    heads = lax.axis_size("head")
    position = lax.axis_index("ctx")
    head = lax.axis_index("head")
    sub = channels // spans
    sub_groups = sub // per_group
    lags = (spans // 2 + 1) * tokens
    feats = grad_out.shape[1]
    dma = pltpu.SemaphoreType.DMA
    wide = pltpu.VMEM((tokens, channels), BF16)
    column = pltpu.VMEM((channels, LANES), I32)

    arrived = [lax.ppermute(grad_out, "head", [(i, (i + r) % heads) for i in range(heads)]) for r in range(1, heads)]

    gate_sorted, rank = call(
        functools.partial(gate_kernel, groups=groups, per_group=per_group),
        (pltpu.VMEM((spans, sub, tokens), BF16), pltpu.VMEM((1, channels), I32)),
        [SMEM, VMEM, ANY, ANY],
        [wide, wide, column, dma((2,))],
    )(head.reshape(1), group_of.reshape(1, channels), query_proj, key_proj)
    gate_moved = lax.all_to_all(gate_sorted, "ctx", 0, 0)

    parts = min(8, feats // LANES)
    acc = None
    for r, grad in enumerate([grad_out] + arrived):
        source = ((head + heads - r) % heads).reshape(1)
        if r < heads - 1:
            acc = call(
                partial_kernel,
                pltpu.VMEM((tokens, channels), F32),
                [SMEM, ANY, ANY] + ([] if acc is None else [VMEM]),
                [
                    pltpu.VMEM((tokens, feats), BF16),
                    pltpu.VMEM((channels, feats), BF16),
                    dma((parts,)),
                    dma,
                ],
            )(source, grad, out_proj, *([] if acc is None else [acc]))
            acc = on_chip(acc)
        else:
            conv_sorted, conv_grad = call(
                last_kernel,
                (pltpu.VMEM((spans, sub, tokens), BF16), pltpu.VMEM((tokens, channels), BF16)),
                [SMEM, VMEM, VMEM, VMEM, ANY, ANY],
                [
                    pltpu.VMEM((tokens, channels), F32),
                    pltpu.VMEM((channels, feats), BF16),
                    wide,
                    column,
                    dma((parts,)),
                    dma,
                ],
            )(source, on_chip(rank), on_chip(grad), acc, out_proj, value_proj)
    conv_moved = lax.all_to_all(on_chip(conv_sorted), "ctx", 0, 0)

    filt_sub = lax.dynamic_slice(filters, (position * sub_groups, 0), (sub_groups, lags)).astype(F32)
    gate_t, rows, doc, skip = call(
        functools.partial(prepare_kernel, per_group=per_group),
        (
            pltpu.VMEM((sub_groups, tokens, spans * per_group), BF16),
            pltpu.VMEM((sub_groups, lags + tokens), F32),
            pltpu.VMEM((spans * per_group, tokens), F32),
            pltpu.VMEM((1, channels), F32),
        ),
        [SMEM, VMEM, VMEM, VMEM],
    )(doc_lengths, filt_sub, on_chip(gate_moved), skip_gain.reshape(1, channels))

    back = call(
        functools.partial(conv_kernel, per_group=per_group),
        pltpu.VMEM((spans, sub + EXTRA, tokens), BF16),
        [VMEM] * 4,
        [
            pltpu.VMEM((sub_groups, spans * per_group, lags), BF16),
            pltpu.VMEM((EXTRA // 2, lags), F32),
        ],
    )(on_chip(conv_moved), on_chip(gate_t), on_chip(rows), on_chip(doc))
    back_moved = lax.all_to_all(on_chip(back), "ctx", 0, 0)

    return call(
        functools.partial(gates_kernel, sub_groups=sub_groups),
        (
            jax.ShapeDtypeStruct((tokens, channels), BF16),
            jax.ShapeDtypeStruct((tokens, channels), BF16),
            jax.ShapeDtypeStruct((groups, tokens), F32),
        ),
        [VMEM, VMEM, VMEM, VMEM, ANY, ANY],
        [wide, wide, wide, wide, pltpu.VMEM((groups, tokens), F32), wide, dma((2,)), dma((2, 8)), dma],
        (ANY, ANY, ANY),
    )(on_chip(back_moved), on_chip(rank), on_chip(conv_grad), on_chip(skip), query_proj, key_proj)


def solution(mesh):
    in_specs = (
        P("ctx", "head"),
        P("ctx", "head"),
        P("ctx", "head"),
        P("ctx", "head"),
        P("head", None),
        P("head", None),
        P("head"),
        P(),
        P("head"),
    )
    out_specs = (P("ctx", "head"), P("ctx", "head"), P("head", "ctx"))

    def body(*args):
        return tuple(per_device(*args))

    return jax.shard_map(body, mesh=mesh, in_specs=in_specs, out_specs=out_specs, check_vma=False)
```

time: 319 us -> 82.4 us (0.26)
  local copies, waits for them, and re-layouts: 178 us -> 0 us
  matrix products: 26.1 us -> 0 us
  Pallas kernels: 0 us -> 25.7 us
  other arithmetic: 22.5 us -> 1.35 us
  waiting for transfers between devices: 34.3 us -> 18.2 us
  between operations: 14.4 us -> 0.71 us
  starting transfers between devices: 24.1 us -> 14.7 us
  blocking collectives: 16.9 us -> 21.2 us
    reshape x4 -> x0, local copies, waits for them, and re-layouts: 65 us -> none  [the longest x1 26.6 us: diagonal_sums(): rows_view = flat.reshape(lead + (block_rows, 2 * block_rows + 1))]
    gather x9 -> x0, local copies, waits for them, and re-layouts: 53.1 us -> none  [the longest x1 11.8 us: per_device(): skip_sorted = jnp.take(skip_gain, ranking)]
    dot_general x3 -> x0, matrix products: 26.1 us -> none  [the longest x1 11.8 us: per_device(): jnp.einsum('tm,cm->tc', lax.all_gather(grad_out, 'head', axis=1, tiled=Tr...]
    pallas_call x0 -> x6, Pallas kernels: none -> 25.7 us  [the longest x1 6.68 us: per_device(): call(last_kernel, (pltpu.VMEM((spans, sub, tokens), BF16), pltpu.VMEM((to...]
    unnamed x21 -> x0, local copies, waits for them, and re-layouts: 23.7 us -> none
    concatenate x4 -> x0, local copies, waits for them, and re-layouts: 22.3 us -> none  [the longest x1 11.3 us: diagonal_sums(): jnp.concatenate([flat, jnp.zeros(lead + (block_rows,), matrix.dtype)], -1)]
    all_to_all x5 -> x2, waiting for transfers between devices: 28.8 us -> 11.8 us  [the longest x1 11.8 us: per_device(): conv_moved = lax.all_to_all(on_chip(conv_sorted), 'ctx', 0, 0)]
    all_to_all x5 -> x2, starting transfers between devices: 24 us -> 13.1 us  [the longest x1 7.4 us: per_device(): gate_moved = lax.all_to_all(gate_sorted, 'ctx', 0, 0)]
  transfers between devices with their start and end apart: 6 -> 3, of which waited for: 5 -> 2; matrix products, arithmetic and copies ran while one was open for 33% -> 2% of each run, Pallas kernels for 0% -> 17%
where the time goes in v2:
time: 82.4 us; the launch traced here: 81.9 us
  Pallas kernels  25.7 us (31%)
  blocking collectives  21.2 us (26%)
  waiting for transfers between devices  18.2 us (22%)
  starting transfers between devices  14.7 us (18%)
  other arithmetic  1.35 us (2%)
    all_to_all x1, blocking collectives, per_device(): back_moved = lax.all_to_all(on_chip(back), 'ctx', 0, 0)  21.2 us
    all_to_all x1, waiting for transfers between devices, per_device(): conv_moved = lax.all_to_all(on_chip(conv_sorted), 'ctx', 0, 0)  11.8 us
    all_to_all x1, starting transfers between devices, per_device(): gate_moved = lax.all_to_all(gate_sorted, 'ctx', 0, 0)  7.4 us
    pallas_call x1, Pallas kernels, per_device(): call(last_kernel, (pltpu.VMEM((spans, sub, tokens), BF16), pltpu.VMEM((to...  6.68 us
    pallas_call x1, Pallas kernels, per_device(): call(partial_kernel, pltpu.VMEM((tokens, channels), F32), [SMEM, ANY, ANY...  6.48 us
    ppermute x1, waiting for transfers between devices, per_device(): lax.ppermute(grad_out, 'head', [(i, (i + r) % heads) for i in range(heads)])  6.37 us
    all_to_all x1, starting transfers between devices, per_device(): conv_moved = lax.all_to_all(on_chip(conv_sorted), 'ctx', 0, 0)  5.72 us
    pallas_call x1, Pallas kernels, per_device(): call(functools.partial(gate_kernel, groups=groups, per_group=per_group),...  4.77 us
  transfers between devices with their start and end apart: 3, of which 2 were waited for; matrix products, arithmetic and copies ran while one was open for 2% of the time, Pallas kernels for 17%

profile of v2, /device:TPU:0, one launch (start us, length us, event | category | flops | bytes accessed | tf_op | source)
XLA Modules:
  0.0 81.9 jit_solution(14624486683255375927)
XLA Ops:
  0.6 4.8 %shard_map.112 = (bf16[16,128,128]{2,1,0:T(8,128)(2,1)}, s32[1,2048]{1,0:T(1,128)S(1)}) custom-call(s32[1]{0:T(128)} %bitcast.1.head_ref, s32[1,2048]{1,0:T(1,128)} %bitcast.5, bf16[128,2048]{1,0:T(8,128)(2,1)} %query_hbm.3, bf16[128,2048]{1,0:T(8,128)(2,1)} %key_hbm.3), custom_call_target="tpu_custom_call" | custom-call | tf_op jit(solution)/shard_map/pallas_call | solution.py:252
  5.4 7.4 %all-to-all-start.1 = ((bf16[16,128,128]{2,1,0:T(8,128)(2,1)}), bf16[16,128,128]{2,1,0:T(8,128)(2,1)S(1)}, u32[]{:S(2)}, u32[]{:S(2)}) async-start(bf16[16,128,128]{2,1,0:T(8,128)(2,1)} %get-tuple-element.13), calls=%async_computation.1 | async-start | bytes 1048576 | tf_op jit(solution)/shard_map/all_to_all | solution.py:258
  12.8 1.6 %collective-permute-start = (bf16[128,2048]{1,0:T(8,128)(2,1)}, bf16[128,2048]{1,0:T(8,128)(2,1)S(1)}, u32[]{:S(2)}, u32[]{:S(2)}) collective-permute-start(bf16[128,2048]{1,0:T(8,128)(2,1)} %grad_hbm.1), channel_id=1, source_target_pairs={{0,1},{1,0},{2,3},{3,2},{4,5},{5,4},{6,7},{7,6},{8,9},{9,8},{10,11... | collective-permute-start | bytes 1572872 | tf_op jit(solution)/shard_map/ppermute | solution.py:250
  14.4 6.5 %shard_map.113.acc_ref = f32[128,2048]{1,0:T(8,128)S(1)} custom-call(s32[1]{0:T(128)} %bitcast.3.half_ref, bf16[128,2048]{1,0:T(8,128)(2,1)} %grad_hbm.1, bf16[2048,4096]{1,0:T(8,128)(2,1)} %weight_hbm.3), custom_call_target="tpu_custom_call" | custom-call | tf_op jit(solution)/shard_map/pallas_call | solution.py:265
  20.9 6.4 %collective-permute-done.grad_ref = bf16[128,2048]{1,0:T(8,128)(2,1)S(1)} collective-permute-done((bf16[128,2048]{1,0:T(8,128)(2,1)}, bf16[128,2048]{1,0:T(8,128)(2,1)S(1)}, u32[]{:S(2)}, u32[]{:S(2)}) %collective-permute-start) | collective-permute-done | bytes 524320 | tf_op jit(solution)/shard_map/ppermute | solution.py:250
  27.3 6.7 %shard_map.114 = (bf16[16,128,128]{2,1,0:T(8,128)(2,1)}, bf16[128,2048]{1,0:T(8,128)(2,1)S(1)}) custom-call(s32[1]{0:T(128)} %bitcast.half_ref, s32[1,2048]{1,0:T(1,128)S(1)} %get-tuple-element.11.rank_ref, bf16[128,2048]{1,0:T(8,128)(2,1)S(1)} %collective-permute-done.grad_ref, f32[128,2048]{1,0:T(8,128)S(1)} %shard_map.113.acc_ref, ...), custom_call_target="tpu_custom_call" | custom-call | tf_op jit(solution)/shard_map/pallas_call | solution.py:278
  34.0 0.0 all-to-all-done.1.gate_ref
  34.0 5.7 %all-to-all-start = ((bf16[16,128,128]{2,1,0:T(8,128)(2,1)}), bf16[16,128,128]{2,1,0:T(8,128)(2,1)S(1)}, u32[]{:S(2)}, u32[]{:S(2)}) async-start(bf16[16,128,128]{2,1,0:T(8,128)(2,1)} %get-tuple-element.12), calls=%async_computation | async-start | bytes 1048576 | tf_op jit(solution)/shard_map/all_to_all | solution.py:291
  39.7 1.3 %dynamic-slice_convert_fusion.filt_ref = f32[8,1152]{1,0:T(8,128)} fusion(bf16[128,2048]{1,0:T(8,128)(2,1)} %param.14, s32[]{:T(128)S(6)} %select_n.16), kind=kLoop, calls=%fused_computation | loop fusion | flops 9216 | bytes 55300 | tf_op jit(solution)/shard_map/convert_element_type | solution.py:293
  41.1 1.1 %shard_map.115 = (bf16[8,128,256]{2,1,0:T(8,128)(2,1)S(1)}, f32[8,1280]{1,0:T(8,128)S(1)}, f32[256,128]{1,0:T(8,128)S(1)}, f32[1,2048]{1,0:T(1,128)S(1)}) custom-call(s32[4]{0:T(128)} %docs_ref.1, f32[8,1152]{1,0:T(8,128)} %dynamic-slice_convert_fusion.filt_ref, bf16[16,128,128]{2,1,0:T(8,128)(2,1)S(1)} %all-to-all-done.1.gate_ref, f32[1,2048]{1,0:T(1,128)} %bitcast.6), custom_call_target="tpu_custom_call" | custom-call | tf_op jit(solution)/shard_map/pallas_call | solution.py:294
  42.1 11.8 %all-to-all-done.grad_ref = bf16[16,128,128]{2,1,0:T(8,128)(2,1)S(1)} async-done(((bf16[16,128,128]{2,1,0:T(8,128)(2,1)}), bf16[16,128,128]{2,1,0:T(8,128)(2,1)S(1)}, u32[]{:S(2)}, u32[]{:S(2)}) %all-to-all-start) | async-done | bytes 524320 | tf_op jit(solution)/shard_map/all_to_all | solution.py:291
  54.0 2.8 %shard_map.116 = bf16[16,144,128]{2,1,0:T(8,128)(2,1)S(1)} custom-call(bf16[16,128,128]{2,1,0:T(8,128)(2,1)S(1)} %all-to-all-done.grad_ref, bf16[8,128,256]{2,1,0:T(8,128)(2,1)S(1)} %get-tuple-element.14.gate_t_ref, f32[8,1280]{1,0:T(8,128)S(1)} %get-tuple-element.15.rows_ref, f32[256,128]{1,0:T(8,128)S(1)} %get-tuple-element.16.doc_ref), custom_call_target="tpu_custom_call" | custom-call | tf_op jit(solution)/shard_map/pallas_call | solution.py:305
  56.7 21.2 %all_to_all.15.back_ref = bf16[16,144,128]{2,1,0:T(8,128)(2,1)S(1)} all-to-all(bf16[16,144,128]{2,1,0:T(8,128)(2,1)S(1)} %shard_map.116), channel_id=1, replica_groups=mesh['ctx'=16,'head'=2] {'ctx'}, dimensions={0} | all-to-all | bytes 1179648 | tf_op jit(solution)/shard_map/all_to_all | solution.py:314
  77.9 3.9 %shard_map.117 = (bf16[128,2048]{1,0:T(8,128)(2,1)}, bf16[128,2048]{1,0:T(8,128)(2,1)}, f32[128,128]{1,0:T(8,128)}) custom-call(bf16[16,144,128]{2,1,0:T(8,128)(2,1)S(1)} %all_to_all.15.back_ref, s32[1,2048]{1,0:T(1,128)S(1)} %get-tuple-element.11.rank_ref, bf16[128,2048]{1,0:T(8,128)(2,1)S(1)} %get-tuple-element.17.conv_ref, ...), custom_call_target="tpu_custom_call" | custom-call | tf_op jit(solution)/shard_map/pallas_call | solution.py:316
Async XLA Ops:
  5.4 28.5 %all-to-all-start.1 = ((bf16[16,128,128]{2,1,0:T(8,128)(2,1)}), bf16[16,128,128]{2,1,0:T(8,128)(2,1)S(1)}, u32[]{:S(2)}, u32[]{:S(2)}) async-start(bf16[16,128,128]{2,1,0:T(8,128)(2,1)} %get-tuple-element.13), calls=%async_computation.1 | async-start | bytes 1048576 | tf_op jit(solution)/shard_map/all_to_all | solution.py:258
  12.8 14.4 %collective-permute-start = (bf16[128,2048]{1,0:T(8,128)(2,1)}, bf16[128,2048]{1,0:T(8,128)(2,1)S(1)}, u32[]{:S(2)}, u32[]{:S(2)}) collective-permute-start(bf16[128,2048]{1,0:T(8,128)(2,1)} %grad_hbm.1), channel_id=1, source_target_pairs={{0,1},{1,0},{2,3},{3,2},{4,5},{5,4},{6,7},{7,6},{8,9},{9,8},{10,11... | collective-permute-start | bytes 1572872 | tf_op jit(solution)/shard_map/ppermute | solution.py:250
  34.0 20.0 %all-to-all-start = ((bf16[16,128,128]{2,1,0:T(8,128)(2,1)}), bf16[16,128,128]{2,1,0:T(8,128)(2,1)S(1)}, u32[]{:S(2)}, u32[]{:S(2)}) async-start(bf16[16,128,128]{2,1,0:T(8,128)(2,1)} %get-tuple-element.12), calls=%async_computation | async-start | bytes 1048576 | tf_op jit(solution)/shard_map/all_to_all | solution.py:291

commit v3 on v2

--- a/solution.py
+++ b/solution.py
@@ -13,6 +13,7 @@
 NT = (((1,), (1,)), ((), ()))
 NN = (((1,), (0,)), ((), ()))
 LANES = 128
+CHUNKS = 2
 EXTRA = 16
 VMEM = pl.BlockSpec(memory_space=pltpu.VMEM)
 SMEM = pl.BlockSpec(memory_space=pltpu.SMEM)
@@ -43,46 +44,69 @@
     column_ref[...] = wide.T.astype(I32)
 
 
-def permute(by_token, column_ref, out_ref):
+def permute(by_token, column_ref, first, count, store):
     channels = column_ref.shape[0]
-    rows = out_ref.shape[1]
-    width = min(2 * LANES, channels)
+    width = min(2 * LANES, count)
     lane = lax.broadcasted_iota(I32, (channels, LANES), 1)
-    for p in range(0, channels, width):
+    for p in range(first, first + count, width):
         picks = [
             jnp.where(column_ref[...] == lane + (p + q), 1.0, 0.0).astype(BF16)
             for q in range(0, width, LANES)
         ]
-        moved = dot(by_token, jnp.concatenate(picks, axis=1), NN).T.astype(BF16)
-        out_ref[p // rows : (p + width) // rows] = moved.reshape(width // rows, rows, -1)
+        store(p, dot(by_token, jnp.concatenate(picks, axis=1), NN).T.astype(BF16))
+
+
+def store_chunk(out_ref, start):
+    rows = out_ref.shape[1]
+
+    def store(p, block):
+        blocks = block.shape[0] // rows
+        at = (p - start) // rows
+        out_ref[at : at + blocks] = block.reshape(blocks, rows, -1)
+
+    return store
 
 
 def gate_kernel(
-    head_ref, group_ref, query_hbm, key_hbm, out_ref, rank_ref, query_ref, key_ref, column_ref, sem, *, groups, per_group
+    group_hbm, query_hbm, key_hbm, out_ref, rank_ref, group_ref, query_ref, key_ref, column_ref, sem, *, groups, per_group
 ):
     loads = [
-        pltpu.make_async_copy(query_hbm, query_ref, sem.at[0]),
-        pltpu.make_async_copy(key_hbm, key_ref, sem.at[1]),
+        pltpu.make_async_copy(group_hbm, group_ref, sem.at[0]),
+        pltpu.make_async_copy(query_hbm, query_ref, sem.at[1]),
+        pltpu.make_async_copy(key_hbm, key_ref, sem.at[2]),
     ]
     for load in loads:
         load.start()
     channels = group_ref.shape[1]
-    local = group_ref[...] - head_ref[0] * groups
+    spans, sub, tokens = out_ref.shape
+    near = (sub // per_group // CHUNKS).bit_length() - 1
+    parts = CHUNKS.bit_length() - 1
     upper = lax.broadcasted_iota(I32, (LANES, LANES), 0) < lax.broadcasted_iota(I32, (LANES, LANES), 1)
     upper = jnp.where(upper, 1.0, 0.0).astype(BF16)
     base = jnp.zeros((groups, 1), F32)
+    loads[0].wait()
+    local = group_ref[...] & (groups - 1)
+    order = (local & ((1 << near) - 1)) | ((local >> (near + parts)) << near)
+    order = order | (((local >> near) & (CHUNKS - 1)) << (groups.bit_length() - 1 - parts))
     for b in range(channels // LANES):
-        here = local[:, b * LANES : (b + 1) * LANES]
-        member = jnp.where(lax.broadcasted_iota(I32, (groups, LANES), 0) == here, 1.0, 0.0)
+        cols = slice(b * LANES, (b + 1) * LANES)
+        member = jnp.where(lax.broadcasted_iota(I32, (groups, LANES), 0) == order[:, cols], 1.0, 0.0)
         before = dot(member.astype(BF16), upper, NN) + base
         place = jnp.sum(member * before, axis=0, keepdims=True)
-        rank_ref[:, b * LANES : (b + 1) * LANES] = here * per_group + place.astype(I32)
+        rank_ref[:, cols] = order[:, cols] * per_group + place.astype(I32)
         base = base + jnp.sum(member, axis=1, keepdims=True)
     rank_column(rank_ref[...], column_ref)
-    for load in loads:
+    for load in loads[1:]:
         load.wait()
     gated = (query_ref[...].astype(F32) * key_ref[...].astype(F32)).astype(BF16)
-    permute(gated, column_ref, out_ref)
+    part = sub // CHUNKS
+
+    def store(p, block):
+        blocks = block.shape[0] // part
+        chunk, at = divmod(p // part, spans)
+        out_ref[at : at + blocks, chunk * part : (chunk + 1) * part, :] = block.reshape(blocks, part, tokens)
+
+    permute(gated, column_ref, 0, channels, store)
 
 
 def stream_weights(half, weight_hbm, weight_ref, sem):
@@ -110,14 +134,11 @@
         out_ref[...] = part if fresh and j == 0 else out_ref[...] + part
 
 
-def partial_kernel(half_ref, grad_hbm, weight_hbm, *refs):
-    *acc, out_ref, grad_ref, weight_ref, sem, grad_sem = refs
-    load = pltpu.make_async_copy(grad_hbm, grad_ref, grad_sem)
-    load.start()
+def partial_kernel(half_ref, grad_ref, weight_hbm, *refs):
+    *acc, out_ref, weight_ref, sem = refs
     copies, width = stream_weights(half_ref[0], weight_hbm, weight_ref, sem)
     if acc:
         out_ref[...] = acc[0][...]
-    load.wait()
     product(copies, width, grad_ref, weight_ref, out_ref, not acc)
 
 
@@ -132,7 +153,13 @@
     product(copies, width, grad_ref, weight_ref, total_ref, False)
     load.wait()
     conv_ref[...] = (total_ref[...] * value_ref[...].astype(F32)).astype(BF16)
-    permute(conv_ref[...], column_ref, out_ref)
+    permute(conv_ref[...], column_ref, 0, out_ref.shape[0] * out_ref.shape[1], store_chunk(out_ref, 0))
+
+
+def more_kernel(rank_ref, conv_ref, out_ref, column_ref, *, chunk):
+    rank_column(rank_ref[...], column_ref)
+    count = out_ref.shape[0] * out_ref.shape[1]
+    permute(conv_ref[...], column_ref, chunk * count, count, store_chunk(out_ref, chunk * count))
 
 
 def prepare_kernel(docs_ref, filt_ref, gate_ref, skip_ref, gate_t_ref, rows_ref, doc_ref, skip_out_ref, *, per_group):
@@ -155,9 +182,12 @@
     skip_out_ref[...] = skip_ref[...]
 
 
-def conv_kernel(grad_ref, gate_t_ref, rows_ref, doc_ref, out_ref, moved_ref, sums_ref, *, per_group):
+def conv_kernel(grad_ref, gate_t_ref, rows_ref, doc_ref, *refs, per_group, chunk):
+    *earlier, out_ref, sums_ref, moved_ref = refs
     spans, sub, tokens = grad_ref.shape
-    groups, padded = rows_ref.shape
+    groups = sub // per_group
+    first = chunk * groups
+    padded = rows_ref.shape[1]
     lags = padded - tokens
     reach = lags // tokens
     for k in range(reach):
@@ -170,17 +200,19 @@
             moved_ref[g, :keep, cols] = grad * same
             if k:
                 moved_ref[g, keep:, cols] = jnp.zeros((cut, tokens), BF16)
-    sums_ref[...] = jnp.zeros(sums_ref.shape, F32)
+    sums_ref[...] = earlier[0][...] if earlier else jnp.zeros(sums_ref.shape, F32)
     for g in range(groups):
         moved = moved_ref[g]
-        wide = jnp.broadcast_to(rows_ref[g : g + 1, :], (tokens, padded))
+        wide = jnp.broadcast_to(rows_ref[first + g : first + g + 1, :], (tokens, padded))
         toeplitz = pltpu.roll(wide, 0, 1, stride=1, stride_axis=0)[:, :lags].astype(BF16)
         back = dot(moved, toeplitz, NT)
         out_ref[:, g * per_group : (g + 1) * per_group, :] = back.astype(BF16).reshape(spans, per_group, tokens)
-        corr = dot(gate_t_ref[g], moved, NN)
+        corr = dot(gate_t_ref[first + g], moved, NN)
         wide = jnp.concatenate([corr, jnp.zeros((tokens, tokens), F32)], axis=1)
         skewed = pltpu.roll(wide, lags + 1, 1, stride=1, stride_axis=0)
-        sums_ref[g : g + 1, :] = jnp.sum(skewed[:, :lags], axis=0, keepdims=True)
+        sums_ref[first + g : first + g + 1, :] = jnp.sum(skewed[:, :lags], axis=0, keepdims=True)
+    if out_ref.shape[1] == sub:
+        return
     for k in range(spans):
         if k < reach:
             exact = sums_ref[:, k * tokens : (k + 1) * tokens]
@@ -191,12 +223,27 @@
         out_ref[k, sub:, :] = both
 
 
+def restore_kernel(back_ref, rank_ref, conv_ref, skip_ref, *refs, chunk):
+    *acc, out_ref, sorted_ref = refs
+    spans, rows, tokens = back_ref.shape
+    count = spans * rows
+    sorted_ref[...] = back_ref[...].reshape(count, tokens).T
+    channels = rank_ref.shape[1]
+    width = min(2 * LANES, channels)
+    for j in range(0, channels, width):
+        cols = slice(j, j + width)
+        picks = lax.broadcasted_iota(I32, (count, width), 0) == rank_ref[:, cols] - chunk * count
+        more = dot(sorted_ref[...], jnp.where(picks, 1.0, 0.0).astype(BF16), NN)
+        out_ref[:, cols] = more + (acc[0][:, cols] if acc else conv_ref[:, cols].astype(F32) * skip_ref[:, cols])
+
+
 def gates_kernel(
-    back_ref, rank_ref, conv_ref, skip_ref, query_hbm, key_hbm, grad_query_hbm, grad_key_hbm, filt_hbm,
+    back_ref, rank_ref, acc_ref, query_hbm, key_hbm, grad_query_hbm, grad_key_hbm, filt_hbm,
     query_ref, key_ref, grad_query_ref, grad_key_ref, filt_ref, sorted_ref, load_sem, store_sem, filt_sem, *, sub_groups
 ):
     spans, rows, tokens = back_ref.shape
     sub = rows - EXTRA
+    count = spans * sub
     channels = rank_ref.shape[1]
     loads = [
         pltpu.make_async_copy(query_hbm, query_ref, load_sem.at[0]),
@@ -204,21 +251,20 @@
     ]
     for load in loads:
         load.start()
+    sorted_ref[...] = back_ref[:, :sub, :].reshape(count, tokens).T
     for d in range(spans):
         tail = back_ref[d, sub:, :].astype(F32)
         both = tail[: EXTRA // 2] + tail[EXTRA // 2 :]
         filt_ref[d * sub_groups : (d + 1) * sub_groups, :] = both[:sub_groups]
     stores = [pltpu.make_async_copy(filt_ref, filt_hbm, filt_sem)]
     stores[0].start()
-    sorted_ref[...] = back_ref[:, :sub, :].reshape(spans * sub, tokens).T
     for load in loads:
         load.wait()
     width = channels // store_sem.shape[1]
     for j in range(store_sem.shape[1]):
         cols = slice(j * width, (j + 1) * width)
-        place = lax.broadcasted_iota(I32, (channels, width), 0)
-        picks = jnp.where(place == rank_ref[:, cols], 1.0, 0.0).astype(BF16)
-        gated_grad = dot(sorted_ref[...], picks, NN) + conv_ref[:, cols].astype(F32) * skip_ref[:, cols]
+        picks = lax.broadcasted_iota(I32, (count, width), 0) == rank_ref[:, cols] - (CHUNKS - 1) * count
+        gated_grad = acc_ref[:, cols] + dot(sorted_ref[...], jnp.where(picks, 1.0, 0.0).astype(BF16), NN)
         grad_query_ref[:, cols] = (gated_grad * key_ref[:, cols].astype(F32)).astype(BF16)
         grad_key_ref[:, cols] = (gated_grad * query_ref[:, cols].astype(F32)).astype(BF16)
         for which, (source, target) in enumerate(((grad_query_ref, grad_query_hbm), (grad_key_ref, grad_key_hbm))):
@@ -241,6 +287,7 @@
     head = lax.axis_index("head")
     sub = channels // spans
     sub_groups = sub // per_group
+    part = sub // CHUNKS
     lags = (spans // 2 + 1) * tokens
     feats = grad_out.shape[1]
     dma = pltpu.SemaphoreType.DMA
@@ -252,12 +299,14 @@
     gate_sorted, rank = call(
         functools.partial(gate_kernel, groups=groups, per_group=per_group),
         (pltpu.VMEM((spans, sub, tokens), BF16), pltpu.VMEM((1, channels), I32)),
-        [SMEM, VMEM, ANY, ANY],
-        [wide, wide, column, dma((2,))],
-    )(head.reshape(1), group_of.reshape(1, channels), query_proj, key_proj)
-    gate_moved = lax.all_to_all(gate_sorted, "ctx", 0, 0)
+        [ANY, ANY, ANY],
+        [pltpu.VMEM((1, channels), I32), wide, wide, column, dma((3,))],
+    )(group_of.reshape(1, channels), query_proj, key_proj)
+    rank = on_chip(rank)
+    gate_moved = lax.all_to_all(on_chip(gate_sorted), "ctx", 0, 0)
 
     parts = min(8, feats // LANES)
+    streams = [pltpu.VMEM((channels, feats), BF16)]
     acc = None
     for r, grad in enumerate([grad_out] + arrived):
         source = ((head + heads - r) % heads).reshape(1)
@@ -265,30 +314,26 @@
             acc = call(
                 partial_kernel,
                 pltpu.VMEM((tokens, channels), F32),
-                [SMEM, ANY, ANY] + ([] if acc is None else [VMEM]),
-                [
-                    pltpu.VMEM((tokens, feats), BF16),
-                    pltpu.VMEM((channels, feats), BF16),
-                    dma((parts,)),
-                    dma,
-                ],
-            )(source, grad, out_proj, *([] if acc is None else [acc]))
+                [SMEM, VMEM, ANY] + ([] if acc is None else [VMEM]),
+                streams + [dma((parts,))],
+            )(source, on_chip(grad), out_proj, *([] if acc is None else [acc]))
             acc = on_chip(acc)
         else:
             conv_sorted, conv_grad = call(
                 last_kernel,
-                (pltpu.VMEM((spans, sub, tokens), BF16), pltpu.VMEM((tokens, channels), BF16)),
+                (pltpu.VMEM((spans, part, tokens), BF16), pltpu.VMEM((tokens, channels), BF16)),
                 [SMEM, VMEM, VMEM, VMEM, ANY, ANY],
-                [
-                    pltpu.VMEM((tokens, channels), F32),
-                    pltpu.VMEM((channels, feats), BF16),
-                    wide,
-                    column,
-                    dma((parts,)),
-                    dma,
-                ],
-            )(source, on_chip(rank), on_chip(grad), acc, out_proj, value_proj)
-    conv_moved = lax.all_to_all(on_chip(conv_sorted), "ctx", 0, 0)
+                [pltpu.VMEM((tokens, channels), F32)] + streams + [wide, column, dma((parts,)), dma],
+            )(source, rank, on_chip(grad), acc, out_proj, value_proj)
+            conv_grad = on_chip(conv_grad)
+
+    conv_moved = []
+    for q in range(CHUNKS):
+        if q:
+            conv_sorted = call(
+                functools.partial(more_kernel, chunk=q), pltpu.VMEM((spans, part, tokens), BF16), [VMEM, VMEM], [column]
+            )(rank, conv_grad)
+        conv_moved.append(lax.all_to_all(on_chip(conv_sorted), "ctx", 0, 0))
 
     filt_sub = lax.dynamic_slice(filters, (position * sub_groups, 0), (sub_groups, lags)).astype(F32)
     gate_t, rows, doc, skip = call(
@@ -301,18 +346,33 @@
         ),
         [SMEM, VMEM, VMEM, VMEM],
     )(doc_lengths, filt_sub, on_chip(gate_moved), skip_gain.reshape(1, channels))
-
-    back = call(
-        functools.partial(conv_kernel, per_group=per_group),
-        pltpu.VMEM((spans, sub + EXTRA, tokens), BF16),
-        [VMEM] * 4,
-        [
-            pltpu.VMEM((sub_groups, spans * per_group, lags), BF16),
-            pltpu.VMEM((EXTRA // 2, lags), F32),
-        ],
-    )(on_chip(conv_moved), on_chip(gate_t), on_chip(rows), on_chip(doc))
-    back_moved = lax.all_to_all(on_chip(back), "ctx", 0, 0)
-
+    gate_t, rows, doc, skip = on_chip(gate_t), on_chip(rows), on_chip(doc), on_chip(skip)
+
+    back_moved = []
+    sums = []
+    for q in range(CHUNKS):
+        final = q == CHUNKS - 1
+        back, total = call(
+            functools.partial(conv_kernel, per_group=per_group, chunk=q),
+            (pltpu.VMEM((spans, part + (EXTRA if final else 0), tokens), BF16), pltpu.VMEM((EXTRA // 2, lags), F32)),
+            [VMEM] * (4 + len(sums)),
+            [pltpu.VMEM((part // per_group, spans * per_group, lags), BF16)],
+        )(on_chip(conv_moved[q]), gate_t, rows, doc, *sums)
+        sums = [on_chip(total)]
+        back_moved.append(lax.all_to_all(on_chip(back), "ctx", 0, 0))
+
+    restored = []
+    for q in range(CHUNKS - 1):
+        restored = [
+            on_chip(
+                call(
+                    functools.partial(restore_kernel, chunk=q),
+                    pltpu.VMEM((tokens, channels), F32),
+                    [VMEM] * (4 + len(restored)),
+                    [pltpu.VMEM((tokens, spans * part), BF16)],
+                )(on_chip(back_moved[q]), rank, conv_grad, skip, *restored)
+            )
+        ]
     return call(
         functools.partial(gates_kernel, sub_groups=sub_groups),
         (
@@ -320,10 +380,11 @@
             jax.ShapeDtypeStruct((tokens, channels), BF16),
             jax.ShapeDtypeStruct((groups, tokens), F32),
         ),
-        [VMEM, VMEM, VMEM, VMEM, ANY, ANY],
-        [wide, wide, wide, wide, pltpu.VMEM((groups, tokens), F32), wide, dma((2,)), dma((2, 8)), dma],
+        [VMEM, VMEM, VMEM, ANY, ANY],
+        [wide, wide, wide, wide, pltpu.VMEM((groups, tokens), F32)]
+        + [pltpu.VMEM((tokens, spans * part), BF16), dma((2,)), dma((2, min(8, channels // LANES))), dma],
         (ANY, ANY, ANY),
-    )(on_chip(back_moved), on_chip(rank), on_chip(conv_grad), on_chip(skip), query_proj, key_proj)
+    )(on_chip(back_moved[-1]), rank, *restored, query_proj, key_proj)
 
 
 def solution(mesh):

time: 82.4 us -> 93.8 us (1.14)
  blocking collectives: 21.2 us -> 0 us
  waiting for transfers between devices: 18.2 us -> 38.6 us
  starting transfers between devices: 14.7 us -> 25.5 us
  local copies, waits for them, and re-layouts: 0 us -> 1.07 us
    all_to_all x1 -> x0, blocking collectives: 21.2 us -> none  [per_device(): back_moved = lax.all_to_all(on_chip(back), 'ctx', 0, 0)]
    all_to_all x2 -> x5, waiting for transfers between devices: 11.8 us -> 31.1 us  [the longest x2 17.4 us: per_device(): back_moved.append(lax.all_to_all(on_chip(back), 'ctx', 0, 0))]
    all_to_all x2 -> x5, starting transfers between devices: 13.1 us -> 23.9 us  [the longest x2 9.26 us: per_device(): conv_moved.append(lax.all_to_all(on_chip(conv_sorted), 'ctx', 0, 0))]
    pallas_call x3 -> x6, Pallas kernels: 15.9 us -> 17.6 us  [the longest x1 5.97 us: per_device(): call(last_kernel, (pltpu.VMEM((spans, part, tokens), BF16), pltpu.VMEM((t...]
    unnamed x0 -> x2, local copies, waits for them, and re-layouts: none -> 1.07 us
    ppermute x1, waiting for transfers between devices: 6.37 us -> 7.43 us  [per_device(): lax.ppermute(grad_out, 'head', [(i, (i + r) % heads) for i in range(heads)])]
    pallas_call x1, Pallas kernels: 4.77 us -> 3.8 us  [per_device(): call(functools.partial(gate_kernel, groups=groups, per_group=per_group),...]
  transfers between devices with their start and end apart: 3 -> 6, of which waited for: 2 -> 5; matrix products, arithmetic and copies ran while one was open for 2% -> 1% of each run, Pallas kernels for 17% -> 20%
where the time goes in v3:
time: 93.8 us; the launch traced here: 93 us
  waiting for transfers between devices  38.6 us (41%)
  Pallas kernels  25.6 us (27%)
  starting transfers between devices  25.5 us (27%)
  other arithmetic  1.35 us (1%)
  local copies, waits for them, and re-layouts  1.07 us (1%)
    all_to_all x2, waiting for transfers between devices, per_device(): back_moved.append(lax.all_to_all(on_chip(back), 'ctx', 0, 0))  17.4 us
    all_to_all x2, waiting for transfers between devices, per_device(): conv_moved.append(lax.all_to_all(on_chip(conv_sorted), 'ctx', 0, 0))  13.8 us
    all_to_all x2, starting transfers between devices, per_device(): conv_moved.append(lax.all_to_all(on_chip(conv_sorted), 'ctx', 0, 0))  9.26 us
    ppermute x1, waiting for transfers between devices, per_device(): lax.ppermute(grad_out, 'head', [(i, (i + r) % heads) for i in range(heads)])  7.43 us
    all_to_all x1, starting transfers between devices, per_device(): gate_moved = lax.all_to_all(on_chip(gate_sorted), 'ctx', 0, 0)  7.4 us
    all_to_all x2, starting transfers between devices, per_device(): back_moved.append(lax.all_to_all(on_chip(back), 'ctx', 0, 0))  7.26 us
    pallas_call x1, Pallas kernels, per_device(): call(last_kernel, (pltpu.VMEM((spans, part, tokens), BF16), pltpu.VMEM((t...  5.97 us
    pallas_call x2, Pallas kernels, per_device(): call(functools.partial(conv_kernel, per_group=per_group, chunk=q), (pltpu...  4.41 us
  transfers between devices with their start and end apart: 6, of which 5 were waited for; matrix products, arithmetic and copies ran while one was open for 1% of the time, Pallas kernels for 20%

profile of v3, /device:TPU:0, one launch (start us, length us, event | category | flops | bytes accessed | tf_op | source)
XLA Modules:
  0.0 93.0 jit_solution(7499499193992763367)
XLA Ops:
  0.6 3.8 %shard_map.112 = (bf16[16,128,128]{2,1,0:T(8,128)(2,1)}, s32[1,2048]{1,0:T(1,128)S(1)}) custom-call(s32[1,2048]{1,0:T(1,128)} %bitcast.4, bf16[128,2048]{1,0:T(8,128)(2,1)} %query_hbm.3, bf16[128,2048]{1,0:T(8,128)(2,1)} %key_hbm.3), custom_call_target="tpu_custom_call" | custom-call | tf_op jit(solution)/shard_map/pallas_call | solution.py:299
  4.4 7.4 %all-to-all-start.1 = ((bf16[16,128,128]{2,1,0:T(8,128)(2,1)}), bf16[16,128,128]{2,1,0:T(8,128)(2,1)S(1)}, u32[]{:S(2)}, u32[]{:S(2)}) async-start(bf16[16,128,128]{2,1,0:T(8,128)(2,1)} %get-tuple-element.16), calls=%async_computation.1 | async-start | bytes 1048576 | tf_op jit(solution)/shard_map/all_to_all | solution.py:306
  11.8 1.6 %collective-permute-start = (bf16[128,2048]{1,0:T(8,128)(2,1)}, bf16[128,2048]{1,0:T(8,128)(2,1)S(1)}, u32[]{:S(2)}, u32[]{:S(2)}) collective-permute-start(bf16[128,2048]{1,0:T(8,128)(2,1)} %grad_ref.1), channel_id=1, source_target_pairs={{0,1},{1,0},{2,3},{3,2},{4,5},{5,4},{6,7},{7,6},{8,9},{9,8},{10,11... | collective-permute-start | bytes 1572872 | tf_op jit(solution)/shard_map/ppermute | solution.py:297
  13.4 0.0 copy-start
  13.4 1.1 %copy-done = bf16[128,2048]{1,0:T(8,128)(2,1)S(1)} copy-done((bf16[128,2048]{1,0:T(8,128)(2,1)S(1)}, bf16[128,2048]{1,0:T(8,128)(2,1)}, u32[]{:S(2)}) %copy-start) | copy-done | bytes 524312
  14.5 4.3 %shard_map.113.acc_ref = f32[128,2048]{1,0:T(8,128)S(1)} custom-call(s32[1]{0:T(128)} %bitcast.2.half_ref, bf16[128,2048]{1,0:T(8,128)(2,1)S(1)} %copy-done, bf16[2048,4096]{1,0:T(8,128)(2,1)} %weight_hbm.3), custom_call_target="tpu_custom_call" | custom-call | tf_op jit(solution)/shard_map/pallas_call | solution.py:314
  18.9 7.4 %collective-permute-done.grad_ref = bf16[128,2048]{1,0:T(8,128)(2,1)S(1)} collective-permute-done((bf16[128,2048]{1,0:T(8,128)(2,1)}, bf16[128,2048]{1,0:T(8,128)(2,1)S(1)}, u32[]{:S(2)}, u32[]{:S(2)}) %collective-permute-start) | collective-permute-done | bytes 524320 | tf_op jit(solution)/shard_map/ppermute | solution.py:297
  26.3 6.0 %shard_map.114 = (bf16[16,64,128]{2,1,0:T(8,128)(2,1)}, bf16[128,2048]{1,0:T(8,128)(2,1)S(1)}) custom-call(s32[1]{0:T(128)} %bitcast.1.half_ref, s32[1,2048]{1,0:T(1,128)S(1)} %get-tuple-element.14.rank_ref, bf16[128,2048]{1,0:T(8,128)(2,1)S(1)} %collective-permute-done.grad_ref, f32[128,2048]{1,0:T(8,128)S(1)} %shard_map.113.acc_ref, ...), custom_call_target="tpu_custom_call" | custom-call | tf_op jit(solution)/shard_map/pallas_call | solution.py:322
  32.3 0.0 all-to-all-done.1.gate_ref
  32.3 5.7 %all-to-all-start.2 = ((bf16[16,64,128]{2,1,0:T(8,128)(2,1)}), bf16[16,64,128]{2,1,0:T(8,128)(2,1)S(1)}, u32[]{:S(2)}, u32[]{:S(2)}) async-start(bf16[16,64,128]{2,1,0:T(8,128)(2,1)} %get-tuple-element.20), calls=%async_computation.2 | async-start | bytes 524288 | tf_op jit(solution)/shard_map/all_to_all | solution.py:336
  38.0 1.6 %shard_map.115 = bf16[16,64,128]{2,1,0:T(8,128)(2,1)} custom-call(s32[1,2048]{1,0:T(1,128)S(1)} %get-tuple-element.14.rank_ref, bf16[128,2048]{1,0:T(8,128)(2,1)S(1)} %get-tuple-element.15.conv_ref), custom_call_target="tpu_custom_call" | custom-call | tf_op jit(solution)/shard_map/pallas_call | solution.py:333
  39.7 8.4 %all-to-all-done.2.grad_ref = bf16[16,64,128]{2,1,0:T(8,128)(2,1)S(1)} async-done(((bf16[16,64,128]{2,1,0:T(8,128)(2,1)}), bf16[16,64,128]{2,1,0:T(8,128)(2,1)S(1)}, u32[]{:S(2)}, u32[]{:S(2)}) %all-to-all-start.2) | async-done | bytes 262176 | tf_op jit(solution)/shard_map/all_to_all | solution.py:336
  48.0 3.5 %all-to-all-start = ((bf16[16,64,128]{2,1,0:T(8,128)(2,1)}), bf16[16,64,128]{2,1,0:T(8,128)(2,1)S(1)}, u32[]{:S(2)}, u32[]{:S(2)}) async-start(bf16[16,64,128]{2,1,0:T(8,128)(2,1)} %shard_map.115), calls=%async_computation | async-start | bytes 524288 | tf_op jit(solution)/shard_map/all_to_all | solution.py:336
  51.6 1.3 %dynamic-slice_convert_fusion.filt_ref = f32[8,1152]{1,0:T(8,128)} fusion(bf16[128,2048]{1,0:T(8,128)(2,1)} %param.14, s32[]{:T(128)S(6)} %select_n.16), kind=kLoop, calls=%fused_computation | loop fusion | flops 9216 | bytes 55300 | tf_op jit(solution)/shard_map/convert_element_type | solution.py:338
  52.9 1.1 %shard_map.116 = (bf16[8,128,256]{2,1,0:T(8,128)(2,1)S(1)}, f32[8,1280]{1,0:T(8,128)S(1)}, f32[256,128]{1,0:T(8,128)S(1)}, f32[1,2048]{1,0:T(1,128)S(1)}) custom-call(s32[4]{0:T(128)} %docs_ref.1, f32[8,1152]{1,0:T(8,128)} %dynamic-slice_convert_fusion.filt_ref, bf16[16,128,128]{2,1,0:T(8,128)(2,1)S(1)} %all-to-all-done.1.gate_ref, f32[1,2048]{1,0:T(1,128)} %bitcast.5), custom_call_target="tpu_custom_call" | custom-call | tf_op jit(solution)/shard_map/pallas_call | solution.py:339
  54.0 2.1 %shard_map.117 = (bf16[16,64,128]{2,1,0:T(8,128)(2,1)}, f32[8,1152]{1,0:T(8,128)S(1)}) custom-call(bf16[16,64,128]{2,1,0:T(8,128)(2,1)S(1)} %all-to-all-done.2.grad_ref, bf16[8,128,256]{2,1,0:T(8,128)(2,1)S(1)} %get-tuple-element.17.gate_t_ref, f32[8,1280]{1,0:T(8,128)S(1)} %get-tuple-element.18.rows_ref, f32[256,128]{1,0:T(8,128)S(1)} %get-tuple-element.19.doc_ref), custom_call_target="tpu_custom_call" | custom-call | tf_op jit(solution)/shard_map/pallas_call | solution.py:355
  56.1 5.4 %all-to-all-done.grad_ref = bf16[16,64,128]{2,1,0:T(8,128)(2,1)S(1)} async-done(((bf16[16,64,128]{2,1,0:T(8,128)(2,1)}), bf16[16,64,128]{2,1,0:T(8,128)(2,1)S(1)}, u32[]{:S(2)}, u32[]{:S(2)}) %all-to-all-start) | async-done | bytes 262176 | tf_op jit(solution)/shard_map/all_to_all | solution.py:336
  61.5 3.7 %all-to-all-start.4 = ((bf16[16,64,128]{2,1,0:T(8,128)(2,1)}), bf16[16,64,128]{2,1,0:T(8,128)(2,1)S(1)}, u32[]{:S(2)}, u32[]{:S(2)}) async-start(bf16[16,64,128]{2,1,0:T(8,128)(2,1)} %get-tuple-element.23), calls=%async_computation.4 | async-start | bytes 524288 | tf_op jit(solution)/shard_map/all_to_all | solution.py:362
  65.3 2.3 %shard_map.118 = (bf16[16,80,128]{2,1,0:T(8,128)(2,1)}, f32[8,1152]{1,0:T(8,128)}) custom-call(bf16[16,64,128]{2,1,0:T(8,128)(2,1)S(1)} %all-to-all-done.grad_ref, bf16[8,128,256]{2,1,0:T(8,128)(2,1)S(1)} %get-tuple-element.17.gate_t_ref, f32[8,1280]{1,0:T(8,128)S(1)} %get-tuple-element.18.rows_ref, f32[256,128]{1,0:T(8,128)S(1)} %get-tuple-element.19.doc_ref, ...), custom_call_target="tpu_custom_call" | custom-call | tf_op jit(solution)/shard_map/pallas_call | solution.py:355
  67.5 7.5 %all-to-all-done.4.back_ref = bf16[16,64,128]{2,1,0:T(8,128)(2,1)S(1)} async-done(((bf16[16,64,128]{2,1,0:T(8,128)(2,1)}), bf16[16,64,128]{2,1,0:T(8,128)(2,1)S(1)}, u32[]{:S(2)}, u32[]{:S(2)}) %all-to-all-start.4) | async-done | bytes 262176 | tf_op jit(solution)/shard_map/all_to_all | solution.py:362
  75.1 3.5 %all-to-all-start.3 = ((bf16[16,80,128]{2,1,0:T(8,128)(2,1)}), bf16[16,80,128]{2,1,0:T(8,128)(2,1)S(1)}, u32[]{:S(2)}, u32[]{:S(2)}) async-start(bf16[16,80,128]{2,1,0:T(8,128)(2,1)} %get-tuple-element.22), calls=%async_computation.3 | async-start | bytes 655360 | tf_op jit(solution)/shard_map/all_to_all | solution.py:362
  78.6 1.2 %shard_map.119.acc_ref = f32[128,2048]{1,0:T(8,128)S(1)} custom-call(bf16[16,64,128]{2,1,0:T(8,128)(2,1)S(1)} %all-to-all-done.4.back_ref, s32[1,2048]{1,0:T(1,128)S(1)} %get-tuple-element.14.rank_ref, bf16[128,2048]{1,0:T(8,128)(2,1)S(1)} %get-tuple-element.15.conv_ref, f32[1,2048]{1,0:T(1,128)S(1)} %get-tuple-element.24.skip_ref), custom_call_target="tpu_custom_call" | custom-call | tf_op jit(solution)/shard_map/pallas_call | solution.py:368
  79.8 9.8 %all-to-all-done.3.back_ref = bf16[16,80,128]{2,1,0:T(8,128)(2,1)S(1)} async-done(((bf16[16,80,128]{2,1,0:T(8,128)(2,1)}), bf16[16,80,128]{2,1,0:T(8,128)(2,1)S(1)}, u32[]{:S(2)}, u32[]{:S(2)}) %all-to-all-start.3) | async-done | bytes 327712 | tf_op jit(solution)/shard_map/all_to_all | solution.py:362
  89.7 3.2 %shard_map.120 = (bf16[128,2048]{1,0:T(8,128)(2,1)}, bf16[128,2048]{1,0:T(8,128)(2,1)}, f32[128,128]{1,0:T(8,128)}) custom-call(bf16[16,80,128]{2,1,0:T(8,128)(2,1)S(1)} %all-to-all-done.3.back_ref, s32[1,2048]{1,0:T(1,128)S(1)} %get-tuple-element.14.rank_ref, f32[128,2048]{1,0:T(8,128)S(1)} %shard_map.119.acc_ref, bf16[128,2048]{1,0:T(8,128)(2,1)} %query_hbm.3, ...), custom_call_target="tpu_custom_call" | custom-call | tf_op jit(solution)/shard_map/pallas_call | solution.py:376
Async XLA Ops:
  4.4 27.8 %all-to-all-start.1 = ((bf16[16,128,128]{2,1,0:T(8,128)(2,1)}), bf16[16,128,128]{2,1,0:T(8,128)(2,1)S(1)}, u32[]{:S(2)}, u32[]{:S(2)}) async-start(bf16[16,128,128]{2,1,0:T(8,128)(2,1)} %get-tuple-element.16), calls=%async_computation.1 | async-start | bytes 1048576 | tf_op jit(solution)/shard_map/all_to_all | solution.py:306
  11.8 14.4 %collective-permute-start = (bf16[128,2048]{1,0:T(8,128)(2,1)}, bf16[128,2048]{1,0:T(8,128)(2,1)S(1)}, u32[]{:S(2)}, u32[]{:S(2)}) collective-permute-start(bf16[128,2048]{1,0:T(8,128)(2,1)} %grad_ref.1), channel_id=1, source_target_pairs={{0,1},{1,0},{2,3},{3,2},{4,5},{5,4},{6,7},{7,6},{8,9},{9,8},{10,11... | collective-permute-start | bytes 1572872 | tf_op jit(solution)/shard_map/ppermute | solution.py:297
  13.4 1.1 %copy-start = (bf16[128,2048]{1,0:T(8,128)(2,1)S(1)}, bf16[128,2048]{1,0:T(8,128)(2,1)}, u32[]{:S(2)}) copy-start(bf16[128,2048]{1,0:T(8,128)(2,1)} %grad_ref.1) | copy-start | bytes 1572868
  32.3 15.8 %all-to-all-start.2 = ((bf16[16,64,128]{2,1,0:T(8,128)(2,1)}), bf16[16,64,128]{2,1,0:T(8,128)(2,1)S(1)}, u32[]{:S(2)}, u32[]{:S(2)}) async-start(bf16[16,64,128]{2,1,0:T(8,128)(2,1)} %get-tuple-element.20), calls=%async_computation.2 | async-start | bytes 524288 | tf_op jit(solution)/shard_map/all_to_all | solution.py:336
  48.0 13.5 %all-to-all-start = ((bf16[16,64,128]{2,1,0:T(8,128)(2,1)}), bf16[16,64,128]{2,1,0:T(8,128)(2,1)S(1)}, u32[]{:S(2)}, u32[]{:S(2)}) async-start(bf16[16,64,128]{2,1,0:T(8,128)(2,1)} %shard_map.115), calls=%async_computation | async-start | bytes 524288 | tf_op jit(solution)/shard_map/all_to_all | solution.py:336
  61.5 13.5 %all-to-all-start.4 = ((bf16[16,64,128]{2,1,0:T(8,128)(2,1)}), bf16[16,64,128]{2,1,0:T(8,128)(2,1)S(1)}, u32[]{:S(2)}, u32[]{:S(2)}) async-start(bf16[16,64,128]{2,1,0:T(8,128)(2,1)} %get-tuple-element.23), calls=%async_computation.4 | async-start | bytes 524288 | tf_op jit(solution)/shard_map/all_to_all | solution.py:362
  75.1 14.6 %all-to-all-start.3 = ((bf16[16,80,128]{2,1,0:T(8,128)(2,1)}), bf16[16,80,128]{2,1,0:T(8,128)(2,1)S(1)}, u32[]{:S(2)}, u32[]{:S(2)}) async-start(bf16[16,80,128]{2,1,0:T(8,128)(2,1)} %get-tuple-element.22), calls=%async_computation.3 | async-start | bytes 655360 | tf_op jit(solution)/shard_map/all_to_all | solution.py:362

commit v4 on v2

--- a/solution.py
+++ b/solution.py
@@ -13,7 +13,7 @@
 NT = (((1,), (1,)), ((), ()))
 NN = (((1,), (0,)), ((), ()))
 LANES = 128
-EXTRA = 16
+EXTRA = 8
 VMEM = pl.BlockSpec(memory_space=pltpu.VMEM)
 SMEM = pl.BlockSpec(memory_space=pltpu.SMEM)
 ANY = pl.BlockSpec(memory_space=pl.ANY)
@@ -58,19 +58,22 @@
 
 
 def gate_kernel(
-    head_ref, group_ref, query_hbm, key_hbm, out_ref, rank_ref, query_ref, key_ref, column_ref, sem, *, groups, per_group
+    group_hbm, query_hbm, key_hbm, grad_hbm, out_ref, rank_ref, grad_ref, group_ref, query_ref, key_ref, column_ref, sem, *, groups, per_group
 ):
     loads = [
-        pltpu.make_async_copy(query_hbm, query_ref, sem.at[0]),
-        pltpu.make_async_copy(key_hbm, key_ref, sem.at[1]),
+        pltpu.make_async_copy(group_hbm, group_ref, sem.at[0]),
+        pltpu.make_async_copy(query_hbm, query_ref, sem.at[1]),
+        pltpu.make_async_copy(key_hbm, key_ref, sem.at[2]),
+        pltpu.make_async_copy(grad_hbm, grad_ref, sem.at[3]),
     ]
     for load in loads:
         load.start()
     channels = group_ref.shape[1]
-    local = group_ref[...] - head_ref[0] * groups
     upper = lax.broadcasted_iota(I32, (LANES, LANES), 0) < lax.broadcasted_iota(I32, (LANES, LANES), 1)
     upper = jnp.where(upper, 1.0, 0.0).astype(BF16)
     base = jnp.zeros((groups, 1), F32)
+    loads[0].wait()
+    local = group_ref[...] & (groups - 1)
     for b in range(channels // LANES):
         here = local[:, b * LANES : (b + 1) * LANES]
         member = jnp.where(lax.broadcasted_iota(I32, (groups, LANES), 0) == here, 1.0, 0.0)
@@ -79,10 +82,11 @@
         rank_ref[:, b * LANES : (b + 1) * LANES] = here * per_group + place.astype(I32)
         base = base + jnp.sum(member, axis=1, keepdims=True)
     rank_column(rank_ref[...], column_ref)
-    for load in loads:
+    for load in loads[1:3]:
         load.wait()
     gated = (query_ref[...].astype(F32) * key_ref[...].astype(F32)).astype(BF16)
     permute(gated, column_ref, out_ref)
+    loads[3].wait()
 
 
 def stream_weights(half, weight_hbm, weight_ref, sem):
@@ -110,14 +114,11 @@
         out_ref[...] = part if fresh and j == 0 else out_ref[...] + part
 
 
-def partial_kernel(half_ref, grad_hbm, weight_hbm, *refs):
-    *acc, out_ref, grad_ref, weight_ref, sem, grad_sem = refs
-    load = pltpu.make_async_copy(grad_hbm, grad_ref, grad_sem)
-    load.start()
+def partial_kernel(half_ref, grad_ref, weight_hbm, *refs):
+    *acc, out_ref, weight_ref, sem = refs
     copies, width = stream_weights(half_ref[0], weight_hbm, weight_ref, sem)
     if acc:
         out_ref[...] = acc[0][...]
-    load.wait()
     product(copies, width, grad_ref, weight_ref, out_ref, not acc)
 
 
@@ -183,36 +184,34 @@
         sums_ref[g : g + 1, :] = jnp.sum(skewed[:, :lags], axis=0, keepdims=True)
     for k in range(spans):
         if k < reach:
-            exact = sums_ref[:, k * tokens : (k + 1) * tokens]
-            high = exact.astype(BF16).astype(F32)
-            both = jnp.concatenate([high, exact - high], axis=0).astype(BF16)
+            out_ref[k, sub:, :] = sums_ref[:, k * tokens : (k + 1) * tokens].astype(BF16)
         else:
-            both = jnp.zeros((EXTRA, tokens), BF16)
-        out_ref[k, sub:, :] = both
+            out_ref[k, sub:, :] = jnp.zeros((EXTRA, tokens), BF16)
+
+
+def fetch_kernel(query_hbm, key_hbm, query_ref, key_ref, sem):
+    loads = [
+        pltpu.make_async_copy(query_hbm, query_ref, sem.at[0]),
+        pltpu.make_async_copy(key_hbm, key_ref, sem.at[1]),
+    ]
+    for load in loads:
+        load.start()
+    for load in loads:
+        load.wait()
 
 
 def gates_kernel(
-    back_ref, rank_ref, conv_ref, skip_ref, query_hbm, key_hbm, grad_query_hbm, grad_key_hbm, filt_hbm,
-    query_ref, key_ref, grad_query_ref, grad_key_ref, filt_ref, sorted_ref, load_sem, store_sem, filt_sem, *, sub_groups
+    back_ref, rank_ref, conv_ref, skip_ref, query_ref, key_ref, grad_query_hbm, grad_key_hbm, filt_hbm,
+    grad_query_ref, grad_key_ref, filt_ref, sorted_ref, store_sem, filt_sem, *, sub_groups
 ):
     spans, rows, tokens = back_ref.shape
     sub = rows - EXTRA
     channels = rank_ref.shape[1]
-    loads = [
-        pltpu.make_async_copy(query_hbm, query_ref, load_sem.at[0]),
-        pltpu.make_async_copy(key_hbm, key_ref, load_sem.at[1]),
-    ]
-    for load in loads:
-        load.start()
+    sorted_ref[...] = back_ref[:, :sub, :].reshape(spans * sub, tokens).T
     for d in range(spans):
-        tail = back_ref[d, sub:, :].astype(F32)
-        both = tail[: EXTRA // 2] + tail[EXTRA // 2 :]
-        filt_ref[d * sub_groups : (d + 1) * sub_groups, :] = both[:sub_groups]
+        filt_ref[d * sub_groups : (d + 1) * sub_groups, :] = back_ref[d, sub:, :].astype(F32)[:sub_groups]
     stores = [pltpu.make_async_copy(filt_ref, filt_hbm, filt_sem)]
     stores[0].start()
-    sorted_ref[...] = back_ref[:, :sub, :].reshape(spans * sub, tokens).T
-    for load in loads:
-        load.wait()
     width = channels // store_sem.shape[1]
     for j in range(store_sem.shape[1]):
         cols = slice(j * width, (j + 1) * width)
@@ -249,30 +248,29 @@
 
     arrived = [lax.ppermute(grad_out, "head", [(i, (i + r) % heads) for i in range(heads)]) for r in range(1, heads)]
 
-    gate_sorted, rank = call(
+    gate_sorted, rank, grad_here = call(
         functools.partial(gate_kernel, groups=groups, per_group=per_group),
-        (pltpu.VMEM((spans, sub, tokens), BF16), pltpu.VMEM((1, channels), I32)),
-        [SMEM, VMEM, ANY, ANY],
-        [wide, wide, column, dma((2,))],
-    )(head.reshape(1), group_of.reshape(1, channels), query_proj, key_proj)
+        (
+            pltpu.VMEM((spans, sub, tokens), BF16),
+            pltpu.VMEM((1, channels), I32),
+            pltpu.VMEM((tokens, feats), BF16),
+        ),
+        [ANY, ANY, ANY, ANY],
+        [pltpu.VMEM((1, channels), I32), wide, wide, column, dma((4,))],
+    )(group_of.reshape(1, channels), query_proj, key_proj, grad_out)
     gate_moved = lax.all_to_all(gate_sorted, "ctx", 0, 0)
 
     parts = min(8, feats // LANES)
     acc = None
-    for r, grad in enumerate([grad_out] + arrived):
+    for r, grad in enumerate([grad_here] + arrived):
         source = ((head + heads - r) % heads).reshape(1)
         if r < heads - 1:
             acc = call(
                 partial_kernel,
                 pltpu.VMEM((tokens, channels), F32),
-                [SMEM, ANY, ANY] + ([] if acc is None else [VMEM]),
-                [
-                    pltpu.VMEM((tokens, feats), BF16),
-                    pltpu.VMEM((channels, feats), BF16),
-                    dma((parts,)),
-                    dma,
-                ],
-            )(source, grad, out_proj, *([] if acc is None else [acc]))
+                [SMEM, VMEM, ANY] + ([] if acc is None else [VMEM]),
+                [pltpu.VMEM((channels, feats), BF16), dma((parts,))],
+            )(source, on_chip(grad), out_proj, *([] if acc is None else [acc]))
             acc = on_chip(acc)
         else:
             conv_sorted, conv_grad = call(
@@ -308,9 +306,10 @@
         [VMEM] * 4,
         [
             pltpu.VMEM((sub_groups, spans * per_group, lags), BF16),
-            pltpu.VMEM((EXTRA // 2, lags), F32),
+            pltpu.VMEM((EXTRA, lags), F32),
         ],
     )(on_chip(conv_moved), on_chip(gate_t), on_chip(rows), on_chip(doc))
+    query_here, key_here = call(fetch_kernel, (wide, wide), [ANY, ANY], [dma((2,))])(query_proj, key_proj)
     back_moved = lax.all_to_all(on_chip(back), "ctx", 0, 0)
 
     return call(
@@ -320,10 +319,17 @@
             jax.ShapeDtypeStruct((tokens, channels), BF16),
             jax.ShapeDtypeStruct((groups, tokens), F32),
         ),
-        [VMEM, VMEM, VMEM, VMEM, ANY, ANY],
-        [wide, wide, wide, wide, pltpu.VMEM((groups, tokens), F32), wide, dma((2,)), dma((2, 8)), dma],
+        [VMEM] * 6,
+        [wide, wide, pltpu.VMEM((groups, tokens), F32), wide, dma((2, min(8, channels // LANES))), dma],
         (ANY, ANY, ANY),
-    )(on_chip(back_moved), on_chip(rank), on_chip(conv_grad), on_chip(skip), query_proj, key_proj)
+    )(
+        on_chip(back_moved),
+        on_chip(rank),
+        on_chip(conv_grad),
+        on_chip(skip),
+        on_chip(query_here),
+        on_chip(key_here),
+    )
 
 
 def solution(mesh):

time: 82.4 us -> 79 us (0.959)
  blocking collectives: 21.2 us -> 0 us
  waiting for transfers between devices: 18.2 us -> 33.9 us
  starting transfers between devices: 14.7 us -> 18.9 us
  Pallas kernels: 25.7 us -> 23.5 us
    all_to_all x1 -> x0, blocking collectives: 21.2 us -> none  [per_device(): back_moved = lax.all_to_all(on_chip(back), 'ctx', 0, 0)]
    all_to_all x0 -> x1, waiting for transfers between devices: none -> 13.6 us  [per_device(): back_moved = lax.all_to_all(on_chip(back), 'ctx', 0, 0)]
    all_to_all x0 -> x1, starting transfers between devices: none -> 4.16 us  [per_device(): back_moved = lax.all_to_all(on_chip(back), 'ctx', 0, 0)]
    ppermute x1, waiting for transfers between devices: 6.37 us -> 8.51 us  [per_device(): lax.ppermute(grad_out, 'head', [(i, (i + r) % heads) for i in range(heads)])]
    pallas_call x1, Pallas kernels: 3.95 us -> 2.85 us  [per_device(): call(functools.partial(gates_kernel, sub_groups=sub_groups), (jax.ShapeDt...]
    pallas_call x1, Pallas kernels: 4.77 us -> 3.8 us  [per_device(): call(functools.partial(gate_kernel, groups=groups, per_group=per_group),...]
    pallas_call x1 -> x2, Pallas kernels: 6.48 us -> 5.57 us  [the longest x1 4.35 us: per_device(): call(partial_kernel, pltpu.VMEM((tokens, channels), F32), [SMEM, VMEM, AN...]
  transfers between devices with their start and end apart: 3 -> 4, of which waited for: 2 -> 3; matrix products, arithmetic and copies ran while one was open for 2% -> 2% of each run, Pallas kernels for 17% -> 17%
where the time goes in v4:
time: 79 us; the launch traced here: 78.4 us
  waiting for transfers between devices  33.9 us (43%)
  Pallas kernels  23.5 us (30%)
  starting transfers between devices  18.9 us (24%)
  other arithmetic  1.35 us (2%)
    all_to_all x1, waiting for transfers between devices, per_device(): back_moved = lax.all_to_all(on_chip(back), 'ctx', 0, 0)  13.6 us
    all_to_all x1, waiting for transfers between devices, per_device(): conv_moved = lax.all_to_all(on_chip(conv_sorted), 'ctx', 0, 0)  11.8 us
    ppermute x1, waiting for transfers between devices, per_device(): lax.ppermute(grad_out, 'head', [(i, (i + r) % heads) for i in range(heads)])  8.51 us
    all_to_all x1, starting transfers between devices, per_device(): gate_moved = lax.all_to_all(gate_sorted, 'ctx', 0, 0)  7.4 us
    pallas_call x1, Pallas kernels, per_device(): call(last_kernel, (pltpu.VMEM((spans, sub, tokens), BF16), pltpu.VMEM((to...  6.68 us
    all_to_all x1, starting transfers between devices, per_device(): conv_moved = lax.all_to_all(on_chip(conv_sorted), 'ctx', 0, 0)  5.73 us
    pallas_call x1, Pallas kernels, per_device(): call(partial_kernel, pltpu.VMEM((tokens, channels), F32), [SMEM, VMEM, AN...  4.35 us
    all_to_all x1, starting transfers between devices, per_device(): back_moved = lax.all_to_all(on_chip(back), 'ctx', 0, 0)  4.16 us
  transfers between devices with their start and end apart: 4, of which 3 were waited for; matrix products, arithmetic and copies ran while one was open for 2% of the time, Pallas kernels for 17%

profile of v4, /device:TPU:0, one launch (start us, length us, event | category | flops | bytes accessed | tf_op | source)
XLA Modules:
  0.0 78.4 jit_solution(8718615704258357635)
XLA Ops:
  0.6 3.8 %shard_map.112 = (bf16[16,128,128]{2,1,0:T(8,128)(2,1)}, s32[1,2048]{1,0:T(1,128)S(1)}, bf16[128,2048]{1,0:T(8,128)(2,1)S(1)}) custom-call(s32[1,2048]{1,0:T(1,128)} %bitcast.4, bf16[128,2048]{1,0:T(8,128)(2,1)} %query_hbm.3, bf16[128,2048]{1,0:T(8,128)(2,1)} %key_hbm.3, bf16[128,2048]{1,0:T(8,128)(2,1)} %grad_hbm.1), custom_call_target="tpu_custom_call" | custom-call | tf_op jit(solution)/shard_map/pallas_call | solution.py:251
  4.4 7.4 %all-to-all-start.1 = ((bf16[16,128,128]{2,1,0:T(8,128)(2,1)}), bf16[16,128,128]{2,1,0:T(8,128)(2,1)S(1)}, u32[]{:S(2)}, u32[]{:S(2)}) async-start(bf16[16,128,128]{2,1,0:T(8,128)(2,1)} %get-tuple-element.17), calls=%async_computation.1 | async-start | bytes 1048576 | tf_op jit(solution)/shard_map/all_to_all | solution.py:261
  11.8 1.6 %collective-permute-start = (bf16[128,2048]{1,0:T(8,128)(2,1)}, bf16[128,2048]{1,0:T(8,128)(2,1)S(1)}, u32[]{:S(2)}, u32[]{:S(2)}) collective-permute-start(bf16[128,2048]{1,0:T(8,128)(2,1)} %grad_hbm.1), channel_id=1, source_target_pairs={{0,1},{1,0},{2,3},{3,2},{4,5},{5,4},{6,7},{7,6},{8,9},{9,8},{10,11... | collective-permute-start | bytes 1572872 | tf_op jit(solution)/shard_map/ppermute | solution.py:249
  13.4 4.3 %shard_map.113.acc_ref = f32[128,2048]{1,0:T(8,128)S(1)} custom-call(s32[1]{0:T(128)} %bitcast.2.half_ref, bf16[128,2048]{1,0:T(8,128)(2,1)S(1)} %get-tuple-element.15.grad_ref, bf16[2048,4096]{1,0:T(8,128)(2,1)} %weight_hbm.3), custom_call_target="tpu_custom_call" | custom-call | tf_op jit(solution)/shard_map/pallas_call | solution.py:268
  17.8 8.5 %collective-permute-done.grad_ref = bf16[128,2048]{1,0:T(8,128)(2,1)S(1)} collective-permute-done((bf16[128,2048]{1,0:T(8,128)(2,1)}, bf16[128,2048]{1,0:T(8,128)(2,1)S(1)}, u32[]{:S(2)}, u32[]{:S(2)}) %collective-permute-start) | collective-permute-done | bytes 524320 | tf_op jit(solution)/shard_map/ppermute | solution.py:249
  26.3 6.7 %shard_map.114 = (bf16[16,128,128]{2,1,0:T(8,128)(2,1)}, bf16[128,2048]{1,0:T(8,128)(2,1)S(1)}) custom-call(s32[1]{0:T(128)} %bitcast.half_ref, s32[1,2048]{1,0:T(1,128)S(1)} %get-tuple-element.14.rank_ref, bf16[128,2048]{1,0:T(8,128)(2,1)S(1)} %collective-permute-done.grad_ref, f32[128,2048]{1,0:T(8,128)S(1)} %shard_map.113.acc_ref, ...), custom_call_target="tpu_custom_call" | custom-call | tf_op jit(solution)/shard_map/pallas_call | solution.py:276
  33.0 0.0 all-to-all-done.1.gate_ref
  33.0 5.7 %all-to-all-start = ((bf16[16,128,128]{2,1,0:T(8,128)(2,1)}), bf16[16,128,128]{2,1,0:T(8,128)(2,1)S(1)}, u32[]{:S(2)}, u32[]{:S(2)}) async-start(bf16[16,128,128]{2,1,0:T(8,128)(2,1)} %get-tuple-element.16), calls=%async_computation | async-start | bytes 1048576 | tf_op jit(solution)/shard_map/all_to_all | solution.py:289
  38.7 1.3 %dynamic-slice_convert_fusion.filt_ref = f32[8,1152]{1,0:T(8,128)} fusion(bf16[128,2048]{1,0:T(8,128)(2,1)} %param.14, s32[]{:T(128)S(6)} %select_n.16), kind=kLoop, calls=%fused_computation | loop fusion | flops 9216 | bytes 55300 | tf_op jit(solution)/shard_map/convert_element_type | solution.py:291
  40.1 1.1 %shard_map.115 = (bf16[8,128,256]{2,1,0:T(8,128)(2,1)S(1)}, f32[8,1280]{1,0:T(8,128)S(1)}, f32[256,128]{1,0:T(8,128)S(1)}, f32[1,2048]{1,0:T(1,128)S(1)}) custom-call(s32[4]{0:T(128)} %docs_ref.1, f32[8,1152]{1,0:T(8,128)} %dynamic-slice_convert_fusion.filt_ref, bf16[16,128,128]{2,1,0:T(8,128)(2,1)S(1)} %all-to-all-done.1.gate_ref, f32[1,2048]{1,0:T(1,128)} %bitcast.5), custom_call_target="tpu_custom_call" | custom-call | tf_op jit(solution)/shard_map/pallas_call | solution.py:292
  41.2 11.8 %all-to-all-done.grad_ref = bf16[16,128,128]{2,1,0:T(8,128)(2,1)S(1)} async-done(((bf16[16,128,128]{2,1,0:T(8,128)(2,1)}), bf16[16,128,128]{2,1,0:T(8,128)(2,1)S(1)}, u32[]{:S(2)}, u32[]{:S(2)}) %all-to-all-start) | async-done | bytes 524320 | tf_op jit(solution)/shard_map/all_to_all | solution.py:289
  53.0 3.6 %shard_map.116 = bf16[16,136,128]{2,1,0:T(8,128)(2,1)} custom-call(bf16[16,128,128]{2,1,0:T(8,128)(2,1)S(1)} %all-to-all-done.grad_ref, bf16[8,128,256]{2,1,0:T(8,128)(2,1)S(1)} %get-tuple-element.18.gate_t_ref, f32[8,1280]{1,0:T(8,128)S(1)} %get-tuple-element.19.rows_ref, f32[256,128]{1,0:T(8,128)S(1)} %get-tuple-element.20.doc_ref), custom_call_target="tpu_custom_call" | custom-call | tf_op jit(solution)/shard_map/pallas_call | solution.py:303
  56.6 4.2 %all-to-all-start.2 = ((bf16[16,136,128]{2,1,0:T(8,128)(2,1)}), bf16[16,136,128]{2,1,0:T(8,128)(2,1)S(1)}, u32[]{:S(2)}, u32[]{:S(2)}) async-start(bf16[16,136,128]{2,1,0:T(8,128)(2,1)} %shard_map.116), calls=%async_computation.2 | async-start | bytes 1114112 | tf_op jit(solution)/shard_map/all_to_all | solution.py:313
  60.7 1.2 %shard_map.117 = (bf16[128,2048]{1,0:T(8,128)(2,1)S(1)}, bf16[128,2048]{1,0:T(8,128)(2,1)S(1)}) custom-call(bf16[128,2048]{1,0:T(8,128)(2,1)} %query_hbm.3, bf16[128,2048]{1,0:T(8,128)(2,1)} %key_hbm.3), custom_call_target="tpu_custom_call" | custom-call | tf_op jit(solution)/shard_map/pallas_call | solution.py:312
  62.0 13.6 %all-to-all-done.2.back_ref = bf16[16,136,128]{2,1,0:T(8,128)(2,1)S(1)} async-done(((bf16[16,136,128]{2,1,0:T(8,128)(2,1)}), bf16[16,136,128]{2,1,0:T(8,128)(2,1)S(1)}, u32[]{:S(2)}, u32[]{:S(2)}) %all-to-all-start.2) | async-done | bytes 557088 | tf_op jit(solution)/shard_map/all_to_all | solution.py:313
  75.5 2.9 %shard_map.118 = (bf16[128,2048]{1,0:T(8,128)(2,1)}, bf16[128,2048]{1,0:T(8,128)(2,1)}, f32[128,128]{1,0:T(8,128)}) custom-call(bf16[16,136,128]{2,1,0:T(8,128)(2,1)S(1)} %all-to-all-done.2.back_ref, s32[1,2048]{1,0:T(1,128)S(1)} %get-tuple-element.14.rank_ref, bf16[128,2048]{1,0:T(8,128)(2,1)S(1)} %get-tuple-element.21.conv_ref, ...), custom_call_target="tpu_custom_call" | custom-call | tf_op jit(solution)/shard_map/pallas_call | solution.py:315
Async XLA Ops:
  4.4 28.5 %all-to-all-start.1 = ((bf16[16,128,128]{2,1,0:T(8,128)(2,1)}), bf16[16,128,128]{2,1,0:T(8,128)(2,1)S(1)}, u32[]{:S(2)}, u32[]{:S(2)}) async-start(bf16[16,128,128]{2,1,0:T(8,128)(2,1)} %get-tuple-element.17), calls=%async_computation.1 | async-start | bytes 1048576 | tf_op jit(solution)/shard_map/all_to_all | solution.py:261
  11.8 14.4 %collective-permute-start = (bf16[128,2048]{1,0:T(8,128)(2,1)}, bf16[128,2048]{1,0:T(8,128)(2,1)S(1)}, u32[]{:S(2)}, u32[]{:S(2)}) collective-permute-start(bf16[128,2048]{1,0:T(8,128)(2,1)} %grad_hbm.1), channel_id=1, source_target_pairs={{0,1},{1,0},{2,3},{3,2},{4,5},{5,4},{6,7},{7,6},{8,9},{9,8},{10,11... | collective-permute-start | bytes 1572872 | tf_op jit(solution)/shard_map/ppermute | solution.py:249
  33.0 20.0 %all-to-all-start = ((bf16[16,128,128]{2,1,0:T(8,128)(2,1)}), bf16[16,128,128]{2,1,0:T(8,128)(2,1)S(1)}, u32[]{:S(2)}, u32[]{:S(2)}) async-start(bf16[16,128,128]{2,1,0:T(8,128)(2,1)} %get-tuple-element.16), calls=%async_computation | async-start | bytes 1048576 | tf_op jit(solution)/shard_map/all_to_all | solution.py:289
  56.6 19.0 %all-to-all-start.2 = ((bf16[16,136,128]{2,1,0:T(8,128)(2,1)}), bf16[16,136,128]{2,1,0:T(8,128)(2,1)S(1)}, u32[]{:S(2)}, u32[]{:S(2)}) async-start(bf16[16,136,128]{2,1,0:T(8,128)(2,1)} %shard_map.116), calls=%async_computation.2 | async-start | bytes 1114112 | tf_op jit(solution)/shard_map/all_to_all | solution.py:313

commit v5 on v4

--- a/solution.py
+++ b/solution.py
@@ -43,18 +43,69 @@
     column_ref[...] = wide.T.astype(I32)
 
 
-def permute(by_token, column_ref, out_ref):
+def permute(by_token, column_ref, starts, width, store):
     channels = column_ref.shape[0]
-    rows = out_ref.shape[1]
-    width = min(2 * LANES, channels)
     lane = lax.broadcasted_iota(I32, (channels, LANES), 1)
-    for p in range(0, channels, width):
-        picks = [
-            jnp.where(column_ref[...] == lane + (p + q), 1.0, 0.0).astype(BF16)
-            for q in range(0, width, LANES)
-        ]
-        moved = dot(by_token, jnp.concatenate(picks, axis=1), NN).T.astype(BF16)
-        out_ref[p // rows : (p + width) // rows] = moved.reshape(width // rows, rows, -1)
+    unit = min(width, LANES)
+    per_dot = max(1, 2 * LANES // width)
+    for i in range(0, len(starts), per_dot):
+        picks = []
+        for start in starts[i : i + per_dot]:
+            for q in range(0, width, unit):
+                picks.append((start + q, unit))
+        mats = []
+        per_tile = LANES // unit
+        for j in range(0, len(picks), per_tile):
+            want = lane + picks[j][0]
+            for t in range(1, per_tile):
+                want = jnp.where(lane >= t * unit, lane + (picks[j + t][0] - t * unit), want)
+            mats.append(jnp.where(column_ref[...] == want, 1.0, 0.0).astype(BF16))
+        moved = dot(by_token, jnp.concatenate(mats, axis=1), NN).T.astype(BF16)
+        for j in range(min(per_dot, len(starts) - i)):
+            store(i + j, moved[j * width : (j + 1) * width])
+
+
+def split_pair(ctx, full_ref, mine_ref, other_ref):
+    place = ctx & 1
+    pair = ctx >> 1
+    for p in range(mine_ref.shape[0]):
+        mine_ref[pair ^ p] = full_ref[2 * p + place]
+        other_ref[pair ^ p] = full_ref[2 * p + 1 - place]
+
+
+def distances(count):
+    ring = count // 4
+
+    def hops(e):
+        return (e & 1) + min(e >> 1, ring - (e >> 1))
+
+    return [0] + sorted(range(1, count // 2), key=lambda e: (-hops(e), -(e == 4), e))
+
+
+def join_pair(ctx, packs, full_ref):
+    for e, pack in zip(distances(2 * len(packs)), packs):
+        full_ref[ctx ^ (2 * e)] = pack[0]
+        full_ref[ctx ^ (2 * e + 1)] = pack[1]
+
+
+def pack_kernel(mine_ref, got_ref, *packs):
+    for e, pack in zip(distances(2 * len(packs)), packs):
+        pack[0] = mine_ref[e]
+        pack[1] = got_ref[e]
+
+
+def exchange(mine, swap_other, count):
+    got = lax.ppermute(on_chip(swap_other), "ctx", [(i, i ^ 1) for i in range(count)])
+    mine = mine()
+    shape = pltpu.VMEM((2,) + mine.shape[1:], BF16)
+    packs = call(pack_kernel, (shape,) * (count // 2), [VMEM, VMEM])(
+        on_chip(mine), on_chip(got)
+    )
+    out = []
+    for e, pack in zip(distances(count), packs):
+        moved = lax.ppermute(on_chip(pack), "ctx", [(i, i ^ (2 * e)) for i in range(count)]) if e else pack
+        out.append(on_chip(moved))
+    return out
 
 
 def gate_kernel(
@@ -85,7 +136,12 @@
     for load in loads[1:3]:
         load.wait()
     gated = (query_ref[...].astype(F32) * key_ref[...].astype(F32)).astype(BF16)
-    permute(gated, column_ref, out_ref)
+    rows = out_ref.shape[1]
+
+    def store(i, block):
+        out_ref[i] = block
+
+    permute(gated, column_ref, range(0, channels, rows), rows, store)
     loads[3].wait()
 
 
@@ -122,8 +178,17 @@
     product(copies, width, grad_ref, weight_ref, out_ref, not acc)
 
 
+def pair_blocks(ctx, place, by_token, column_ref, out_ref):
+    pairs, rows, _ = out_ref.shape
+
+    def store(p, block):
+        out_ref[(ctx >> 1) ^ p] = block
+
+    permute(by_token, column_ref, [(2 * p + place) * rows for p in range(pairs)], rows, store)
+
+
 def last_kernel(
-    half_ref, rank_ref, grad_ref, acc_ref, weight_hbm, value_hbm, out_ref, conv_ref, total_ref, weight_ref, value_ref, column_ref, sem, value_sem
+    half_ref, ctx_ref, rank_ref, grad_ref, acc_ref, weight_hbm, value_hbm, out_ref, conv_ref, total_ref, weight_ref, value_ref, column_ref, sem, value_sem
 ):
     load = pltpu.make_async_copy(value_hbm, value_ref, value_sem)
     copies, width = stream_weights(half_ref[0], weight_hbm, weight_ref, sem)
@@ -133,7 +198,14 @@
     product(copies, width, grad_ref, weight_ref, total_ref, False)
     load.wait()
     conv_ref[...] = (total_ref[...] * value_ref[...].astype(F32)).astype(BF16)
-    permute(conv_ref[...], column_ref, out_ref)
+    ctx = ctx_ref[0]
+    pair_blocks(ctx, 1 - (ctx & 1), conv_ref[...], column_ref, out_ref)
+
+
+def mine_kernel(ctx_ref, rank_ref, conv_ref, out_ref, column_ref):
+    rank_column(rank_ref[...], column_ref)
+    ctx = ctx_ref[0]
+    pair_blocks(ctx, ctx & 1, conv_ref[...], column_ref, out_ref)
 
 
 def prepare_kernel(docs_ref, filt_ref, gate_ref, skip_ref, gate_t_ref, rows_ref, doc_ref, skip_out_ref, *, per_group):
@@ -156,7 +228,9 @@
     skip_out_ref[...] = skip_ref[...]
 
 
-def conv_kernel(grad_ref, gate_t_ref, rows_ref, doc_ref, out_ref, moved_ref, sums_ref, *, per_group):
+def conv_kernel(ctx_ref, gate_t_ref, rows_ref, doc_ref, *refs, per_group):
+    *packs, mine_ref, other_ref, grad_ref, out_ref, moved_ref, sums_ref = refs
+    join_pair(ctx_ref[0], packs, grad_ref)
     spans, sub, tokens = grad_ref.shape
     groups, padded = rows_ref.shape
     lags = padded - tokens
@@ -187,6 +261,7 @@
             out_ref[k, sub:, :] = sums_ref[:, k * tokens : (k + 1) * tokens].astype(BF16)
         else:
             out_ref[k, sub:, :] = jnp.zeros((EXTRA, tokens), BF16)
+    split_pair(ctx_ref[0], out_ref, mine_ref, other_ref)
 
 
 def fetch_kernel(query_hbm, key_hbm, query_ref, key_ref, sem):
@@ -201,9 +276,11 @@
 
 
 def gates_kernel(
-    back_ref, rank_ref, conv_ref, skip_ref, query_ref, key_ref, grad_query_hbm, grad_key_hbm, filt_hbm,
-    grad_query_ref, grad_key_ref, filt_ref, sorted_ref, store_sem, filt_sem, *, sub_groups
+    ctx_ref, rank_ref, conv_ref, skip_ref, query_ref, key_ref, *refs, sub_groups
 ):
+    *packs, grad_query_hbm, grad_key_hbm, filt_hbm = refs[:-7]
+    grad_query_ref, grad_key_ref, filt_ref, sorted_ref, back_ref, store_sem, filt_sem = refs[-7:]
+    join_pair(ctx_ref[0], packs, back_ref)
     spans, rows, tokens = back_ref.shape
     sub = rows - EXTRA
     channels = rank_ref.shape[1]
@@ -237,6 +314,7 @@
     spans = lax.axis_size("ctx")
     heads = lax.axis_size("head")
     position = lax.axis_index("ctx")
+    ctx = position.reshape(1)
     head = lax.axis_index("head")
     sub = channels // spans
     sub_groups = sub // per_group
@@ -275,8 +353,8 @@
         else:
             conv_sorted, conv_grad = call(
                 last_kernel,
-                (pltpu.VMEM((spans, sub, tokens), BF16), pltpu.VMEM((tokens, channels), BF16)),
-                [SMEM, VMEM, VMEM, VMEM, ANY, ANY],
+                (pltpu.VMEM((spans // 2, sub, tokens), BF16), pltpu.VMEM((tokens, channels), BF16)),
+                [SMEM, SMEM, VMEM, VMEM, VMEM, ANY, ANY],
                 [
                     pltpu.VMEM((tokens, channels), F32),
                     pltpu.VMEM((channels, feats), BF16),
@@ -285,8 +363,14 @@
                     dma((parts,)),
                     dma,
                 ],
-            )(source, on_chip(rank), on_chip(grad), acc, out_proj, value_proj)
-    conv_moved = lax.all_to_all(on_chip(conv_sorted), "ctx", 0, 0)
+            )(source, ctx, on_chip(rank), on_chip(grad), acc, out_proj, value_proj)
+
+    def conv_mine():
+        return call(
+            mine_kernel, pltpu.VMEM((spans // 2, sub, tokens), BF16), [SMEM, VMEM, VMEM], [column]
+        )(ctx, on_chip(rank), on_chip(conv_grad))
+
+    conv_moved = exchange(conv_mine, conv_sorted, spans)
 
     filt_sub = lax.dynamic_slice(filters, (position * sub_groups, 0), (sub_groups, lags)).astype(F32)
     gate_t, rows, doc, skip = call(
@@ -300,17 +384,19 @@
         [SMEM, VMEM, VMEM, VMEM],
     )(doc_lengths, filt_sub, on_chip(gate_moved), skip_gain.reshape(1, channels))
 
-    back = call(
+    back, back_other = call(
         functools.partial(conv_kernel, per_group=per_group),
-        pltpu.VMEM((spans, sub + EXTRA, tokens), BF16),
-        [VMEM] * 4,
+        (pltpu.VMEM((spans // 2, sub + EXTRA, tokens), BF16),) * 2,
+        [SMEM] + [VMEM] * (3 + spans // 2),
         [
+            pltpu.VMEM((spans, sub, tokens), BF16),
+            pltpu.VMEM((spans, sub + EXTRA, tokens), BF16),
             pltpu.VMEM((sub_groups, spans * per_group, lags), BF16),
             pltpu.VMEM((EXTRA, lags), F32),
         ],
-    )(on_chip(conv_moved), on_chip(gate_t), on_chip(rows), on_chip(doc))
+    )(ctx, on_chip(gate_t), on_chip(rows), on_chip(doc), *conv_moved)
     query_here, key_here = call(fetch_kernel, (wide, wide), [ANY, ANY], [dma((2,))])(query_proj, key_proj)
-    back_moved = lax.all_to_all(on_chip(back), "ctx", 0, 0)
+    back_moved = exchange(lambda: back, back_other, spans)
 
     return call(
         functools.partial(gates_kernel, sub_groups=sub_groups),
@@ -319,16 +405,18 @@
             jax.ShapeDtypeStruct((tokens, channels), BF16),
             jax.ShapeDtypeStruct((groups, tokens), F32),
         ),
-        [VMEM] * 6,
-        [wide, wide, pltpu.VMEM((groups, tokens), F32), wide, dma((2, min(8, channels // LANES))), dma],
+        [SMEM] + [VMEM] * (5 + spans // 2),
+        [wide, wide, pltpu.VMEM((groups, tokens), F32), wide]
+        + [pltpu.VMEM((spans, sub + EXTRA, tokens), BF16), dma((2, min(8, channels // LANES))), dma],
         (ANY, ANY, ANY),
     )(
-        on_chip(back_moved),
+        ctx,
         on_chip(rank),
         on_chip(conv_grad),
         on_chip(skip),
         on_chip(query_here),
         on_chip(key_here),
+        *back_moved,
     )
 
 

time: 79 us -> 67.9 us (0.86)
  waiting for transfers between devices: 33.9 us -> 8.27 us
  starting transfers between devices: 18.9 us -> 34.5 us
  Pallas kernels: 23.5 us -> 22.5 us
    ppermute x0 -> x16, starting transfers between devices: none -> 25.5 us  [the longest x14 25 us: exchange(): lax.ppermute(on_chip(pack), 'ctx', [(i, i ^ 2 * e) for i in range(count)])]
    all_to_all x2 -> x0, waiting for transfers between devices: 25.4 us -> none  [the longest x1 13.6 us: per_device(): back_moved = lax.all_to_all(on_chip(back), 'ctx', 0, 0)]
    all_to_all x2 -> x0, starting transfers between devices: 9.89 us -> none  [the longest x1 5.73 us: per_device(): conv_moved = lax.all_to_all(on_chip(conv_sorted), 'ctx', 0, 0)]
    ppermute x1, waiting for transfers between devices: 8.51 us -> 0.01 us  [per_device(): lax.ppermute(grad_out, 'head', [(i, (i + r) % heads) for i in range(heads)])]
    ppermute x0 -> x16, waiting for transfers between devices: none -> 8.26 us  [the longest x14 6.44 us: exchange(): lax.ppermute(on_chip(pack), 'ctx', [(i, i ^ 2 * e) for i in range(count)])]
    ppermute x1, starting transfers between devices: 1.58 us -> 3.06 us  [per_device(): lax.ppermute(grad_out, 'head', [(i, (i + r) % heads) for i in range(heads)])]
    all_to_all x1, starting transfers between devices: 7.4 us -> 5.93 us  [per_device(): gate_moved = lax.all_to_all(gate_sorted, 'ctx', 0, 0)]
    pallas_call x2 -> x5, Pallas kernels: 10.3 us -> 9.13 us  [the longest x1 5.2 us: per_device(): call(last_kernel, (pltpu.VMEM((spans // 2, sub, tokens), BF16), pltpu.VME...]
  transfers between devices with their start and end apart: 4 -> 18, of which waited for: 3 -> 6; matrix products, arithmetic and copies ran while one was open for 2% -> 2% of each run, Pallas kernels for 17% -> 24%
where the time goes in v5:
time: 67.9 us; the launch traced here: 67.6 us
  starting transfers between devices  34.5 us (51%)
  Pallas kernels  22.5 us (33%)
  waiting for transfers between devices  8.27 us (12%)
  other arithmetic  1.34 us (2%)
  between operations  0.97 us (1%)
    ppermute x14, starting transfers between devices, exchange(): lax.ppermute(on_chip(pack), 'ctx', [(i, i ^ 2 * e) for i in range(count)])  25 us
    ppermute x14, waiting for transfers between devices, exchange(): lax.ppermute(on_chip(pack), 'ctx', [(i, i ^ 2 * e) for i in range(count)])  6.44 us
    all_to_all x1, starting transfers between devices, per_device(): gate_moved = lax.all_to_all(gate_sorted, 'ctx', 0, 0)  5.93 us
    pallas_call x1, Pallas kernels, per_device(): call(last_kernel, (pltpu.VMEM((spans // 2, sub, tokens), BF16), pltpu.VME...  5.2 us
    pallas_call x1, Pallas kernels, per_device(): call(partial_kernel, pltpu.VMEM((tokens, channels), F32), [SMEM, VMEM, AN...  4.35 us
    pallas_call x1, Pallas kernels, per_device(): call(functools.partial(gate_kernel, groups=groups, per_group=per_group),...  3.8 us
    ppermute x1, starting transfers between devices, per_device(): lax.ppermute(grad_out, 'head', [(i, (i + r) % heads) for i in range(heads)])  3.06 us
    pallas_call x1, Pallas kernels, per_device(): call(functools.partial(conv_kernel, per_group=per_group), (pltpu.VMEM((sp...  2.99 us
  transfers between devices with their start and end apart: 18, of which 6 were waited for; matrix products, arithmetic and copies ran while one was open for 2% of the time, Pallas kernels for 24%

profile of v5, /device:TPU:0, one launch (start us, length us, event | category | flops | bytes accessed | tf_op | source)
XLA Modules:
  0.0 67.6 jit_solution(5470626047279774815)
XLA Ops:
  0.6 3.1 %collective-permute-start = (bf16[128,2048]{1,0:T(8,128)(2,1)}, bf16[128,2048]{1,0:T(8,128)(2,1)S(1)}, u32[]{:S(2)}, u32[]{:S(2)}) collective-permute-start(bf16[128,2048]{1,0:T(8,128)(2,1)} %grad_hbm.1), channel_id=1, source_target_pairs={{0,1},{1,0},{2,3},{3,2},{4,5},{5,4},{6,7},{7,6},{8,9},{9,8},{10,11... | collective-permute-start | bytes 1572872 | tf_op jit(solution)/shard_map/ppermute | solution.py:327
  3.7 3.8 %shard_map.112 = (bf16[16,128,128]{2,1,0:T(8,128)(2,1)}, s32[1,2048]{1,0:T(1,128)S(1)}, bf16[128,2048]{1,0:T(8,128)(2,1)S(1)}) custom-call(s32[1,2048]{1,0:T(1,128)} %bitcast.5, bf16[128,2048]{1,0:T(8,128)(2,1)} %query_hbm.3, bf16[128,2048]{1,0:T(8,128)(2,1)} %key_hbm.3, bf16[128,2048]{1,0:T(8,128)(2,1)} %grad_hbm.1), custom_call_target="tpu_custom_call" | custom-call | tf_op jit(solution)/shard_map/pallas_call | solution.py:329
  7.5 5.9 %all-to-all-start = ((bf16[16,128,128]{2,1,0:T(8,128)(2,1)}), bf16[16,128,128]{2,1,0:T(8,128)(2,1)S(1)}, u32[]{:S(2)}, u32[]{:S(2)}) async-start(bf16[16,128,128]{2,1,0:T(8,128)(2,1)} %get-tuple-element.35), calls=%async_computation | async-start | bytes 1048576 | tf_op jit(solution)/shard_map/all_to_all | solution.py:339
  13.5 4.4 %shard_map.113.acc_ref = f32[128,2048]{1,0:T(8,128)S(1)} custom-call(s32[1]{0:T(128)} %bitcast.3.half_ref, bf16[128,2048]{1,0:T(8,128)(2,1)S(1)} %get-tuple-element.33.grad_ref, bf16[2048,4096]{1,0:T(8,128)(2,1)} %weight_hbm.3), custom_call_target="tpu_custom_call" | custom-call | tf_op jit(solution)/shard_map/pallas_call | solution.py:346
  17.8 5.2 %shard_map.114 = (bf16[8,128,128]{2,1,0:T(8,128)(2,1)S(1)}, bf16[128,2048]{1,0:T(8,128)(2,1)S(1)}) custom-call(s32[1]{0:T(128)} %bitcast.2.half_ref, s32[1]{0:T(128)} %bitcast.ctx_ref, s32[1,2048]{1,0:T(1,128)S(1)} %get-tuple-element.32.rank_ref, bf16[128,2048]{1,0:T(8,128)(2,1)S(1)} %collective-permute-done.grad_ref, f32[128,2048]{1,0:T(8,128)S(1)} %shard_map.113.acc_ref, ...), custom_call_target="tpu_custom_call" | custom-call | tf_op jit(solution)/shard_map/pallas_call | solution.py:354
  24.7 3.8 %collective-permute-start.2 = (bf16[2,128,128]{2,1,0:T(8,128)(2,1)S(1)}, bf16[2,128,128]{2,1,0:T(8,128)(2,1)S(1)}, u32[]{:S(2)}, u32[]{:S(2)}) collective-permute-start(bf16[2,128,128]{2,1,0:T(8,128)(2,1)S(1)} %get-tuple-element.44), channel_id=1, source_target_pairs={{0,20},{2,22},{4,16},{6,18},{8,28},{10,30},{12,24},{14,26},{16,4},... | collective-permute-start | bytes 196616 | tf_op jit(solution)/shard_map/ppermute | solution.py:106
  29.0 1.5 %collective-permute-start.4 = (bf16[2,128,128]{2,1,0:T(8,128)(2,1)S(1)}, bf16[2,128,128]{2,1,0:T(8,128)(2,1)S(1)}, u32[]{:S(2)}, u32[]{:S(2)}) collective-permute-start(bf16[2,128,128]{2,1,0:T(8,128)(2,1)S(1)} %get-tuple-element.46), channel_id=1, source_target_pairs={{0,12},{2,14},{4,8},{6,10},{8,4},{10,6},{12,0},{14,2},{16,28},{18,... | collective-permute-start | bytes 196616 | tf_op jit(solution)/shard_map/ppermute | solution.py:106
  30.5 3.3 %collective-permute-start.5 = (bf16[2,128,128]{2,1,0:T(8,128)(2,1)S(1)}, bf16[2,128,128]{2,1,0:T(8,128)(2,1)S(1)}, u32[]{:S(2)}, u32[]{:S(2)}) collective-permute-start(bf16[2,128,128]{2,1,0:T(8,128)(2,1)S(1)} %get-tuple-element.47), channel_id=1, source_target_pairs={{0,28},{2,30},{4,24},{6,26},{8,20},{10,22},{12,16},{14,18},{16,12}... | collective-permute-start | bytes 196616 | tf_op jit(solution)/shard_map/ppermute | solution.py:106
  34.9 1.8 %collective-permute-done.3.refs_2_ = bf16[2,128,128]{2,1,0:T(8,128)(2,1)S(1)} collective-permute-done((bf16[2,128,128]{2,1,0:T(8,128)(2,1)S(1)}, bf16[2,128,128]{2,1,0:T(8,128)(2,1)S(1)}, u32[]{:S(2)}, u32[]{:S(2)}) %collective-permute-start.3) | collective-permute-done | bytes 65568 | tf_op jit(solution)/shard_map/ppermute | solution.py:106
  36.6 3.0 %collective-permute-start.8 = (bf16[2,128,128]{2,1,0:T(8,128)(2,1)S(1)}, bf16[2,128,128]{2,1,0:T(8,128)(2,1)S(1)}, u32[]{:S(2)}, u32[]{:S(2)}) collective-permute-start(bf16[2,128,128]{2,1,0:T(8,128)(2,1)S(1)} %get-tuple-element.50), channel_id=1, source_target_pairs={{0,24},{2,26},{4,28},{6,30},{8,16},{10,18},{12,20},{14,22},{16,8},... | collective-permute-start | bytes 196616 | tf_op jit(solution)/shard_map/ppermute | solution.py:106
  39.7 1.3 %dynamic-slice_convert_fusion.filt_ref = f32[8,1152]{1,0:T(8,128)} fusion(bf16[128,2048]{1,0:T(8,128)(2,1)} %param.14, s32[]{:T(128)S(6)} %select_n.16), kind=kLoop, calls=%fused_computation | loop fusion | flops 9216 | bytes 55300 | tf_op jit(solution)/shard_map/convert_element_type | solution.py:375
  41.0 1.1 %shard_map.115 = (bf16[8,128,256]{2,1,0:T(8,128)(2,1)S(1)}, f32[8,1280]{1,0:T(8,128)S(1)}, f32[256,128]{1,0:T(8,128)S(1)}, f32[1,2048]{1,0:T(1,128)S(1)}) custom-call(s32[4]{0:T(128)} %docs_ref.1, f32[8,1152]{1,0:T(8,128)} %dynamic-slice_convert_fusion.filt_ref, bf16[16,128,128]{2,1,0:T(8,128)(2,1)S(1)} %all-to-all-done.gate_ref, f32[1,2048]{1,0:T(1,128)} %bitcast.6), custom_call_target="tpu_custom_call" | custom-call | tf_op jit(solution)/shard_map/pallas_call | solution.py:376
  42.7 3.0 %shard_map.119 = (bf16[8,136,128]{2,1,0:T(8,128)(2,1)S(1)}, bf16[8,136,128]{2,1,0:T(8,128)(2,1)S(1)}) custom-call(s32[1]{0:T(128)} %bitcast.ctx_ref, bf16[8,128,256]{2,1,0:T(8,128)(2,1)S(1)} %get-tuple-element.39.gate_t_ref, f32[8,1280]{1,0:T(8,128)S(1)} %get-tuple-element.40.rows_ref, f32[256,128]{1,0:T(8,128)S(1)} %get-tuple-element.41.doc_ref, ...), custom_call_target="tpu_custom_call" | custom-call | tf_op jit(solution)/shard_map/pallas_call | solution.py:387
  45.8 1.5 %collective-permute-done.9.got_ref = bf16[8,136,128]{2,1,0:T(8,128)(2,1)S(1)} collective-permute-done((bf16[8,136,128]{2,1,0:T(8,128)(2,1)S(1)}, bf16[8,136,128]{2,1,0:T(8,128)(2,1)S(1)}, u32[]{:S(2)}, u32[]{:S(2)}) %collective-permute-start.9) | collective-permute-done | bytes 278560 | tf_op jit(solution)/shard_map/ppermute | solution.py:98
  47.4 1.2 %collective-permute-start.10 = (bf16[2,136,128]{2,1,0:T(8,128)(2,1)S(1)}, bf16[2,136,128]{2,1,0:T(8,128)(2,1)S(1)}, u32[]{:S(2)}, u32[]{:S(2)}) collective-permute-start(bf16[2,136,128]{2,1,0:T(8,128)(2,1)S(1)} %get-tuple-element.54), channel_id=1, source_target_pairs={{0,20},{2,22},{4,16},{6,18},{8,28},{10,30},{12,24},{14,26},{16,4},... | collective-permute-start | bytes 208904 | tf_op jit(solution)/shard_map/ppermute | solution.py:106
  48.5 1.4 %collective-permute-start.11 = (bf16[2,136,128]{2,1,0:T(8,128)(2,1)S(1)}, bf16[2,136,128]{2,1,0:T(8,128)(2,1)S(1)}, u32[]{:S(2)}, u32[]{:S(2)}) collective-permute-start(bf16[2,136,128]{2,1,0:T(8,128)(2,1)S(1)} %get-tuple-element.55), channel_id=1, source_target_pairs={{0,16},{2,18},{4,20},{6,22},{8,24},{10,26},{12,28},{14,30},{16,0},... | collective-permute-start | bytes 208904 | tf_op jit(solution)/shard_map/ppermute | solution.py:106
  49.9 2.0 %collective-permute-start.12 = (bf16[2,136,128]{2,1,0:T(8,128)(2,1)S(1)}, bf16[2,136,128]{2,1,0:T(8,128)(2,1)S(1)}, u32[]{:S(2)}, u32[]{:S(2)}) collective-permute-start(bf16[2,136,128]{2,1,0:T(8,128)(2,1)S(1)} %get-tuple-element.56), channel_id=1, source_target_pairs={{0,12},{2,14},{4,8},{6,10},{8,4},{10,6},{12,0},{14,2},{16,28},{18,... | collective-permute-start | bytes 208904 | tf_op jit(solution)/shard_map/ppermute | solution.py:106
  51.9 2.4 %collective-permute-start.13 = (bf16[2,136,128]{2,1,0:T(8,128)(2,1)S(1)}, bf16[2,136,128]{2,1,0:T(8,128)(2,1)S(1)}, u32[]{:S(2)}, u32[]{:S(2)}) collective-permute-start(bf16[2,136,128]{2,1,0:T(8,128)(2,1)S(1)} %get-tuple-element.57), channel_id=1, source_target_pairs={{0,28},{2,30},{4,24},{6,26},{8,20},{10,22},{12,16},{14,18},{16,12}... | collective-permute-start | bytes 208904 | tf_op jit(solution)/shard_map/ppermute | solution.py:106
  54.9 1.9 %collective-permute-start.15 = (bf16[2,136,128]{2,1,0:T(8,128)(2,1)S(1)}, bf16[2,136,128]{2,1,0:T(8,128)(2,1)S(1)}, u32[]{:S(2)}, u32[]{:S(2)}) collective-permute-start(bf16[2,136,128]{2,1,0:T(8,128)(2,1)S(1)} %get-tuple-element.59), channel_id=1, source_target_pairs={{0,8},{2,10},{4,12},{6,14},{8,0},{10,2},{12,4},{14,6},{16,24},{18,... | collective-permute-start | bytes 208904 | tf_op jit(solution)/shard_map/ppermute | solution.py:106
  56.9 1.5 %collective-permute-done.11.refs_2_ = bf16[2,136,128]{2,1,0:T(8,128)(2,1)S(1)} collective-permute-done((bf16[2,136,128]{2,1,0:T(8,128)(2,1)S(1)}, bf16[2,136,128]{2,1,0:T(8,128)(2,1)S(1)}, u32[]{:S(2)}, u32[]{:S(2)}) %collective-permute-start.11) | collective-permute-done | bytes 69664 | tf_op jit(solution)/shard_map/ppermute | solution.py:106
  58.4 2.3 %collective-permute-start.16 = (bf16[2,136,128]{2,1,0:T(8,128)(2,1)S(1)}, bf16[2,136,128]{2,1,0:T(8,128)(2,1)S(1)}, u32[]{:S(2)}, u32[]{:S(2)}) collective-permute-start(bf16[2,136,128]{2,1,0:T(8,128)(2,1)S(1)} %get-tuple-element.60), channel_id=1, source_target_pairs={{0,24},{2,26},{4,28},{6,30},{8,16},{10,18},{12,20},{14,22},{16,8},... | collective-permute-start | bytes 208904 | tf_op jit(solution)/shard_map/ppermute | solution.py:106
  60.7 1.2 %shard_map.116 = (bf16[128,2048]{1,0:T(8,128)(2,1)S(1)}, bf16[128,2048]{1,0:T(8,128)(2,1)S(1)}) custom-call(bf16[128,2048]{1,0:T(8,128)(2,1)} %query_hbm.3, bf16[128,2048]{1,0:T(8,128)(2,1)} %key_hbm.3), custom_call_target="tpu_custom_call" | custom-call | tf_op jit(solution)/shard_map/pallas_call | solution.py:398
  61.9 2.6 %collective-permute-done.16.refs_7_ = bf16[2,136,128]{2,1,0:T(8,128)(2,1)S(1)} collective-permute-done((bf16[2,136,128]{2,1,0:T(8,128)(2,1)S(1)}, bf16[2,136,128]{2,1,0:T(8,128)(2,1)S(1)}, u32[]{:S(2)}, u32[]{:S(2)}) %collective-permute-start.16) | collective-permute-done | bytes 69664 | tf_op jit(solution)/shard_map/ppermute | solution.py:106
  64.5 2.9 %shard_map.121 = (bf16[128,2048]{1,0:T(8,128)(2,1)}, bf16[128,2048]{1,0:T(8,128)(2,1)}, f32[128,128]{1,0:T(8,128)}) custom-call(s32[1]{0:T(128)} %bitcast.ctx_ref, s32[1,2048]{1,0:T(1,128)S(1)} %get-tuple-element.32.rank_ref, bf16[128,2048]{1,0:T(8,128)(2,1)S(1)} %get-tuple-element.34.conv_ref, f32[1,2048]{1,0:T(1,128)S(1)} %get-tuple-element.36.skip_ref, ...), custom_call_target="tpu_custom_call" | custom-call | tf_op jit(solution)/shard_map/pallas_call | solution.py:401
  (23 shorter events, 4.7 us)
Async XLA Ops:
  0.6 17.2 %collective-permute-start = (bf16[128,2048]{1,0:T(8,128)(2,1)}, bf16[128,2048]{1,0:T(8,128)(2,1)S(1)}, u32[]{:S(2)}, u32[]{:S(2)}) collective-permute-start(bf16[128,2048]{1,0:T(8,128)(2,1)} %grad_hbm.1), channel_id=1, source_target_pairs={{0,1},{1,0},{2,3},{3,2},{4,5},{5,4},{6,7},{7,6},{8,9},{9,8},{10,11... | collective-permute-start | bytes 1572872 | tf_op jit(solution)/shard_map/ppermute | solution.py:327
  7.5 33.5 %all-to-all-start = ((bf16[16,128,128]{2,1,0:T(8,128)(2,1)}), bf16[16,128,128]{2,1,0:T(8,128)(2,1)S(1)}, u32[]{:S(2)}, u32[]{:S(2)}) async-start(bf16[16,128,128]{2,1,0:T(8,128)(2,1)} %get-tuple-element.35), calls=%async_computation | async-start | bytes 1048576 | tf_op jit(solution)/shard_map/all_to_all | solution.py:339
  23.0 1.6 %collective-permute-start.1 = (bf16[8,128,128]{2,1,0:T(8,128)(2,1)S(1)}, bf16[8,128,128]{2,1,0:T(8,128)(2,1)S(1)}, u32[]{:S(2)}, u32[]{:S(2)}) collective-permute-start(bf16[8,128,128]{2,1,0:T(8,128)(2,1)S(1)} %get-tuple-element.42), channel_id=1, source_target_pairs={{0,2},{2,0},{4,6},{6,4},{8,10},{10,8},{12,14},{14,12},{16,18},{18,... | collective-permute-start | bytes 786440 | tf_op jit(solution)/shard_map/ppermute | solution.py:98
  24.7 9.6 %collective-permute-start.2 = (bf16[2,128,128]{2,1,0:T(8,128)(2,1)S(1)}, bf16[2,128,128]{2,1,0:T(8,128)(2,1)S(1)}, u32[]{:S(2)}, u32[]{:S(2)}) collective-permute-start(bf16[2,128,128]{2,1,0:T(8,128)(2,1)S(1)} %get-tuple-element.44), channel_id=1, source_target_pairs={{0,20},{2,22},{4,16},{6,18},{8,28},{10,30},{12,24},{14,26},{16,4},... | collective-permute-start | bytes 196616 | tf_op jit(solution)/shard_map/ppermute | solution.py:106
  28.4 8.2 %collective-permute-start.3 = (bf16[2,128,128]{2,1,0:T(8,128)(2,1)S(1)}, bf16[2,128,128]{2,1,0:T(8,128)(2,1)S(1)}, u32[]{:S(2)}, u32[]{:S(2)}) collective-permute-start(bf16[2,128,128]{2,1,0:T(8,128)(2,1)S(1)} %get-tuple-element.45), channel_id=1, source_target_pairs={{0,16},{2,18},{4,20},{6,22},{8,24},{10,26},{12,28},{14,30},{16,0},... | collective-permute-start | bytes 196616 | tf_op jit(solution)/shard_map/ppermute | solution.py:106
  29.0 13.1 %collective-permute-start.4 = (bf16[2,128,128]{2,1,0:T(8,128)(2,1)S(1)}, bf16[2,128,128]{2,1,0:T(8,128)(2,1)S(1)}, u32[]{:S(2)}, u32[]{:S(2)}) collective-permute-start(bf16[2,128,128]{2,1,0:T(8,128)(2,1)S(1)} %get-tuple-element.46), channel_id=1, source_target_pairs={{0,12},{2,14},{4,8},{6,10},{8,4},{10,6},{12,0},{14,2},{16,28},{18,... | collective-permute-start | bytes 196616 | tf_op jit(solution)/shard_map/ppermute | solution.py:106
  30.5 11.6 %collective-permute-start.5 = (bf16[2,128,128]{2,1,0:T(8,128)(2,1)S(1)}, bf16[2,128,128]{2,1,0:T(8,128)(2,1)S(1)}, u32[]{:S(2)}, u32[]{:S(2)}) collective-permute-start(bf16[2,128,128]{2,1,0:T(8,128)(2,1)S(1)} %get-tuple-element.47), channel_id=1, source_target_pairs={{0,28},{2,30},{4,24},{6,26},{8,20},{10,22},{12,16},{14,18},{16,12}... | collective-permute-start | bytes 196616 | tf_op jit(solution)/shard_map/ppermute | solution.py:106
  33.7 8.4 %collective-permute-start.6 = (bf16[2,128,128]{2,1,0:T(8,128)(2,1)S(1)}, bf16[2,128,128]{2,1,0:T(8,128)(2,1)S(1)}, u32[]{:S(2)}, u32[]{:S(2)}) collective-permute-start(bf16[2,128,128]{2,1,0:T(8,128)(2,1)S(1)} %get-tuple-element.48), channel_id=1, source_target_pairs={{0,4},{2,6},{4,0},{6,2},{8,12},{10,14},{12,8},{14,10},{16,20},{18,... | collective-permute-start | bytes 196616 | tf_op jit(solution)/shard_map/ppermute | solution.py:106
  34.3 7.8 %collective-permute-start.7 = (bf16[2,128,128]{2,1,0:T(8,128)(2,1)S(1)}, bf16[2,128,128]{2,1,0:T(8,128)(2,1)S(1)}, u32[]{:S(2)}, u32[]{:S(2)}) collective-permute-start(bf16[2,128,128]{2,1,0:T(8,128)(2,1)S(1)} %get-tuple-element.49), channel_id=1, source_target_pairs={{0,8},{2,10},{4,12},{6,14},{8,0},{10,2},{12,4},{14,6},{16,24},{18,... | collective-permute-start | bytes 196616 | tf_op jit(solution)/shard_map/ppermute | solution.py:106
  36.6 6.1 %collective-permute-start.8 = (bf16[2,128,128]{2,1,0:T(8,128)(2,1)S(1)}, bf16[2,128,128]{2,1,0:T(8,128)(2,1)S(1)}, u32[]{:S(2)}, u32[]{:S(2)}) collective-permute-start(bf16[2,128,128]{2,1,0:T(8,128)(2,1)S(1)} %get-tuple-element.50), channel_id=1, source_target_pairs={{0,24},{2,26},{4,28},{6,30},{8,16},{10,18},{12,20},{14,22},{16,8},... | collective-permute-start | bytes 196616 | tf_op jit(solution)/shard_map/ppermute | solution.py:106
  45.7 1.6 %collective-permute-start.9 = (bf16[8,136,128]{2,1,0:T(8,128)(2,1)S(1)}, bf16[8,136,128]{2,1,0:T(8,128)(2,1)S(1)}, u32[]{:S(2)}, u32[]{:S(2)}) collective-permute-start(bf16[8,136,128]{2,1,0:T(8,128)(2,1)S(1)} %get-tuple-element.52), channel_id=1, source_target_pairs={{0,2},{2,0},{4,6},{6,4},{8,10},{10,8},{12,14},{14,12},{16,18},{18,... | collective-permute-start | bytes 835592 | tf_op jit(solution)/shard_map/ppermute | solution.py:98
  47.4 7.6 %collective-permute-start.10 = (bf16[2,136,128]{2,1,0:T(8,128)(2,1)S(1)}, bf16[2,136,128]{2,1,0:T(8,128)(2,1)S(1)}, u32[]{:S(2)}, u32[]{:S(2)}) collective-permute-start(bf16[2,136,128]{2,1,0:T(8,128)(2,1)S(1)} %get-tuple-element.54), channel_id=1, source_target_pairs={{0,20},{2,22},{4,16},{6,18},{8,28},{10,30},{12,24},{14,26},{16,4},... | collective-permute-start | bytes 208904 | tf_op jit(solution)/shard_map/ppermute | solution.py:106
  48.5 9.9 %collective-permute-start.11 = (bf16[2,136,128]{2,1,0:T(8,128)(2,1)S(1)}, bf16[2,136,128]{2,1,0:T(8,128)(2,1)S(1)}, u32[]{:S(2)}, u32[]{:S(2)}) collective-permute-start(bf16[2,136,128]{2,1,0:T(8,128)(2,1)S(1)} %get-tuple-element.55), channel_id=1, source_target_pairs={{0,16},{2,18},{4,20},{6,22},{8,24},{10,26},{12,28},{14,30},{16,0},... | collective-permute-start | bytes 208904 | tf_op jit(solution)/shard_map/ppermute | solution.py:106
  49.9 12.0 %collective-permute-start.12 = (bf16[2,136,128]{2,1,0:T(8,128)(2,1)S(1)}, bf16[2,136,128]{2,1,0:T(8,128)(2,1)S(1)}, u32[]{:S(2)}, u32[]{:S(2)}) collective-permute-start(bf16[2,136,128]{2,1,0:T(8,128)(2,1)S(1)} %get-tuple-element.56), channel_id=1, source_target_pairs={{0,12},{2,14},{4,8},{6,10},{8,4},{10,6},{12,0},{14,2},{16,28},{18,... | collective-permute-start | bytes 208904 | tf_op jit(solution)/shard_map/ppermute | solution.py:106
  51.9 10.0 %collective-permute-start.13 = (bf16[2,136,128]{2,1,0:T(8,128)(2,1)S(1)}, bf16[2,136,128]{2,1,0:T(8,128)(2,1)S(1)}, u32[]{:S(2)}, u32[]{:S(2)}) collective-permute-start(bf16[2,136,128]{2,1,0:T(8,128)(2,1)S(1)} %get-tuple-element.57), channel_id=1, source_target_pairs={{0,28},{2,30},{4,24},{6,26},{8,20},{10,22},{12,16},{14,18},{16,12}... | collective-permute-start | bytes 208904 | tf_op jit(solution)/shard_map/ppermute | solution.py:106
  54.3 7.6 %collective-permute-start.14 = (bf16[2,136,128]{2,1,0:T(8,128)(2,1)S(1)}, bf16[2,136,128]{2,1,0:T(8,128)(2,1)S(1)}, u32[]{:S(2)}, u32[]{:S(2)}) collective-permute-start(bf16[2,136,128]{2,1,0:T(8,128)(2,1)S(1)} %get-tuple-element.58), channel_id=1, source_target_pairs={{0,4},{2,6},{4,0},{6,2},{8,12},{10,14},{12,8},{14,10},{16,20},{18,... | collective-permute-start | bytes 208904 | tf_op jit(solution)/shard_map/ppermute | solution.py:106
  54.9 7.0 %collective-permute-start.15 = (bf16[2,136,128]{2,1,0:T(8,128)(2,1)S(1)}, bf16[2,136,128]{2,1,0:T(8,128)(2,1)S(1)}, u32[]{:S(2)}, u32[]{:S(2)}) collective-permute-start(bf16[2,136,128]{2,1,0:T(8,128)(2,1)S(1)} %get-tuple-element.59), channel_id=1, source_target_pairs={{0,8},{2,10},{4,12},{6,14},{8,0},{10,2},{12,4},{14,6},{16,24},{18,... | collective-permute-start | bytes 208904 | tf_op jit(solution)/shard_map/ppermute | solution.py:106
  58.4 6.1 %collective-permute-start.16 = (bf16[2,136,128]{2,1,0:T(8,128)(2,1)S(1)}, bf16[2,136,128]{2,1,0:T(8,128)(2,1)S(1)}, u32[]{:S(2)}, u32[]{:S(2)}) collective-permute-start(bf16[2,136,128]{2,1,0:T(8,128)(2,1)S(1)} %get-tuple-element.60), channel_id=1, source_target_pairs={{0,24},{2,26},{4,28},{6,30},{8,16},{10,18},{12,20},{14,22},{16,8},... | collective-permute-start | bytes 208904 | tf_op jit(solution)/shard_map/ppermute | solution.py:106

commit v6 on v5

--- a/solution.py
+++ b/solution.py
@@ -13,6 +13,7 @@
 NT = (((1,), (1,)), ((), ()))
 NN = (((1,), (0,)), ((), ()))
 LANES = 128
+SWAPS = 2
 EXTRA = 8
 VMEM = pl.BlockSpec(memory_space=pltpu.VMEM)
 SMEM = pl.BlockSpec(memory_space=pltpu.SMEM)
@@ -108,8 +109,31 @@
     return out
 
 
-def gate_kernel(
-    group_hbm, query_hbm, key_hbm, grad_hbm, out_ref, rank_ref, grad_ref, group_ref, query_ref, key_ref, column_ref, sem, *, groups, per_group
+def stream_weights(first, weight_hbm, weight_ref, sem):
+    count = sem.shape[0]
+    width = weight_ref.shape[1] // count
+    return [
+        pltpu.make_async_copy(
+            weight_hbm.at[:, pl.ds(pl.multiple_of(first + j * width, LANES), width)],
+            weight_ref.at[:, pl.ds(j * width, width)],
+            sem.at[j],
+        )
+        for j in range(count)
+    ]
+
+
+def product(copies, grad_ref, weight_ref, out_ref, fresh):
+    width = weight_ref.shape[1] // len(copies)
+    for j, copy in enumerate(copies):
+        copy.wait()
+        cols = slice(j * width, (j + 1) * width)
+        part = dot(grad_ref[:, cols], weight_ref[:, cols], NT)
+        out_ref[...] = part if fresh and j == 0 else out_ref[...] + part
+
+
+def begin_kernel(
+    first_ref, group_hbm, query_hbm, key_hbm, grad_hbm, weight_hbm, out_hbm, rank_ref, acc_ref,
+    group_ref, query_ref, key_ref, grad_ref, weight_ref, out_ref, column_ref, sem, weight_sem, store_sem, *, groups, per_group
 ):
     loads = [
         pltpu.make_async_copy(group_hbm, group_ref, sem.at[0]),
@@ -133,49 +157,30 @@
         rank_ref[:, b * LANES : (b + 1) * LANES] = here * per_group + place.astype(I32)
         base = base + jnp.sum(member, axis=1, keepdims=True)
     rank_column(rank_ref[...], column_ref)
-    for load in loads[1:3]:
+    for load in loads[1:]:
         load.wait()
+    copies = stream_weights(first_ref[0], weight_hbm, weight_ref, weight_sem)
+    for copy in copies:
+        copy.start()
     gated = (query_ref[...].astype(F32) * key_ref[...].astype(F32)).astype(BF16)
     rows = out_ref.shape[1]
 
-    def store(i, block):
+    def save(i, block):
         out_ref[i] = block
 
-    permute(gated, column_ref, range(0, channels, rows), rows, store)
-    loads[3].wait()
-
-
-def stream_weights(half, weight_hbm, weight_ref, sem):
-    _, feats = weight_ref.shape
-    count = sem.shape[0]
-    width = feats // count
-    copies = [
-        pltpu.make_async_copy(
-            weight_hbm.at[:, pl.ds(pl.multiple_of(half * feats + j * width, width), width)],
-            weight_ref.at[:, pl.ds(j * width, width)],
-            sem.at[j],
-        )
-        for j in range(count)
-    ]
+    permute(gated, column_ref, range(0, channels, rows), rows, save)
+    store = pltpu.make_async_copy(out_ref, out_hbm, store_sem)
+    store.start()
+    product(copies, grad_ref, weight_ref, acc_ref, True)
+    store.wait()
+
+
+def more_kernel(first_ref, grad_ref, acc_ref, weight_hbm, out_ref, weight_ref, sem):
+    copies = stream_weights(first_ref[0], weight_hbm, weight_ref, sem)
     for copy in copies:
         copy.start()
-    return copies, width
-
-
-def product(copies, width, grad_ref, weight_ref, out_ref, fresh):
-    for j, copy in enumerate(copies):
-        copy.wait()
-        cols = slice(j * width, (j + 1) * width)
-        part = dot(grad_ref[:, cols], weight_ref[:, cols], NT)
-        out_ref[...] = part if fresh and j == 0 else out_ref[...] + part
-
-
-def partial_kernel(half_ref, grad_ref, weight_hbm, *refs):
-    *acc, out_ref, weight_ref, sem = refs
-    copies, width = stream_weights(half_ref[0], weight_hbm, weight_ref, sem)
-    if acc:
-        out_ref[...] = acc[0][...]
-    product(copies, width, grad_ref, weight_ref, out_ref, not acc)
+    out_ref[...] = acc_ref[...]
+    product(copies, grad_ref, weight_ref, out_ref, False)
 
 
 def pair_blocks(ctx, place, by_token, column_ref, out_ref):
@@ -188,14 +193,16 @@
 
 
 def last_kernel(
-    half_ref, ctx_ref, rank_ref, grad_ref, acc_ref, weight_hbm, value_hbm, out_ref, conv_ref, total_ref, weight_ref, value_ref, column_ref, sem, value_sem
+    first_ref, ctx_ref, rank_ref, grad_ref, acc_ref, weight_hbm, value_hbm, out_ref, conv_ref, total_ref, weight_ref, value_ref, column_ref, sem, value_sem
 ):
     load = pltpu.make_async_copy(value_hbm, value_ref, value_sem)
-    copies, width = stream_weights(half_ref[0], weight_hbm, weight_ref, sem)
+    copies = stream_weights(first_ref[0], weight_hbm, weight_ref, sem)
+    for copy in copies:
+        copy.start()
     load.start()
     rank_column(rank_ref[...], column_ref)
     total_ref[...] = acc_ref[...]
-    product(copies, width, grad_ref, weight_ref, total_ref, False)
+    product(copies, grad_ref, weight_ref, total_ref, False)
     load.wait()
     conv_ref[...] = (total_ref[...] * value_ref[...].astype(F32)).astype(BF16)
     ctx = ctx_ref[0]
@@ -319,51 +326,53 @@
     sub = channels // spans
     sub_groups = sub // per_group
     lags = (spans // 2 + 1) * tokens
-    feats = grad_out.shape[1]
     dma = pltpu.SemaphoreType.DMA
     wide = pltpu.VMEM((tokens, channels), BF16)
     column = pltpu.VMEM((channels, LANES), I32)
 
-    arrived = [lax.ppermute(grad_out, "head", [(i, (i + r) % heads) for i in range(heads)]) for r in range(1, heads)]
-
-    gate_sorted, rank, grad_here = call(
-        functools.partial(gate_kernel, groups=groups, per_group=per_group),
+    feats = grad_out.shape[1]
+    width = feats // SWAPS
+    arrived = []
+    for r in range(1, heads):
+        for q in range(SWAPS):
+            piece = grad_out[:, q * width : (q + 1) * width]
+            moved = lax.ppermute(piece, "head", [(i, (i + r) % heads) for i in range(heads)])
+            arrived.append((((head + heads - r) % heads) * feats + q * width, moved))
+
+    def weights(size):
+        return [pltpu.VMEM((channels, size), BF16)], dma((max(1, size // (2 * LANES)),))
+
+    scratch, sems = weights(feats)
+    gate_sorted, rank, acc = call(
+        functools.partial(begin_kernel, groups=groups, per_group=per_group),
         (
-            pltpu.VMEM((spans, sub, tokens), BF16),
+            jax.ShapeDtypeStruct((spans, sub, tokens), BF16),
             pltpu.VMEM((1, channels), I32),
-            pltpu.VMEM((tokens, feats), BF16),
+            pltpu.VMEM((tokens, channels), F32),
         ),
-        [ANY, ANY, ANY, ANY],
-        [pltpu.VMEM((1, channels), I32), wide, wide, column, dma((4,))],
-    )(group_of.reshape(1, channels), query_proj, key_proj, grad_out)
+        [SMEM, ANY, ANY, ANY, ANY, ANY],
+        [pltpu.VMEM((1, channels), I32), wide, wide, pltpu.VMEM((tokens, feats), BF16)]
+        + scratch
+        + [pltpu.VMEM((spans, sub, tokens), BF16), column, dma((4,)), sems, dma],
+        (ANY, VMEM, VMEM),
+    )((head * feats).reshape(1), group_of.reshape(1, channels), query_proj, key_proj, grad_out, out_proj)
+    rank, acc = on_chip(rank), on_chip(acc)
     gate_moved = lax.all_to_all(gate_sorted, "ctx", 0, 0)
 
-    parts = min(8, feats // LANES)
-    acc = None
-    for r, grad in enumerate([grad_here] + arrived):
-        source = ((head + heads - r) % heads).reshape(1)
-        if r < heads - 1:
+    scratch, sems = weights(width)
+    for p, (first, grad) in enumerate(arrived):
+        if p < len(arrived) - 1:
             acc = call(
-                partial_kernel,
-                pltpu.VMEM((tokens, channels), F32),
-                [SMEM, VMEM, ANY] + ([] if acc is None else [VMEM]),
-                [pltpu.VMEM((channels, feats), BF16), dma((parts,))],
-            )(source, on_chip(grad), out_proj, *([] if acc is None else [acc]))
+                more_kernel, pltpu.VMEM((tokens, channels), F32), [SMEM, VMEM, VMEM, ANY], scratch + [sems]
+            )(first.reshape(1), on_chip(grad), acc, out_proj)
             acc = on_chip(acc)
         else:
             conv_sorted, conv_grad = call(
                 last_kernel,
                 (pltpu.VMEM((spans // 2, sub, tokens), BF16), pltpu.VMEM((tokens, channels), BF16)),
                 [SMEM, SMEM, VMEM, VMEM, VMEM, ANY, ANY],
-                [
-                    pltpu.VMEM((tokens, channels), F32),
-                    pltpu.VMEM((channels, feats), BF16),
-                    wide,
-                    column,
-                    dma((parts,)),
-                    dma,
-                ],
-            )(source, ctx, on_chip(rank), on_chip(grad), acc, out_proj, value_proj)
+                [pltpu.VMEM((tokens, channels), F32)] + scratch + [wide, column, sems, dma],
+            )(first.reshape(1), ctx, rank, on_chip(grad), acc, out_proj, value_proj)
 
     def conv_mine():
         return call(

time: 67.9 us -> 77.1 us (1.14)
  waiting for transfers between devices: 8.27 us -> 19.4 us
  starting transfers between devices: 34.5 us -> 33 us
    ppermute x1 -> x2, waiting for transfers between devices: 0.01 us -> 9.32 us  [per_device(): lax.ppermute(piece, 'head', [(i, (i + r) % heads) for i in range(heads)])]
    ppermute x14, starting transfers between devices: 25 us -> 23.4 us  [exchange(): lax.ppermute(on_chip(pack), 'ctx', [(i, i ^ 2 * e) for i in range(count)])]
    pallas_call x1, Pallas kernels: 5.2 us -> 3.68 us  [per_device(): call(last_kernel, (pltpu.VMEM((spans // 2, sub, tokens), BF16), pltpu.VME...]
    all_to_all x1, starting transfers between devices: 5.93 us -> 7.42 us  [per_device(): gate_moved = lax.all_to_all(gate_sorted, 'ctx', 0, 0)]
    ppermute x14, waiting for transfers between devices: 6.44 us -> 7.93 us  [exchange(): lax.ppermute(on_chip(pack), 'ctx', [(i, i ^ 2 * e) for i in range(count)])]
    ppermute x1 -> x2, starting transfers between devices: 3.06 us -> 2.09 us  [per_device(): lax.ppermute(piece, 'head', [(i, (i + r) % heads) for i in range(heads)])]
    pallas_call x2, Pallas kernels: 8.15 us -> 9.07 us  [the longest x1 6.2 us: per_device(): call(functools.partial(begin_kernel, groups=groups, per_group=per_group),...]
  transfers between devices with their start and end apart: 18 -> 19, of which waited for: 6 -> 8; matrix products, arithmetic and copies ran while one was open for 2% -> 2% of each run, Pallas kernels for 24% -> 13%
where the time goes in v6:
time: 77.1 us; the launch traced here: 76.7 us
  starting transfers between devices  33 us (43%)
  Pallas kernels  21.9 us (28%)
  waiting for transfers between devices  19.4 us (25%)
  other arithmetic  1.34 us (2%)
  between operations  0.98 us (1%)
    ppermute x14, starting transfers between devices, exchange(): lax.ppermute(on_chip(pack), 'ctx', [(i, i ^ 2 * e) for i in range(count)])  23.4 us
    ppermute x2, waiting for transfers between devices, per_device(): lax.ppermute(piece, 'head', [(i, (i + r) % heads) for i in range(heads)])  9.32 us
    ppermute x14, waiting for transfers between devices, exchange(): lax.ppermute(on_chip(pack), 'ctx', [(i, i ^ 2 * e) for i in range(count)])  7.93 us
    all_to_all x1, starting transfers between devices, per_device(): gate_moved = lax.all_to_all(gate_sorted, 'ctx', 0, 0)  7.42 us
    pallas_call x1, Pallas kernels, per_device(): call(functools.partial(begin_kernel, groups=groups, per_group=per_group),...  6.2 us
    pallas_call x1, Pallas kernels, per_device(): call(last_kernel, (pltpu.VMEM((spans // 2, sub, tokens), BF16), pltpu.VME...  3.68 us
    pallas_call x1, Pallas kernels, per_device(): call(functools.partial(conv_kernel, per_group=per_group), (pltpu.VMEM((sp...  2.97 us
    pallas_call x1, Pallas kernels, per_device(): call(functools.partial(gates_kernel, sub_groups=sub_groups), (jax.ShapeDt...  2.88 us
  transfers between devices with their start and end apart: 19, of which 8 were waited for; matrix products, arithmetic and copies ran while one was open for 2% of the time, Pallas kernels for 13%

profile of v6, /device:TPU:0, one launch (start us, length us, event | category | flops | bytes accessed | tf_op | source)
XLA Modules:
  0.0 76.7 jit_solution(16608920354149190272)
XLA Ops:
  0.6 6.2 %shard_map.112 = (bf16[16,128,128]{2,1,0:T(8,128)(2,1)}, s32[1,2048]{1,0:T(1,128)S(1)}, f32[128,2048]{1,0:T(8,128)S(1)}) custom-call(s32[1]{0:T(128)} %bitcast.1.first_ref, s32[1,2048]{1,0:T(1,128)} %bitcast.6, bf16[128,2048]{1,0:T(8,128)(2,1)} %query_hbm.3, bf16[128,2048]{1,0:T(8,128)(2,1)} %key_hbm.3, bf16[128,2048]{1,0:T(8,128)(2,1)} %grad_hbm.1, ...), custom_call_target="tpu_custom_call" | custom-call | tf_op jit(solution)/shard_map/pallas_call | solution.py:346
  6.9 7.4 %all-to-all-start = ((bf16[16,128,128]{2,1,0:T(8,128)(2,1)}), bf16[16,128,128]{2,1,0:T(8,128)(2,1)S(1)}, u32[]{:S(2)}, u32[]{:S(2)}) async-start(bf16[16,128,128]{2,1,0:T(8,128)(2,1)} %get-tuple-element.35), calls=%async_computation | async-start | bytes 1048576 | tf_op jit(solution)/shard_map/all_to_all | solution.py:360
  14.3 1.6 %collective-permute-start.1 = (bf16[128,1024]{1,0:T(8,128)(2,1)S(1)}, bf16[128,1024]{1,0:T(8,128)(2,1)S(1)}, u32[]{:S(2)}, u32[]{:S(2)}) collective-permute-start(bf16[128,1024]{1,0:T(8,128)(2,1)S(1)} %get-tuple-element.61), channel_id=1, source_target_pairs={{0,1},{1,0},{2,3},{3,2},{4,5},{5,4},{6,7},{7,6},{8,9},{9,8},{10,11... | collective-permute-start | bytes 786440 | tf_op jit(solution)/shard_map/ppermute | solution.py:339
  16.4 7.2 %collective-permute-done.1.grad_ref = bf16[128,1024]{1,0:T(8,128)(2,1)S(1)} collective-permute-done((bf16[128,1024]{1,0:T(8,128)(2,1)S(1)}, bf16[128,1024]{1,0:T(8,128)(2,1)S(1)}, u32[]{:S(2)}, u32[]{:S(2)}) %collective-permute-start.1) | collective-permute-done | bytes 262176 | tf_op jit(solution)/shard_map/ppermute | solution.py:339
  23.6 2.9 %shard_map.113.acc_ref = f32[128,2048]{1,0:T(8,128)S(1)} custom-call(s32[1]{0:T(128)} %bitcast.4.first_ref, bf16[128,1024]{1,0:T(8,128)(2,1)S(1)} %collective-permute-done.1.grad_ref, f32[128,2048]{1,0:T(8,128)S(1)} %get-tuple-element.33.acc_ref, bf16[2048,4096]{1,0:T(8,128)(2,1)} %weight_hbm.5), custom_call_target="tpu_custom_call" | custom-call | tf_op jit(solution)/shard_map/pallas_call | solution.py:365
  26.5 2.2 %collective-permute-done.grad_ref = bf16[128,1024]{1,0:T(8,128)(2,1)S(1)} collective-permute-done((bf16[128,1024]{1,0:T(8,128)(2,1)S(1)}, bf16[128,1024]{1,0:T(8,128)(2,1)S(1)}, u32[]{:S(2)}, u32[]{:S(2)}) %collective-permute-start) | collective-permute-done | bytes 262176 | tf_op jit(solution)/shard_map/ppermute | solution.py:339
  28.6 3.7 %shard_map.114 = (bf16[8,128,128]{2,1,0:T(8,128)(2,1)S(1)}, bf16[128,2048]{1,0:T(8,128)(2,1)S(1)}) custom-call(s32[1]{0:T(128)} %bitcast.3.first_ref, s32[1]{0:T(128)} %bitcast.ctx_ref, s32[1,2048]{1,0:T(1,128)S(1)} %get-tuple-element.32.rank_ref, bf16[128,1024]{1,0:T(8,128)(2,1)S(1)} %collective-permute-done.grad_ref, f32[128,2048]{1,0:T(8,128)S(1)} %shard_map.113.acc_ref, ...), custom_call_target="tpu_custom_call" | custom-call | tf_op jit(solution)/shard_map/pallas_call | solution.py:370
  34.0 3.5 %collective-permute-start.3 = (bf16[2,128,128]{2,1,0:T(8,128)(2,1)S(1)}, bf16[2,128,128]{2,1,0:T(8,128)(2,1)S(1)}, u32[]{:S(2)}, u32[]{:S(2)}) collective-permute-start(bf16[2,128,128]{2,1,0:T(8,128)(2,1)S(1)} %get-tuple-element.44), channel_id=1, source_target_pairs={{0,20},{2,22},{4,16},{6,18},{8,28},{10,30},{12,24},{14,26},{16,4},... | collective-permute-start | bytes 196616 | tf_op jit(solution)/shard_map/ppermute | solution.py:107
  38.0 1.5 %collective-permute-start.5 = (bf16[2,128,128]{2,1,0:T(8,128)(2,1)S(1)}, bf16[2,128,128]{2,1,0:T(8,128)(2,1)S(1)}, u32[]{:S(2)}, u32[]{:S(2)}) collective-permute-start(bf16[2,128,128]{2,1,0:T(8,128)(2,1)S(1)} %get-tuple-element.46), channel_id=1, source_target_pairs={{0,12},{2,14},{4,8},{6,10},{8,4},{10,6},{12,0},{14,2},{16,28},{18,... | collective-permute-start | bytes 196616 | tf_op jit(solution)/shard_map/ppermute | solution.py:107
  39.5 3.3 %collective-permute-start.6 = (bf16[2,128,128]{2,1,0:T(8,128)(2,1)S(1)}, bf16[2,128,128]{2,1,0:T(8,128)(2,1)S(1)}, u32[]{:S(2)}, u32[]{:S(2)}) collective-permute-start(bf16[2,128,128]{2,1,0:T(8,128)(2,1)S(1)} %get-tuple-element.47), channel_id=1, source_target_pairs={{0,28},{2,30},{4,24},{6,26},{8,20},{10,22},{12,16},{14,18},{16,12}... | collective-permute-start | bytes 196616 | tf_op jit(solution)/shard_map/ppermute | solution.py:107
  43.9 1.8 %collective-permute-done.4.refs_2_ = bf16[2,128,128]{2,1,0:T(8,128)(2,1)S(1)} collective-permute-done((bf16[2,128,128]{2,1,0:T(8,128)(2,1)S(1)}, bf16[2,128,128]{2,1,0:T(8,128)(2,1)S(1)}, u32[]{:S(2)}, u32[]{:S(2)}) %collective-permute-start.4) | collective-permute-done | bytes 65568 | tf_op jit(solution)/shard_map/ppermute | solution.py:107
  45.7 3.0 %collective-permute-start.9 = (bf16[2,128,128]{2,1,0:T(8,128)(2,1)S(1)}, bf16[2,128,128]{2,1,0:T(8,128)(2,1)S(1)}, u32[]{:S(2)}, u32[]{:S(2)}) collective-permute-start(bf16[2,128,128]{2,1,0:T(8,128)(2,1)S(1)} %get-tuple-element.50), channel_id=1, source_target_pairs={{0,24},{2,26},{4,28},{6,30},{8,16},{10,18},{12,20},{14,22},{16,8},... | collective-permute-start | bytes 196616 | tf_op jit(solution)/shard_map/ppermute | solution.py:107
  48.7 1.3 %dynamic-slice_convert_fusion.filt_ref = f32[8,1152]{1,0:T(8,128)} fusion(bf16[128,2048]{1,0:T(8,128)(2,1)} %param.14, s32[]{:T(128)S(6)} %select_n.13), kind=kLoop, calls=%fused_computation | loop fusion | flops 9216 | bytes 55300 | tf_op jit(solution)/shard_map/convert_element_type | solution.py:384
  50.0 1.1 %shard_map.115 = (bf16[8,128,256]{2,1,0:T(8,128)(2,1)S(1)}, f32[8,1280]{1,0:T(8,128)S(1)}, f32[256,128]{1,0:T(8,128)S(1)}, f32[1,2048]{1,0:T(1,128)S(1)}) custom-call(s32[4]{0:T(128)} %docs_ref.1, f32[8,1152]{1,0:T(8,128)} %dynamic-slice_convert_fusion.filt_ref, bf16[16,128,128]{2,1,0:T(8,128)(2,1)S(1)} %all-to-all-done.gate_ref, f32[1,2048]{1,0:T(1,128)} %bitcast.7), custom_call_target="tpu_custom_call" | custom-call | tf_op jit(solution)/shard_map/pallas_call | solution.py:385
  51.7 3.0 %shard_map.119 = (bf16[8,136,128]{2,1,0:T(8,128)(2,1)S(1)}, bf16[8,136,128]{2,1,0:T(8,128)(2,1)S(1)}) custom-call(s32[1]{0:T(128)} %bitcast.ctx_ref, bf16[8,128,256]{2,1,0:T(8,128)(2,1)S(1)} %get-tuple-element.39.gate_t_ref, f32[8,1280]{1,0:T(8,128)S(1)} %get-tuple-element.40.rows_ref, f32[256,128]{1,0:T(8,128)S(1)} %get-tuple-element.41.doc_ref, ...), custom_call_target="tpu_custom_call" | custom-call | tf_op jit(solution)/shard_map/pallas_call | solution.py:396
  54.8 1.5 %collective-permute-done.10.got_ref = bf16[8,136,128]{2,1,0:T(8,128)(2,1)S(1)} collective-permute-done((bf16[8,136,128]{2,1,0:T(8,128)(2,1)S(1)}, bf16[8,136,128]{2,1,0:T(8,128)(2,1)S(1)}, u32[]{:S(2)}, u32[]{:S(2)}) %collective-permute-start.10) | collective-permute-done | bytes 278560 | tf_op jit(solution)/shard_map/ppermute | solution.py:99
  56.9 2.0 %collective-permute-start.12 = (bf16[2,136,128]{2,1,0:T(8,128)(2,1)S(1)}, bf16[2,136,128]{2,1,0:T(8,128)(2,1)S(1)}, u32[]{:S(2)}, u32[]{:S(2)}) collective-permute-start(bf16[2,136,128]{2,1,0:T(8,128)(2,1)S(1)} %get-tuple-element.55), channel_id=1, source_target_pairs={{0,16},{2,18},{4,20},{6,22},{8,24},{10,26},{12,28},{14,30},{16,0},... | collective-permute-start | bytes 208904 | tf_op jit(solution)/shard_map/ppermute | solution.py:107
  58.9 2.1 %collective-permute-start.13 = (bf16[2,136,128]{2,1,0:T(8,128)(2,1)S(1)}, bf16[2,136,128]{2,1,0:T(8,128)(2,1)S(1)}, u32[]{:S(2)}, u32[]{:S(2)}) collective-permute-start(bf16[2,136,128]{2,1,0:T(8,128)(2,1)S(1)} %get-tuple-element.56), channel_id=1, source_target_pairs={{0,12},{2,14},{4,8},{6,10},{8,4},{10,6},{12,0},{14,2},{16,28},{18,... | collective-permute-start | bytes 208904 | tf_op jit(solution)/shard_map/ppermute | solution.py:107
  60.9 2.4 %collective-permute-start.14 = (bf16[2,136,128]{2,1,0:T(8,128)(2,1)S(1)}, bf16[2,136,128]{2,1,0:T(8,128)(2,1)S(1)}, u32[]{:S(2)}, u32[]{:S(2)}) collective-permute-start(bf16[2,136,128]{2,1,0:T(8,128)(2,1)S(1)} %get-tuple-element.57), channel_id=1, source_target_pairs={{0,28},{2,30},{4,24},{6,26},{8,20},{10,22},{12,16},{14,18},{16,12}... | collective-permute-start | bytes 208904 | tf_op jit(solution)/shard_map/ppermute | solution.py:107
  63.9 2.0 %collective-permute-start.16 = (bf16[2,136,128]{2,1,0:T(8,128)(2,1)S(1)}, bf16[2,136,128]{2,1,0:T(8,128)(2,1)S(1)}, u32[]{:S(2)}, u32[]{:S(2)}) collective-permute-start(bf16[2,136,128]{2,1,0:T(8,128)(2,1)S(1)} %get-tuple-element.59), channel_id=1, source_target_pairs={{0,8},{2,10},{4,12},{6,14},{8,0},{10,2},{12,4},{14,6},{16,24},{18,... | collective-permute-start | bytes 208904 | tf_op jit(solution)/shard_map/ppermute | solution.py:107
  65.9 1.6 %collective-permute-done.12.refs_2_ = bf16[2,136,128]{2,1,0:T(8,128)(2,1)S(1)} collective-permute-done((bf16[2,136,128]{2,1,0:T(8,128)(2,1)S(1)}, bf16[2,136,128]{2,1,0:T(8,128)(2,1)S(1)}, u32[]{:S(2)}, u32[]{:S(2)}) %collective-permute-start.12) | collective-permute-done | bytes 69664 | tf_op jit(solution)/shard_map/ppermute | solution.py:107
  68.5 1.2 %shard_map.116 = (bf16[128,2048]{1,0:T(8,128)(2,1)S(1)}, bf16[128,2048]{1,0:T(8,128)(2,1)S(1)}) custom-call(bf16[128,2048]{1,0:T(8,128)(2,1)} %query_hbm.3, bf16[128,2048]{1,0:T(8,128)(2,1)} %key_hbm.3), custom_call_target="tpu_custom_call" | custom-call | tf_op jit(solution)/shard_map/pallas_call | solution.py:407
  69.8 3.9 %collective-permute-done.17.refs_7_ = bf16[2,136,128]{2,1,0:T(8,128)(2,1)S(1)} collective-permute-done((bf16[2,136,128]{2,1,0:T(8,128)(2,1)S(1)}, bf16[2,136,128]{2,1,0:T(8,128)(2,1)S(1)}, u32[]{:S(2)}, u32[]{:S(2)}) %collective-permute-start.17) | collective-permute-done | bytes 69664 | tf_op jit(solution)/shard_map/ppermute | solution.py:107
  73.6 2.9 %shard_map.121 = (bf16[128,2048]{1,0:T(8,128)(2,1)}, bf16[128,2048]{1,0:T(8,128)(2,1)}, f32[128,128]{1,0:T(8,128)}) custom-call(s32[1]{0:T(128)} %bitcast.ctx_ref, s32[1,2048]{1,0:T(1,128)S(1)} %get-tuple-element.32.rank_ref, bf16[128,2048]{1,0:T(8,128)(2,1)S(1)} %get-tuple-element.34.conv_ref, f32[1,2048]{1,0:T(1,128)S(1)} %get-tuple-element.36.skip_ref, ...), custom_call_target="tpu_custom_call" | custom-call | tf_op jit(solution)/shard_map/pallas_call | solution.py:410
  (28 shorter events, 6.6 us)
Async XLA Ops:
  0.6 13.7 %copy-start = (bf16[128,2048]{1,0:T(8,128)(2,1)S(1)}, bf16[128,2048]{1,0:T(8,128)(2,1)}, u32[]{:S(2)}) copy-start(bf16[128,2048]{1,0:T(8,128)(2,1)} %grad_hbm.1) | copy-start | bytes 1572868
  6.9 43.2 %all-to-all-start = ((bf16[16,128,128]{2,1,0:T(8,128)(2,1)}), bf16[16,128,128]{2,1,0:T(8,128)(2,1)S(1)}, u32[]{:S(2)}, u32[]{:S(2)}) async-start(bf16[16,128,128]{2,1,0:T(8,128)(2,1)} %get-tuple-element.35), calls=%async_computation | async-start | bytes 1048576 | tf_op jit(solution)/shard_map/all_to_all | solution.py:360
  14.3 9.2 %collective-permute-start.1 = (bf16[128,1024]{1,0:T(8,128)(2,1)S(1)}, bf16[128,1024]{1,0:T(8,128)(2,1)S(1)}, u32[]{:S(2)}, u32[]{:S(2)}) collective-permute-start(bf16[128,1024]{1,0:T(8,128)(2,1)S(1)} %get-tuple-element.61), channel_id=1, source_target_pairs={{0,1},{1,0},{2,3},{3,2},{4,5},{5,4},{6,7},{7,6},{8,9},{9,8},{10,11... | collective-permute-start | bytes 786440 | tf_op jit(solution)/shard_map/ppermute | solution.py:339
  15.9 12.7 %collective-permute-start = (bf16[128,1024]{1,0:T(8,128)(2,1)S(1)}, bf16[128,1024]{1,0:T(8,128)(2,1)S(1)}, u32[]{:S(2)}, u32[]{:S(2)}) collective-permute-start(bf16[128,1024]{1,0:T(8,128)(2,1)S(1)} %get-tuple-element.62), channel_id=1, source_target_pairs={{0,1},{1,0},{2,3},{3,2},{4,5},{5,4},{6,7},{7,6},{8,9},{9,8},{10,11... | collective-permute-start | bytes 786440 | tf_op jit(solution)/shard_map/ppermute | solution.py:339
  32.3 1.6 %collective-permute-start.2 = (bf16[8,128,128]{2,1,0:T(8,128)(2,1)S(1)}, bf16[8,128,128]{2,1,0:T(8,128)(2,1)S(1)}, u32[]{:S(2)}, u32[]{:S(2)}) collective-permute-start(bf16[8,128,128]{2,1,0:T(8,128)(2,1)S(1)} %get-tuple-element.42), channel_id=1, source_target_pairs={{0,2},{2,0},{4,6},{6,4},{8,10},{10,8},{12,14},{14,12},{16,18},{18,... | collective-permute-start | bytes 786440 | tf_op jit(solution)/shard_map/ppermute | solution.py:99
  34.0 9.3 %collective-permute-start.3 = (bf16[2,128,128]{2,1,0:T(8,128)(2,1)S(1)}, bf16[2,128,128]{2,1,0:T(8,128)(2,1)S(1)}, u32[]{:S(2)}, u32[]{:S(2)}) collective-permute-start(bf16[2,128,128]{2,1,0:T(8,128)(2,1)S(1)} %get-tuple-element.44), channel_id=1, source_target_pairs={{0,20},{2,22},{4,16},{6,18},{8,28},{10,30},{12,24},{14,26},{16,4},... | collective-permute-start | bytes 196616 | tf_op jit(solution)/shard_map/ppermute | solution.py:107
  37.5 8.2 %collective-permute-start.4 = (bf16[2,128,128]{2,1,0:T(8,128)(2,1)S(1)}, bf16[2,128,128]{2,1,0:T(8,128)(2,1)S(1)}, u32[]{:S(2)}, u32[]{:S(2)}) collective-permute-start(bf16[2,128,128]{2,1,0:T(8,128)(2,1)S(1)} %get-tuple-element.45), channel_id=1, source_target_pairs={{0,16},{2,18},{4,20},{6,22},{8,24},{10,26},{12,28},{14,30},{16,0},... | collective-permute-start | bytes 196616 | tf_op jit(solution)/shard_map/ppermute | solution.py:107
  38.0 13.1 %collective-permute-start.5 = (bf16[2,128,128]{2,1,0:T(8,128)(2,1)S(1)}, bf16[2,128,128]{2,1,0:T(8,128)(2,1)S(1)}, u32[]{:S(2)}, u32[]{:S(2)}) collective-permute-start(bf16[2,128,128]{2,1,0:T(8,128)(2,1)S(1)} %get-tuple-element.46), channel_id=1, source_target_pairs={{0,12},{2,14},{4,8},{6,10},{8,4},{10,6},{12,0},{14,2},{16,28},{18,... | collective-permute-start | bytes 196616 | tf_op jit(solution)/shard_map/ppermute | solution.py:107
  39.5 11.7 %collective-permute-start.6 = (bf16[2,128,128]{2,1,0:T(8,128)(2,1)S(1)}, bf16[2,128,128]{2,1,0:T(8,128)(2,1)S(1)}, u32[]{:S(2)}, u32[]{:S(2)}) collective-permute-start(bf16[2,128,128]{2,1,0:T(8,128)(2,1)S(1)} %get-tuple-element.47), channel_id=1, source_target_pairs={{0,28},{2,30},{4,24},{6,26},{8,20},{10,22},{12,16},{14,18},{16,12}... | collective-permute-start | bytes 196616 | tf_op jit(solution)/shard_map/ppermute | solution.py:107
  42.7 8.4 %collective-permute-start.7 = (bf16[2,128,128]{2,1,0:T(8,128)(2,1)S(1)}, bf16[2,128,128]{2,1,0:T(8,128)(2,1)S(1)}, u32[]{:S(2)}, u32[]{:S(2)}) collective-permute-start(bf16[2,128,128]{2,1,0:T(8,128)(2,1)S(1)} %get-tuple-element.48), channel_id=1, source_target_pairs={{0,4},{2,6},{4,0},{6,2},{8,12},{10,14},{12,8},{14,10},{16,20},{18,... | collective-permute-start | bytes 196616 | tf_op jit(solution)/shard_map/ppermute | solution.py:107
  43.3 7.9 %collective-permute-start.8 = (bf16[2,128,128]{2,1,0:T(8,128)(2,1)S(1)}, bf16[2,128,128]{2,1,0:T(8,128)(2,1)S(1)}, u32[]{:S(2)}, u32[]{:S(2)}) collective-permute-start(bf16[2,128,128]{2,1,0:T(8,128)(2,1)S(1)} %get-tuple-element.49), channel_id=1, source_target_pairs={{0,8},{2,10},{4,12},{6,14},{8,0},{10,2},{12,4},{14,6},{16,24},{18,... | collective-permute-start | bytes 196616 | tf_op jit(solution)/shard_map/ppermute | solution.py:107
  45.7 6.1 %collective-permute-start.9 = (bf16[2,128,128]{2,1,0:T(8,128)(2,1)S(1)}, bf16[2,128,128]{2,1,0:T(8,128)(2,1)S(1)}, u32[]{:S(2)}, u32[]{:S(2)}) collective-permute-start(bf16[2,128,128]{2,1,0:T(8,128)(2,1)S(1)} %get-tuple-element.50), channel_id=1, source_target_pairs={{0,24},{2,26},{4,28},{6,30},{8,16},{10,18},{12,20},{14,22},{16,8},... | collective-permute-start | bytes 196616 | tf_op jit(solution)/shard_map/ppermute | solution.py:107
  54.7 1.6 %collective-permute-start.10 = (bf16[8,136,128]{2,1,0:T(8,128)(2,1)S(1)}, bf16[8,136,128]{2,1,0:T(8,128)(2,1)S(1)}, u32[]{:S(2)}, u32[]{:S(2)}) collective-permute-start(bf16[8,136,128]{2,1,0:T(8,128)(2,1)S(1)} %get-tuple-element.52), channel_id=1, source_target_pairs={{0,2},{2,0},{4,6},{6,4},{8,10},{10,8},{12,14},{14,12},{16,18},{18,... | collective-permute-start | bytes 835592 | tf_op jit(solution)/shard_map/ppermute | solution.py:99
  56.4 7.5 %collective-permute-start.11 = (bf16[2,136,128]{2,1,0:T(8,128)(2,1)S(1)}, bf16[2,136,128]{2,1,0:T(8,128)(2,1)S(1)}, u32[]{:S(2)}, u32[]{:S(2)}) collective-permute-start(bf16[2,136,128]{2,1,0:T(8,128)(2,1)S(1)} %get-tuple-element.54), channel_id=1, source_target_pairs={{0,20},{2,22},{4,16},{6,18},{8,28},{10,30},{12,24},{14,26},{16,4},... | collective-permute-start | bytes 208904 | tf_op jit(solution)/shard_map/ppermute | solution.py:107
  56.9 10.7 %collective-permute-start.12 = (bf16[2,136,128]{2,1,0:T(8,128)(2,1)S(1)}, bf16[2,136,128]{2,1,0:T(8,128)(2,1)S(1)}, u32[]{:S(2)}, u32[]{:S(2)}) collective-permute-start(bf16[2,136,128]{2,1,0:T(8,128)(2,1)S(1)} %get-tuple-element.55), channel_id=1, source_target_pairs={{0,16},{2,18},{4,20},{6,22},{8,24},{10,26},{12,28},{14,30},{16,0},... | collective-permute-start | bytes 208904 | tf_op jit(solution)/shard_map/ppermute | solution.py:107
  58.9 10.8 %collective-permute-start.13 = (bf16[2,136,128]{2,1,0:T(8,128)(2,1)S(1)}, bf16[2,136,128]{2,1,0:T(8,128)(2,1)S(1)}, u32[]{:S(2)}, u32[]{:S(2)}) collective-permute-start(bf16[2,136,128]{2,1,0:T(8,128)(2,1)S(1)} %get-tuple-element.56), channel_id=1, source_target_pairs={{0,12},{2,14},{4,8},{6,10},{8,4},{10,6},{12,0},{14,2},{16,28},{18,... | collective-permute-start | bytes 208904 | tf_op jit(solution)/shard_map/ppermute | solution.py:107
  60.9 8.8 %collective-permute-start.14 = (bf16[2,136,128]{2,1,0:T(8,128)(2,1)S(1)}, bf16[2,136,128]{2,1,0:T(8,128)(2,1)S(1)}, u32[]{:S(2)}, u32[]{:S(2)}) collective-permute-start(bf16[2,136,128]{2,1,0:T(8,128)(2,1)S(1)} %get-tuple-element.57), channel_id=1, source_target_pairs={{0,28},{2,30},{4,24},{6,26},{8,20},{10,22},{12,16},{14,18},{16,12}... | collective-permute-start | bytes 208904 | tf_op jit(solution)/shard_map/ppermute | solution.py:107
  63.3 6.4 %collective-permute-start.15 = (bf16[2,136,128]{2,1,0:T(8,128)(2,1)S(1)}, bf16[2,136,128]{2,1,0:T(8,128)(2,1)S(1)}, u32[]{:S(2)}, u32[]{:S(2)}) collective-permute-start(bf16[2,136,128]{2,1,0:T(8,128)(2,1)S(1)} %get-tuple-element.58), channel_id=1, source_target_pairs={{0,4},{2,6},{4,0},{6,2},{8,12},{10,14},{12,8},{14,10},{16,20},{18,... | collective-permute-start | bytes 208904 | tf_op jit(solution)/shard_map/ppermute | solution.py:107
  63.9 5.8 %collective-permute-start.16 = (bf16[2,136,128]{2,1,0:T(8,128)(2,1)S(1)}, bf16[2,136,128]{2,1,0:T(8,128)(2,1)S(1)}, u32[]{:S(2)}, u32[]{:S(2)}) collective-permute-start(bf16[2,136,128]{2,1,0:T(8,128)(2,1)S(1)} %get-tuple-element.59), channel_id=1, source_target_pairs={{0,8},{2,10},{4,12},{6,14},{8,0},{10,2},{12,4},{14,6},{16,24},{18,... | collective-permute-start | bytes 208904 | tf_op jit(solution)/shard_map/ppermute | solution.py:107
  67.5 6.1 %collective-permute-start.17 = (bf16[2,136,128]{2,1,0:T(8,128)(2,1)S(1)}, bf16[2,136,128]{2,1,0:T(8,128)(2,1)S(1)}, u32[]{:S(2)}, u32[]{:S(2)}) collective-permute-start(bf16[2,136,128]{2,1,0:T(8,128)(2,1)S(1)} %get-tuple-element.60), channel_id=1, source_target_pairs={{0,24},{2,26},{4,28},{6,30},{8,16},{10,18},{12,20},{14,22},{16,8},... | collective-permute-start | bytes 208904 | tf_op jit(solution)/shard_map/ppermute | solution.py:107

commit v7 on v5

--- a/solution.py
+++ b/solution.py
@@ -82,25 +82,26 @@
     return [0] + sorted(range(1, count // 2), key=lambda e: (-hops(e), -(e == 4), e))
 
 
-def join_pair(ctx, packs, full_ref):
+def pack_kernel(*refs, parts):
+    mine, got, packs = refs[:parts], refs[parts : 2 * parts], refs[2 * parts :]
     for e, pack in zip(distances(2 * len(packs)), packs):
-        full_ref[ctx ^ (2 * e)] = pack[0]
-        full_ref[ctx ^ (2 * e + 1)] = pack[1]
-
-
-def pack_kernel(mine_ref, got_ref, *packs):
-    for e, pack in zip(distances(2 * len(packs)), packs):
-        pack[0] = mine_ref[e]
-        pack[1] = got_ref[e]
-
-
-def exchange(mine, swap_other, count):
-    got = lax.ppermute(on_chip(swap_other), "ctx", [(i, i ^ 1) for i in range(count)])
-    mine = mine()
-    shape = pltpu.VMEM((2,) + mine.shape[1:], BF16)
-    packs = call(pack_kernel, (shape,) * (count // 2), [VMEM, VMEM])(
-        on_chip(mine), on_chip(got)
-    )
+        for which, pieces in enumerate((mine, got)):
+            at = 0
+            for piece in pieces:
+                pack[which, at : at + piece.shape[1]] = piece[e]
+                at = at + piece.shape[1]
+
+
+def swap_pair(blocks, count):
+    return on_chip(lax.ppermute(on_chip(blocks), "ctx", [(i, i ^ 1) for i in range(count)]))
+
+
+def spread(mine, got, count):
+    rows = sum(piece.shape[1] for piece in mine)
+    shape = pltpu.VMEM((2, rows, mine[0].shape[2]), BF16)
+    packs = call(
+        functools.partial(pack_kernel, parts=len(mine)), (shape,) * (count // 2), [VMEM] * (2 * len(mine))
+    )(*[on_chip(piece) for piece in mine], *got)
     out = []
     for e, pack in zip(distances(count), packs):
         moved = lax.ppermute(on_chip(pack), "ctx", [(i, i ^ (2 * e)) for i in range(count)]) if e else pack
@@ -109,7 +110,8 @@
 
 
 def gate_kernel(
-    group_hbm, query_hbm, key_hbm, grad_hbm, out_ref, rank_ref, grad_ref, group_ref, query_ref, key_ref, column_ref, sem, *, groups, per_group
+    group_hbm, query_hbm, key_hbm, grad_hbm, out_hbm, rank_ref, grad_ref,
+    group_ref, query_ref, key_ref, out_ref, column_ref, sem, store_sem, *, groups, per_group
 ):
     loads = [
         pltpu.make_async_copy(group_hbm, group_ref, sem.at[0]),
@@ -137,12 +139,16 @@
         load.wait()
     gated = (query_ref[...].astype(F32) * key_ref[...].astype(F32)).astype(BF16)
     rows = out_ref.shape[1]
-
-    def store(i, block):
+    stores = []
+
+    def save(i, block):
         out_ref[i] = block
-
-    permute(gated, column_ref, range(0, channels, rows), rows, store)
-    loads[3].wait()
+        stores.append(pltpu.make_async_copy(out_ref.at[i], out_hbm.at[i], store_sem.at[i]))
+        stores[-1].start()
+
+    permute(gated, column_ref, range(0, channels, rows), rows, save)
+    for copy in [loads[3]] + stores:
+        copy.wait()
 
 
 def stream_weights(half, weight_hbm, weight_ref, sem):
@@ -228,11 +234,16 @@
     skip_out_ref[...] = skip_ref[...]
 
 
-def conv_kernel(ctx_ref, gate_t_ref, rows_ref, doc_ref, *refs, per_group):
-    *packs, mine_ref, other_ref, grad_ref, out_ref, moved_ref, sums_ref = refs
-    join_pair(ctx_ref[0], packs, grad_ref)
+def conv_kernel(ctx_ref, gate_t_ref, rows_ref, doc_ref, *refs, per_group, first, final):
+    *packs, mine_ref, other_ref, total_ref, grad_ref, out_ref, moved_ref = refs
+    earlier = packs.pop() if first else None
     spans, sub, tokens = grad_ref.shape
-    groups, padded = rows_ref.shape
+    groups = sub // per_group
+    top = first * per_group
+    for e, pack in zip(distances(spans), packs):
+        grad_ref[ctx_ref[0] ^ (2 * e)] = pack[0, top : top + sub]
+        grad_ref[ctx_ref[0] ^ (2 * e + 1)] = pack[1, top : top + sub]
+    padded = rows_ref.shape[1]
     lags = padded - tokens
     reach = lags // tokens
     for k in range(reach):
@@ -245,26 +256,28 @@
             moved_ref[g, :keep, cols] = grad * same
             if k:
                 moved_ref[g, keep:, cols] = jnp.zeros((cut, tokens), BF16)
-    sums_ref[...] = jnp.zeros(sums_ref.shape, F32)
+    total_ref[...] = earlier[...] if first else jnp.zeros(total_ref.shape, F32)
     for g in range(groups):
         moved = moved_ref[g]
-        wide = jnp.broadcast_to(rows_ref[g : g + 1, :], (tokens, padded))
+        row = slice(first + g, first + g + 1)
+        wide = jnp.broadcast_to(rows_ref[row, :], (tokens, padded))
         toeplitz = pltpu.roll(wide, 0, 1, stride=1, stride_axis=0)[:, :lags].astype(BF16)
         back = dot(moved, toeplitz, NT)
         out_ref[:, g * per_group : (g + 1) * per_group, :] = back.astype(BF16).reshape(spans, per_group, tokens)
-        corr = dot(gate_t_ref[g], moved, NN)
+        corr = dot(gate_t_ref[first + g], moved, NN)
         wide = jnp.concatenate([corr, jnp.zeros((tokens, tokens), F32)], axis=1)
         skewed = pltpu.roll(wide, lags + 1, 1, stride=1, stride_axis=0)
-        sums_ref[g : g + 1, :] = jnp.sum(skewed[:, :lags], axis=0, keepdims=True)
-    for k in range(spans):
-        if k < reach:
-            out_ref[k, sub:, :] = sums_ref[:, k * tokens : (k + 1) * tokens].astype(BF16)
-        else:
-            out_ref[k, sub:, :] = jnp.zeros((EXTRA, tokens), BF16)
+        total_ref[row, :] = jnp.sum(skewed[:, :lags], axis=0, keepdims=True)
+    if final:
+        for k in range(spans):
+            if k < reach:
+                out_ref[k, sub:, :] = total_ref[:, k * tokens : (k + 1) * tokens].astype(BF16)
+            else:
+                out_ref[k, sub:, :] = jnp.zeros((EXTRA, tokens), BF16)
     split_pair(ctx_ref[0], out_ref, mine_ref, other_ref)
 
 
-def fetch_kernel(query_hbm, key_hbm, query_ref, key_ref, sem):
+def fetch_kernel(query_hbm, key_hbm, after_ref, query_ref, key_ref, sem):
     loads = [
         pltpu.make_async_copy(query_hbm, query_ref, sem.at[0]),
         pltpu.make_async_copy(key_hbm, key_ref, sem.at[1]),
@@ -275,26 +288,53 @@
         load.wait()
 
 
-def gates_kernel(
-    ctx_ref, rank_ref, conv_ref, skip_ref, query_ref, key_ref, *refs, sub_groups
-):
-    *packs, grad_query_hbm, grad_key_hbm, filt_hbm = refs[:-7]
-    grad_query_ref, grad_key_ref, filt_ref, sorted_ref, back_ref, store_sem, filt_sem = refs[-7:]
-    join_pair(ctx_ref[0], packs, back_ref)
-    spans, rows, tokens = back_ref.shape
-    sub = rows - EXTRA
+def by_token(packs, sorted_ref):
+    sub = packs[0].shape[1] - EXTRA
+    for i, pack in enumerate(packs):
+        flat = pack[:, :sub, :].reshape(2 * sub, pack.shape[2])
+        sorted_ref[:, i * 2 * sub : (i + 1) * 2 * sub] = flat.T
+
+
+def picks_of(ctx, rank, apart, sub):
+    shape = (sub, rank.shape[1])
+    row = lax.broadcasted_iota(I32, shape, 0)
+    blocks = []
+    for e in apart:
+        for which in range(2):
+            source = ctx ^ (2 * e + which)
+            blocks.append(jnp.where(row == rank - source * sub, 1.0, 0.0).astype(BF16))
+    return jnp.concatenate(blocks, axis=0)
+
+
+def restore_kernel(ctx_ref, rank_ref, conv_ref, skip_ref, *refs, apart):
+    *packs, out_ref, sorted_ref = refs
+    sub = packs[0].shape[1] - EXTRA
+    by_token(packs, sorted_ref)
     channels = rank_ref.shape[1]
-    sorted_ref[...] = back_ref[:, :sub, :].reshape(spans * sub, tokens).T
-    for d in range(spans):
-        filt_ref[d * sub_groups : (d + 1) * sub_groups, :] = back_ref[d, sub:, :].astype(F32)[:sub_groups]
+    width = min(2 * LANES, channels)
+    for j in range(0, channels, width):
+        cols = slice(j, j + width)
+        picks = picks_of(ctx_ref[0], rank_ref[:, cols], apart, sub)
+        out_ref[:, cols] = dot(sorted_ref[...], picks, NN) + conv_ref[:, cols].astype(F32) * skip_ref[:, cols]
+
+
+def gates_kernel(ctx_ref, rank_ref, acc_ref, query_ref, key_ref, *refs, early, sub_groups):
+    *packs, grad_query_hbm, grad_key_hbm, filt_hbm = refs[:-6]
+    grad_query_ref, grad_key_ref, filt_ref, sorted_ref, store_sem, filt_sem = refs[-6:]
+    channels = rank_ref.shape[1]
+    sub = packs[0].shape[1] - EXTRA
+    apart = distances(2 * len(packs))
+    by_token(packs[early:], sorted_ref)
+    for e, pack in zip(apart, packs):
+        for which in range(2):
+            filt_ref[ctx_ref[0] ^ (2 * e + which)] = pack[which, sub:, :].astype(F32)[:sub_groups]
     stores = [pltpu.make_async_copy(filt_ref, filt_hbm, filt_sem)]
     stores[0].start()
     width = channels // store_sem.shape[1]
     for j in range(store_sem.shape[1]):
         cols = slice(j * width, (j + 1) * width)
-        place = lax.broadcasted_iota(I32, (channels, width), 0)
-        picks = jnp.where(place == rank_ref[:, cols], 1.0, 0.0).astype(BF16)
-        gated_grad = dot(sorted_ref[...], picks, NN) + conv_ref[:, cols].astype(F32) * skip_ref[:, cols]
+        picks = picks_of(ctx_ref[0], rank_ref[:, cols], apart[early:], sub)
+        gated_grad = acc_ref[:, cols] + dot(sorted_ref[...], picks, NN)
         grad_query_ref[:, cols] = (gated_grad * key_ref[:, cols].astype(F32)).astype(BF16)
         grad_key_ref[:, cols] = (gated_grad * query_ref[:, cols].astype(F32)).astype(BF16)
         for which, (source, target) in enumerate(((grad_query_ref, grad_query_hbm), (grad_key_ref, grad_key_hbm))):
@@ -329,12 +369,14 @@
     gate_sorted, rank, grad_here = call(
         functools.partial(gate_kernel, groups=groups, per_group=per_group),
         (
-            pltpu.VMEM((spans, sub, tokens), BF16),
+            jax.ShapeDtypeStruct((spans, sub, tokens), BF16),
             pltpu.VMEM((1, channels), I32),
             pltpu.VMEM((tokens, feats), BF16),
         ),
         [ANY, ANY, ANY, ANY],
-        [pltpu.VMEM((1, channels), I32), wide, wide, column, dma((4,))],
+        [pltpu.VMEM((1, channels), I32), wide, wide, pltpu.VMEM((spans, sub, tokens), BF16)]
+        + [column, dma((4,)), dma((spans,))],
+        (ANY, VMEM, VMEM),
     )(group_of.reshape(1, channels), query_proj, key_proj, grad_out)
     gate_moved = lax.all_to_all(gate_sorted, "ctx", 0, 0)
 
@@ -364,13 +406,11 @@
                     dma,
                 ],
             )(source, ctx, on_chip(rank), on_chip(grad), acc, out_proj, value_proj)
-
-    def conv_mine():
-        return call(
-            mine_kernel, pltpu.VMEM((spans // 2, sub, tokens), BF16), [SMEM, VMEM, VMEM], [column]
-        )(ctx, on_chip(rank), on_chip(conv_grad))
-
-    conv_moved = exchange(conv_mine, conv_sorted, spans)
+    got = swap_pair(conv_sorted, spans)
+    mine = call(
+        mine_kernel, pltpu.VMEM((spans // 2, sub, tokens), BF16), [SMEM, VMEM, VMEM], [column]
+    )(ctx, on_chip(rank), on_chip(conv_grad))
+    conv_moved = spread([mine], [got], spans)
 
     filt_sub = lax.dynamic_slice(filters, (position * sub_groups, 0), (sub_groups, lags)).astype(F32)
     gate_t, rows, doc, skip = call(
@@ -384,40 +424,52 @@
         [SMEM, VMEM, VMEM, VMEM],
     )(doc_lengths, filt_sub, on_chip(gate_moved), skip_gain.reshape(1, channels))
 
-    back, back_other = call(
-        functools.partial(conv_kernel, per_group=per_group),
-        (pltpu.VMEM((spans // 2, sub + EXTRA, tokens), BF16),) * 2,
-        [SMEM] + [VMEM] * (3 + spans // 2),
-        [
-            pltpu.VMEM((spans, sub, tokens), BF16),
-            pltpu.VMEM((spans, sub + EXTRA, tokens), BF16),
-            pltpu.VMEM((sub_groups, spans * per_group, lags), BF16),
-            pltpu.VMEM((EXTRA, lags), F32),
-        ],
-    )(ctx, on_chip(gate_t), on_chip(rows), on_chip(doc), *conv_moved)
-    query_here, key_here = call(fetch_kernel, (wide, wide), [ANY, ANY], [dma((2,))])(query_proj, key_proj)
-    back_moved = exchange(lambda: back, back_other, spans)
-
-    return call(
-        functools.partial(gates_kernel, sub_groups=sub_groups),
+    mine, got, sums = [], [], []
+    tail = max(1, sub_groups // 4)
+    for first, count in ((0, sub_groups - tail), (sub_groups - tail, tail)):
+        final = first > 0
+        part = count * per_group
+        full = part + (EXTRA if final else 0)
+        back, other, total = call(
+            functools.partial(conv_kernel, per_group=per_group, first=first, final=final),
+            (pltpu.VMEM((spans // 2, full, tokens), BF16),) * 2 + (pltpu.VMEM((EXTRA, lags), F32),),
+            [SMEM] + [VMEM] * (3 + spans // 2 + len(sums)),
+            [
+                pltpu.VMEM((spans, part, tokens), BF16),
+                pltpu.VMEM((spans, full, tokens), BF16),
+                pltpu.VMEM((count, spans * per_group, lags), BF16),
+            ],
+        )(ctx, on_chip(gate_t), on_chip(rows), on_chip(doc), *conv_moved, *sums)
+        sums = [on_chip(total)]
+        mine.append(back)
+        got.append(swap_pair(other, spans))
+    back_moved = spread(mine, got, spans)
+
+    early = 3
+    apart = distances(spans)
+    acc = on_chip(
+        call(
+            functools.partial(restore_kernel, apart=apart[:early]),
+            pltpu.VMEM((tokens, channels), F32),
+            [SMEM] + [VMEM] * (3 + early),
+            [pltpu.VMEM((tokens, early * 2 * sub), BF16)],
+        )(ctx, on_chip(rank), on_chip(conv_grad), on_chip(skip), *back_moved[:early])
+    )
+    query_here, key_here = call(fetch_kernel, (wide, wide), [ANY, ANY, VMEM], [dma((2,))])(query_proj, key_proj, acc)
+    grad_query, grad_key, grad_filters = call(
+        functools.partial(gates_kernel, early=early, sub_groups=sub_groups),
         (
             jax.ShapeDtypeStruct((tokens, channels), BF16),
             jax.ShapeDtypeStruct((tokens, channels), BF16),
-            jax.ShapeDtypeStruct((groups, tokens), F32),
+            jax.ShapeDtypeStruct((spans, sub_groups, tokens), F32),
         ),
-        [SMEM] + [VMEM] * (5 + spans // 2),
-        [wide, wide, pltpu.VMEM((groups, tokens), F32), wide]
-        + [pltpu.VMEM((spans, sub + EXTRA, tokens), BF16), dma((2, min(8, channels // LANES))), dma],
+        [SMEM] + [VMEM] * (4 + spans // 2),
+        [wide, wide, pltpu.VMEM((spans, sub_groups, tokens), F32)]
+        + [pltpu.VMEM((tokens, channels - early * 2 * sub), BF16)]
+        + [dma((2, min(8, channels // LANES))), dma],
         (ANY, ANY, ANY),
-    )(
-        ctx,
-        on_chip(rank),
-        on_chip(conv_grad),
-        on_chip(skip),
-        on_chip(query_here),
-        on_chip(key_here),
-        *back_moved,
-    )
+    )(ctx, on_chip(rank), acc, on_chip(query_here), on_chip(key_here), *back_moved)
+    return grad_query, grad_key, grad_filters.reshape(groups, tokens)
 
 
 def solution(mesh):

time: 67.9 us -> 68.1 us (level)
  Pallas kernels: 22.5 us -> 23.5 us
  starting transfers between devices: 34.5 us -> 33.6 us
    ppermute x16 -> x17, starting transfers between devices: 25.5 us -> 24.4 us  [the longest x14 23.6 us: spread(): lax.ppermute(on_chip(pack), 'ctx', [(i, i ^ 2 * e) for i in range(count)])]
    pallas_call x6 -> x8, Pallas kernels: 8.05 us -> 9.05 us  [the longest x2 3.66 us: per_device(): call(functools.partial(conv_kernel, per_group=per_group, first=first, fin...]
    ppermute x16 -> x17, waiting for transfers between devices: 8.26 us -> 8.3 us  [the longest x14 6.93 us: spread(): lax.ppermute(on_chip(pack), 'ctx', [(i, i ^ 2 * e) for i in range(count)])]
  transfers between devices with their start and end apart: 18 -> 19, of which waited for: 6 -> 6; matrix products, arithmetic and copies ran while one was open for 2% -> 2% of each run, Pallas kernels for 24% -> 28%
where the time goes in v7:
time: 68.1 us; the launch traced here: 67.7 us
  starting transfers between devices  33.6 us (49%)
  Pallas kernels  23.5 us (35%)
  waiting for transfers between devices  8.31 us (12%)
  other arithmetic  1.34 us (2%)
  between operations  0.98 us (1%)
    ppermute x14, starting transfers between devices, spread(): lax.ppermute(on_chip(pack), 'ctx', [(i, i ^ 2 * e) for i in range(count)])  23.6 us
    ppermute x14, waiting for transfers between devices, spread(): lax.ppermute(on_chip(pack), 'ctx', [(i, i ^ 2 * e) for i in range(count)])  6.93 us
    all_to_all x1, starting transfers between devices, per_device(): gate_moved = lax.all_to_all(gate_sorted, 'ctx', 0, 0)  6.1 us
    pallas_call x1, Pallas kernels, per_device(): call(last_kernel, (pltpu.VMEM((spans // 2, sub, tokens), BF16), pltpu.VME...  5.2 us
    pallas_call x1, Pallas kernels, per_device(): call(partial_kernel, pltpu.VMEM((tokens, channels), F32), [SMEM, VMEM, AN...  4.38 us
    pallas_call x1, Pallas kernels, per_device(): call(functools.partial(gate_kernel, groups=groups, per_group=per_group),...  3.79 us
    pallas_call x2, Pallas kernels, per_device(): call(functools.partial(conv_kernel, per_group=per_group, first=first, fin...  3.66 us
    ppermute x1, starting transfers between devices, per_device(): lax.ppermute(grad_out, 'head', [(i, (i + r) % heads) for i in range(heads)])  3.06 us
  transfers between devices with their start and end apart: 19, of which 6 were waited for; matrix products, arithmetic and copies ran while one was open for 2% of the time, Pallas kernels for 28%

profile of v7, /device:TPU:0, one launch (start us, length us, event | category | flops | bytes accessed | tf_op | source)
XLA Modules:
  0.0 67.7 jit_solution(3264592682432790959)
XLA Ops:
  0.6 3.1 %collective-permute-start = (bf16[128,2048]{1,0:T(8,128)(2,1)}, bf16[128,2048]{1,0:T(8,128)(2,1)S(1)}, u32[]{:S(2)}, u32[]{:S(2)}) collective-permute-start(bf16[128,2048]{1,0:T(8,128)(2,1)} %grad_hbm.1), channel_id=1, source_target_pairs={{0,1},{1,0},{2,3},{3,2},{4,5},{5,4},{6,7},{7,6},{8,9},{9,8},{10,11... | collective-permute-start | bytes 1572872 | tf_op jit(solution)/shard_map/ppermute | solution.py:367
  3.7 3.8 %shard_map.112 = (bf16[16,128,128]{2,1,0:T(8,128)(2,1)}, s32[1,2048]{1,0:T(1,128)S(1)}, bf16[128,2048]{1,0:T(8,128)(2,1)S(1)}) custom-call(s32[1,2048]{1,0:T(1,128)} %bitcast.6, bf16[128,2048]{1,0:T(8,128)(2,1)} %query_hbm.3, bf16[128,2048]{1,0:T(8,128)(2,1)} %key_hbm.3, bf16[128,2048]{1,0:T(8,128)(2,1)} %grad_hbm.1), custom_call_target="tpu_custom_call" | custom-call | tf_op jit(solution)/shard_map/pallas_call | solution.py:369
  7.5 6.1 %all-to-all-start = ((bf16[16,128,128]{2,1,0:T(8,128)(2,1)}), bf16[16,128,128]{2,1,0:T(8,128)(2,1)S(1)}, u32[]{:S(2)}, u32[]{:S(2)}) async-start(bf16[16,128,128]{2,1,0:T(8,128)(2,1)} %get-tuple-element.41), calls=%async_computation | async-start | bytes 1048576 | tf_op jit(solution)/shard_map/all_to_all | solution.py:381
  13.6 4.4 %shard_map.113.acc_ref = f32[128,2048]{1,0:T(8,128)S(1)} custom-call(s32[1]{0:T(128)} %bitcast.3.half_ref, bf16[128,2048]{1,0:T(8,128)(2,1)S(1)} %get-tuple-element.39.grad_ref, bf16[2048,4096]{1,0:T(8,128)(2,1)} %weight_hbm.3), custom_call_target="tpu_custom_call" | custom-call | tf_op jit(solution)/shard_map/pallas_call | solution.py:388
  18.0 5.2 %shard_map.114 = (bf16[8,128,128]{2,1,0:T(8,128)(2,1)S(1)}, bf16[128,2048]{1,0:T(8,128)(2,1)S(1)}) custom-call(s32[1]{0:T(128)} %bitcast.2.half_ref, s32[1]{0:T(128)} %bitcast.ctx_ref, s32[1,2048]{1,0:T(1,128)S(1)} %get-tuple-element.38.rank_ref, bf16[128,2048]{1,0:T(8,128)(2,1)S(1)} %collective-permute-done.grad_ref, f32[128,2048]{1,0:T(8,128)S(1)} %shard_map.113.acc_ref, ...), custom_call_target="tpu_custom_call" | custom-call | tf_op jit(solution)/shard_map/pallas_call | solution.py:396
  24.9 3.6 %collective-permute-start.2 = (bf16[2,128,128]{2,1,0:T(8,128)(2,1)S(1)}, bf16[2,128,128]{2,1,0:T(8,128)(2,1)S(1)}, u32[]{:S(2)}, u32[]{:S(2)}) collective-permute-start(bf16[2,128,128]{2,1,0:T(8,128)(2,1)S(1)} %get-tuple-element.48), channel_id=1, source_target_pairs={{0,20},{2,22},{4,16},{6,18},{8,28},{10,30},{12,24},{14,26},{16,4},... | collective-permute-start | bytes 196616 | tf_op jit(solution)/shard_map/ppermute | solution.py:107
  29.0 1.5 %collective-permute-start.4 = (bf16[2,128,128]{2,1,0:T(8,128)(2,1)S(1)}, bf16[2,128,128]{2,1,0:T(8,128)(2,1)S(1)}, u32[]{:S(2)}, u32[]{:S(2)}) collective-permute-start(bf16[2,128,128]{2,1,0:T(8,128)(2,1)S(1)} %get-tuple-element.50), channel_id=1, source_target_pairs={{0,12},{2,14},{4,8},{6,10},{8,4},{10,6},{12,0},{14,2},{16,28},{18,... | collective-permute-start | bytes 196616 | tf_op jit(solution)/shard_map/ppermute | solution.py:107
  30.5 3.2 %collective-permute-start.5 = (bf16[2,128,128]{2,1,0:T(8,128)(2,1)S(1)}, bf16[2,128,128]{2,1,0:T(8,128)(2,1)S(1)}, u32[]{:S(2)}, u32[]{:S(2)}) collective-permute-start(bf16[2,128,128]{2,1,0:T(8,128)(2,1)S(1)} %get-tuple-element.51), channel_id=1, source_target_pairs={{0,28},{2,30},{4,24},{6,26},{8,20},{10,22},{12,16},{14,18},{16,12}... | collective-permute-start | bytes 196616 | tf_op jit(solution)/shard_map/ppermute | solution.py:107
  34.9 1.8 %collective-permute-done.3.refs_2_ = bf16[2,128,128]{2,1,0:T(8,128)(2,1)S(1)} collective-permute-done((bf16[2,128,128]{2,1,0:T(8,128)(2,1)S(1)}, bf16[2,128,128]{2,1,0:T(8,128)(2,1)S(1)}, u32[]{:S(2)}, u32[]{:S(2)}) %collective-permute-start.3) | collective-permute-done | bytes 65568 | tf_op jit(solution)/shard_map/ppermute | solution.py:107
  36.7 3.0 %collective-permute-start.8 = (bf16[2,128,128]{2,1,0:T(8,128)(2,1)S(1)}, bf16[2,128,128]{2,1,0:T(8,128)(2,1)S(1)}, u32[]{:S(2)}, u32[]{:S(2)}) collective-permute-start(bf16[2,128,128]{2,1,0:T(8,128)(2,1)S(1)} %get-tuple-element.54), channel_id=1, source_target_pairs={{0,24},{2,26},{4,28},{6,30},{8,16},{10,18},{12,20},{14,22},{16,8},... | collective-permute-start | bytes 196616 | tf_op jit(solution)/shard_map/ppermute | solution.py:107
  39.7 1.3 %dynamic-slice_convert_fusion.filt_ref = f32[8,1152]{1,0:T(8,128)} fusion(bf16[128,2048]{1,0:T(8,128)(2,1)} %param.14, s32[]{:T(128)S(6)} %select_n.16), kind=kLoop, calls=%fused_computation | loop fusion | flops 9216 | bytes 55300 | tf_op jit(solution)/shard_map/convert_element_type | solution.py:415
  41.0 1.1 %shard_map.115 = (bf16[8,128,256]{2,1,0:T(8,128)(2,1)S(1)}, f32[8,1280]{1,0:T(8,128)S(1)}, f32[256,128]{1,0:T(8,128)S(1)}, f32[1,2048]{1,0:T(1,128)S(1)}) custom-call(s32[4]{0:T(128)} %docs_ref.1, f32[8,1152]{1,0:T(8,128)} %dynamic-slice_convert_fusion.filt_ref, bf16[16,128,128]{2,1,0:T(8,128)(2,1)S(1)} %all-to-all-done.gate_ref, f32[1,2048]{1,0:T(1,128)} %bitcast.7), custom_call_target="tpu_custom_call" | custom-call | tf_op jit(solution)/shard_map/pallas_call | solution.py:416
  42.7 2.2 %shard_map.118 = (bf16[8,96,128]{2,1,0:T(8,128)(2,1)S(1)}, bf16[8,96,128]{2,1,0:T(8,128)(2,1)S(1)}, f32[8,1152]{1,0:T(8,128)S(1)}) custom-call(s32[1]{0:T(128)} %bitcast.ctx_ref, bf16[8,128,256]{2,1,0:T(8,128)(2,1)S(1)} %get-tuple-element.43.gate_t_ref, f32[8,1280]{1,0:T(8,128)S(1)} %get-tuple-element.44.rows_ref, f32[256,128]{1,0:T(8,128)S(1)} %get-tuple-element.45.doc_ref, ...), custom_call_target="tpu_custom_call" | custom-call | tf_op jit(solution)/shard_map/pallas_call | solution.py:433
  45.0 1.5 %shard_map.119 = (bf16[8,40,128]{2,1,0:T(8,128)(2,1)S(1)}, bf16[8,40,128]{2,1,0:T(8,128)(2,1)S(1)}, f32[8,1152]{1,0:T(8,128)}) custom-call(s32[1]{0:T(128)} %bitcast.ctx_ref, bf16[8,128,256]{2,1,0:T(8,128)(2,1)S(1)} %get-tuple-element.43.gate_t_ref, f32[8,1280]{1,0:T(8,128)S(1)} %get-tuple-element.44.rows_ref, f32[256,128]{1,0:T(8,128)S(1)} %get-tuple-element.45.doc_ref, ...), custom_call_target="tpu_custom_call" | custom-call | tf_op jit(solution)/shard_map/pallas_call | solution.py:433
  48.4 2.0 %collective-permute-start.12 = (bf16[2,136,128]{2,1,0:T(8,128)(2,1)S(1)}, bf16[2,136,128]{2,1,0:T(8,128)(2,1)S(1)}, u32[]{:S(2)}, u32[]{:S(2)}) collective-permute-start(bf16[2,136,128]{2,1,0:T(8,128)(2,1)S(1)} %get-tuple-element.62), channel_id=1, source_target_pairs={{0,16},{2,18},{4,20},{6,22},{8,24},{10,26},{12,28},{14,30},{16,0},... | collective-permute-start | bytes 208904 | tf_op jit(solution)/shard_map/ppermute | solution.py:107
  50.4 2.1 %collective-permute-start.13 = (bf16[2,136,128]{2,1,0:T(8,128)(2,1)S(1)}, bf16[2,136,128]{2,1,0:T(8,128)(2,1)S(1)}, u32[]{:S(2)}, u32[]{:S(2)}) collective-permute-start(bf16[2,136,128]{2,1,0:T(8,128)(2,1)S(1)} %get-tuple-element.65), channel_id=1, source_target_pairs={{0,12},{2,14},{4,8},{6,10},{8,4},{10,6},{12,0},{14,2},{16,28},{18,... | collective-permute-start | bytes 208904 | tf_op jit(solution)/shard_map/ppermute | solution.py:107
  52.5 2.4 %collective-permute-start.14 = (bf16[2,136,128]{2,1,0:T(8,128)(2,1)S(1)}, bf16[2,136,128]{2,1,0:T(8,128)(2,1)S(1)}, u32[]{:S(2)}, u32[]{:S(2)}) collective-permute-start(bf16[2,136,128]{2,1,0:T(8,128)(2,1)S(1)} %get-tuple-element.66), channel_id=1, source_target_pairs={{0,28},{2,30},{4,24},{6,26},{8,20},{10,22},{12,16},{14,18},{16,12}... | collective-permute-start | bytes 208904 | tf_op jit(solution)/shard_map/ppermute | solution.py:107
  55.5 2.0 %collective-permute-start.16 = (bf16[2,136,128]{2,1,0:T(8,128)(2,1)S(1)}, bf16[2,136,128]{2,1,0:T(8,128)(2,1)S(1)}, u32[]{:S(2)}, u32[]{:S(2)}) collective-permute-start(bf16[2,136,128]{2,1,0:T(8,128)(2,1)S(1)} %get-tuple-element.68), channel_id=1, source_target_pairs={{0,8},{2,10},{4,12},{6,14},{8,0},{10,2},{12,4},{14,6},{16,24},{18,... | collective-permute-start | bytes 208904 | tf_op jit(solution)/shard_map/ppermute | solution.py:107
  57.4 1.7 %collective-permute-done.12.refs_2_ = bf16[2,136,128]{2,1,0:T(8,128)(2,1)S(1)} collective-permute-done((bf16[2,136,128]{2,1,0:T(8,128)(2,1)S(1)}, bf16[2,136,128]{2,1,0:T(8,128)(2,1)S(1)}, u32[]{:S(2)}, u32[]{:S(2)}) %collective-permute-start.12) | collective-permute-done | bytes 69664 | tf_op jit(solution)/shard_map/ppermute | solution.py:107
  59.2 1.0 %collective-permute-start.17 = (bf16[2,136,128]{2,1,0:T(8,128)(2,1)S(1)}, bf16[2,136,128]{2,1,0:T(8,128)(2,1)S(1)}, u32[]{:S(2)}, u32[]{:S(2)}) collective-permute-start(bf16[2,136,128]{2,1,0:T(8,128)(2,1)S(1)} %get-tuple-element.69), channel_id=1, source_target_pairs={{0,24},{2,26},{4,28},{6,30},{8,16},{10,18},{12,20},{14,22},{16,8},... | collective-permute-start | bytes 208904 | tf_op jit(solution)/shard_map/ppermute | solution.py:107
  60.2 1.0 %shard_map.121.after_ref.acc_ref = f32[128,2048]{1,0:T(8,128)S(1)} custom-call(s32[1]{0:T(128)} %bitcast.ctx_ref, s32[1,2048]{1,0:T(1,128)S(1)} %get-tuple-element.38.rank_ref, bf16[128,2048]{1,0:T(8,128)(2,1)S(1)} %get-tuple-element.40.conv_ref, f32[1,2048]{1,0:T(1,128)S(1)} %get-tuple-element.42.skip_ref, ...), custom_call_target="tpu_custom_call" | custom-call | tf_op jit(solution)/shard_map/pallas_call | solution.py:451
  61.2 1.2 %shard_map.122 = (bf16[128,2048]{1,0:T(8,128)(2,1)S(1)}, bf16[128,2048]{1,0:T(8,128)(2,1)S(1)}) custom-call(bf16[128,2048]{1,0:T(8,128)(2,1)} %query_hbm.3, bf16[128,2048]{1,0:T(8,128)(2,1)} %key_hbm.3, f32[128,2048]{1,0:T(8,128)S(1)} %shard_map.121.after_ref.acc_ref), custom_call_target="tpu_custom_call" | custom-call | tf_op jit(solution)/shard_map/pallas_call | solution.py:458
  62.5 2.8 %collective-permute-done.17.refs_7_ = bf16[2,136,128]{2,1,0:T(8,128)(2,1)S(1)} collective-permute-done((bf16[2,136,128]{2,1,0:T(8,128)(2,1)S(1)}, bf16[2,136,128]{2,1,0:T(8,128)(2,1)S(1)}, u32[]{:S(2)}, u32[]{:S(2)}) %collective-permute-start.17) | collective-permute-done | bytes 69664 | tf_op jit(solution)/shard_map/ppermute | solution.py:107
  65.3 2.3 %shard_map.123 = (bf16[128,2048]{1,0:T(8,128)(2,1)}, bf16[128,2048]{1,0:T(8,128)(2,1)}, f32[16,8,128]{2,1,0:T(8,128)}) custom-call(s32[1]{0:T(128)} %bitcast.ctx_ref, s32[1,2048]{1,0:T(1,128)S(1)} %get-tuple-element.38.rank_ref, f32[128,2048]{1,0:T(8,128)S(1)} %shard_map.121.after_ref.acc_ref, bf16[128,2048]{1,0:T(8,128)(2,1)S(1)} %get-tuple-element.63.query_ref, ...), custom_call_target="tpu_custom_call" | custom-call | tf_op jit(solution)/shard_map/pallas_call | solution.py:459
  (27 shorter events, 6.5 us)
Async XLA Ops:
  0.6 17.4 %collective-permute-start = (bf16[128,2048]{1,0:T(8,128)(2,1)}, bf16[128,2048]{1,0:T(8,128)(2,1)S(1)}, u32[]{:S(2)}, u32[]{:S(2)}) collective-permute-start(bf16[128,2048]{1,0:T(8,128)(2,1)} %grad_hbm.1), channel_id=1, source_target_pairs={{0,1},{1,0},{2,3},{3,2},{4,5},{5,4},{6,7},{7,6},{8,9},{9,8},{10,11... | collective-permute-start | bytes 1572872 | tf_op jit(solution)/shard_map/ppermute | solution.py:367
  7.5 33.5 %all-to-all-start = ((bf16[16,128,128]{2,1,0:T(8,128)(2,1)}), bf16[16,128,128]{2,1,0:T(8,128)(2,1)S(1)}, u32[]{:S(2)}, u32[]{:S(2)}) async-start(bf16[16,128,128]{2,1,0:T(8,128)(2,1)} %get-tuple-element.41), calls=%async_computation | async-start | bytes 1048576 | tf_op jit(solution)/shard_map/all_to_all | solution.py:381
  23.2 1.6 %collective-permute-start.1 = (bf16[8,128,128]{2,1,0:T(8,128)(2,1)S(1)}, bf16[8,128,128]{2,1,0:T(8,128)(2,1)S(1)}, u32[]{:S(2)}, u32[]{:S(2)}) collective-permute-start(bf16[8,128,128]{2,1,0:T(8,128)(2,1)S(1)} %get-tuple-element.46), channel_id=1, source_target_pairs={{0,2},{2,0},{4,6},{6,4},{8,10},{10,8},{12,14},{14,12},{16,18},{18,... | collective-permute-start | bytes 786440 | tf_op jit(solution)/shard_map/ppermute | solution.py:96
  24.9 9.4 %collective-permute-start.2 = (bf16[2,128,128]{2,1,0:T(8,128)(2,1)S(1)}, bf16[2,128,128]{2,1,0:T(8,128)(2,1)S(1)}, u32[]{:S(2)}, u32[]{:S(2)}) collective-permute-start(bf16[2,128,128]{2,1,0:T(8,128)(2,1)S(1)} %get-tuple-element.48), channel_id=1, source_target_pairs={{0,20},{2,22},{4,16},{6,18},{8,28},{10,30},{12,24},{14,26},{16,4},... | collective-permute-start | bytes 196616 | tf_op jit(solution)/shard_map/ppermute | solution.py:107
  28.4 8.2 %collective-permute-start.3 = (bf16[2,128,128]{2,1,0:T(8,128)(2,1)S(1)}, bf16[2,128,128]{2,1,0:T(8,128)(2,1)S(1)}, u32[]{:S(2)}, u32[]{:S(2)}) collective-permute-start(bf16[2,128,128]{2,1,0:T(8,128)(2,1)S(1)} %get-tuple-element.49), channel_id=1, source_target_pairs={{0,16},{2,18},{4,20},{6,22},{8,24},{10,26},{12,28},{14,30},{16,0},... | collective-permute-start | bytes 196616 | tf_op jit(solution)/shard_map/ppermute | solution.py:107
  29.0 13.1 %collective-permute-start.4 = (bf16[2,128,128]{2,1,0:T(8,128)(2,1)S(1)}, bf16[2,128,128]{2,1,0:T(8,128)(2,1)S(1)}, u32[]{:S(2)}, u32[]{:S(2)}) collective-permute-start(bf16[2,128,128]{2,1,0:T(8,128)(2,1)S(1)} %get-tuple-element.50), channel_id=1, source_target_pairs={{0,12},{2,14},{4,8},{6,10},{8,4},{10,6},{12,0},{14,2},{16,28},{18,... | collective-permute-start | bytes 196616 | tf_op jit(solution)/shard_map/ppermute | solution.py:107
  30.5 11.6 %collective-permute-start.5 = (bf16[2,128,128]{2,1,0:T(8,128)(2,1)S(1)}, bf16[2,128,128]{2,1,0:T(8,128)(2,1)S(1)}, u32[]{:S(2)}, u32[]{:S(2)}) collective-permute-start(bf16[2,128,128]{2,1,0:T(8,128)(2,1)S(1)} %get-tuple-element.51), channel_id=1, source_target_pairs={{0,28},{2,30},{4,24},{6,26},{8,20},{10,22},{12,16},{14,18},{16,12}... | collective-permute-start | bytes 196616 | tf_op jit(solution)/shard_map/ppermute | solution.py:107
  33.7 8.4 %collective-permute-start.6 = (bf16[2,128,128]{2,1,0:T(8,128)(2,1)S(1)}, bf16[2,128,128]{2,1,0:T(8,128)(2,1)S(1)}, u32[]{:S(2)}, u32[]{:S(2)}) collective-permute-start(bf16[2,128,128]{2,1,0:T(8,128)(2,1)S(1)} %get-tuple-element.52), channel_id=1, source_target_pairs={{0,4},{2,6},{4,0},{6,2},{8,12},{10,14},{12,8},{14,10},{16,20},{18,... | collective-permute-start | bytes 196616 | tf_op jit(solution)/shard_map/ppermute | solution.py:107
  34.3 7.8 %collective-permute-start.7 = (bf16[2,128,128]{2,1,0:T(8,128)(2,1)S(1)}, bf16[2,128,128]{2,1,0:T(8,128)(2,1)S(1)}, u32[]{:S(2)}, u32[]{:S(2)}) collective-permute-start(bf16[2,128,128]{2,1,0:T(8,128)(2,1)S(1)} %get-tuple-element.53), channel_id=1, source_target_pairs={{0,8},{2,10},{4,12},{6,14},{8,0},{10,2},{12,4},{14,6},{16,24},{18,... | collective-permute-start | bytes 196616 | tf_op jit(solution)/shard_map/ppermute | solution.py:107
  36.7 6.1 %collective-permute-start.8 = (bf16[2,128,128]{2,1,0:T(8,128)(2,1)S(1)}, bf16[2,128,128]{2,1,0:T(8,128)(2,1)S(1)}, u32[]{:S(2)}, u32[]{:S(2)}) collective-permute-start(bf16[2,128,128]{2,1,0:T(8,128)(2,1)S(1)} %get-tuple-element.54), channel_id=1, source_target_pairs={{0,24},{2,26},{4,28},{6,30},{8,16},{10,18},{12,20},{14,22},{16,8},... | collective-permute-start | bytes 196616 | tf_op jit(solution)/shard_map/ppermute | solution.py:107
  44.9 3.0 %collective-permute-start.9 = (bf16[8,96,128]{2,1,0:T(8,128)(2,1)S(1)}, bf16[8,96,128]{2,1,0:T(8,128)(2,1)S(1)}, u32[]{:S(2)}, u32[]{:S(2)}) collective-permute-start(bf16[8,96,128]{2,1,0:T(8,128)(2,1)S(1)} %get-tuple-element.58), channel_id=1, source_target_pairs={{0,2},{2,0},{4,6},{6,4},{8,10},{10,8},{12,14},{14,12},{16,18},{18,... | collective-permute-start | bytes 589832 | tf_op jit(solution)/shard_map/ppermute | solution.py:96
  46.5 1.4 %collective-permute-start.10 = (bf16[8,40,128]{2,1,0:T(8,128)(2,1)S(1)}, bf16[8,40,128]{2,1,0:T(8,128)(2,1)S(1)}, u32[]{:S(2)}, u32[]{:S(2)}) collective-permute-start(bf16[8,40,128]{2,1,0:T(8,128)(2,1)S(1)} %get-tuple-element.59), channel_id=1, source_target_pairs={{0,2},{2,0},{4,6},{6,4},{8,10},{10,8},{12,14},{14,12},{16,18},{18,... | collective-permute-start | bytes 245768 | tf_op jit(solution)/shard_map/ppermute | solution.py:96
  47.9 7.5 %collective-permute-start.11 = (bf16[2,136,128]{2,1,0:T(8,128)(2,1)S(1)}, bf16[2,136,128]{2,1,0:T(8,128)(2,1)S(1)}, u32[]{:S(2)}, u32[]{:S(2)}) collective-permute-start(bf16[2,136,128]{2,1,0:T(8,128)(2,1)S(1)} %get-tuple-element.61), channel_id=1, source_target_pairs={{0,20},{2,22},{4,16},{6,18},{8,28},{10,30},{12,24},{14,26},{16,4},... | collective-permute-start | bytes 208904 | tf_op jit(solution)/shard_map/ppermute | solution.py:107
  48.4 10.8 %collective-permute-start.12 = (bf16[2,136,128]{2,1,0:T(8,128)(2,1)S(1)}, bf16[2,136,128]{2,1,0:T(8,128)(2,1)S(1)}, u32[]{:S(2)}, u32[]{:S(2)}) collective-permute-start(bf16[2,136,128]{2,1,0:T(8,128)(2,1)S(1)} %get-tuple-element.62), channel_id=1, source_target_pairs={{0,16},{2,18},{4,20},{6,22},{8,24},{10,26},{12,28},{14,30},{16,0},... | collective-permute-start | bytes 208904 | tf_op jit(solution)/shard_map/ppermute | solution.py:107
  50.4 12.0 %collective-permute-start.13 = (bf16[2,136,128]{2,1,0:T(8,128)(2,1)S(1)}, bf16[2,136,128]{2,1,0:T(8,128)(2,1)S(1)}, u32[]{:S(2)}, u32[]{:S(2)}) collective-permute-start(bf16[2,136,128]{2,1,0:T(8,128)(2,1)S(1)} %get-tuple-element.65), channel_id=1, source_target_pairs={{0,12},{2,14},{4,8},{6,10},{8,4},{10,6},{12,0},{14,2},{16,28},{18,... | collective-permute-start | bytes 208904 | tf_op jit(solution)/shard_map/ppermute | solution.py:107
  52.5 9.9 %collective-permute-start.14 = (bf16[2,136,128]{2,1,0:T(8,128)(2,1)S(1)}, bf16[2,136,128]{2,1,0:T(8,128)(2,1)S(1)}, u32[]{:S(2)}, u32[]{:S(2)}) collective-permute-start(bf16[2,136,128]{2,1,0:T(8,128)(2,1)S(1)} %get-tuple-element.66), channel_id=1, source_target_pairs={{0,28},{2,30},{4,24},{6,26},{8,20},{10,22},{12,16},{14,18},{16,12}... | collective-permute-start | bytes 208904 | tf_op jit(solution)/shard_map/ppermute | solution.py:107
  54.8 7.6 %collective-permute-start.15 = (bf16[2,136,128]{2,1,0:T(8,128)(2,1)S(1)}, bf16[2,136,128]{2,1,0:T(8,128)(2,1)S(1)}, u32[]{:S(2)}, u32[]{:S(2)}) collective-permute-start(bf16[2,136,128]{2,1,0:T(8,128)(2,1)S(1)} %get-tuple-element.67), channel_id=1, source_target_pairs={{0,4},{2,6},{4,0},{6,2},{8,12},{10,14},{12,8},{14,10},{16,20},{18,... | collective-permute-start | bytes 208904 | tf_op jit(solution)/shard_map/ppermute | solution.py:107
  55.5 7.0 %collective-permute-start.16 = (bf16[2,136,128]{2,1,0:T(8,128)(2,1)S(1)}, bf16[2,136,128]{2,1,0:T(8,128)(2,1)S(1)}, u32[]{:S(2)}, u32[]{:S(2)}) collective-permute-start(bf16[2,136,128]{2,1,0:T(8,128)(2,1)S(1)} %get-tuple-element.68), channel_id=1, source_target_pairs={{0,8},{2,10},{4,12},{6,14},{8,0},{10,2},{12,4},{14,6},{16,24},{18,... | collective-permute-start | bytes 208904 | tf_op jit(solution)/shard_map/ppermute | solution.py:107
  59.2 6.1 %collective-permute-start.17 = (bf16[2,136,128]{2,1,0:T(8,128)(2,1)S(1)}, bf16[2,136,128]{2,1,0:T(8,128)(2,1)S(1)}, u32[]{:S(2)}, u32[]{:S(2)}) collective-permute-start(bf16[2,136,128]{2,1,0:T(8,128)(2,1)S(1)} %get-tuple-element.69), channel_id=1, source_target_pairs={{0,24},{2,26},{4,28},{6,30},{8,16},{10,18},{12,20},{14,22},{16,8},... | collective-permute-start | bytes 208904 | tf_op jit(solution)/shard_map/ppermute | solution.py:107
